TPU v7x, 1024 devices: a whole 4x4x32 slice. The times are simulated.
1024 devices in a mesh: slab: 128 (over x, z), chan: 8 (over y, core).
Axes of the slice: x: 4, y: 4, z: 32, core: 2. Of those that a mesh axis runs over, the one named last changes fastest.
Arguments:
- volume: bfloat16 [64, 128, 16, 128], P('chan', 'slab'), may hold values from -6 to 6
- kernel: bfloat16 [3, 3, 3, 64, 128], P(None, None, None, None, 'chan'), may hold values from -0.15625 to 0.15625
- bias: float32 [128], P('chan'), may hold values from -3 to 3
- out_grad: bfloat16 [128, 128, 16, 128], P('chan', 'slab'), may hold values from -6 to 6
Outputs:
- feature: bfloat16 [128, 128, 16, 128], P('chan', 'slab')
- input_grad: bfloat16 [64, 128, 16, 128], P('chan', 'slab')
- kernel_grad: float32 [3, 3, 3, 64, 128], P(None, None, None, None, 'chan')
- bias_grad: float32 [128], P('chan')
All inputs are finite; a program needn't handle non-finite values.
Results may differ from a plain program's by a relative error of at most 0.00105.
Values may be sent and summed in bfloat16 or wider, within the bound.
No kernel may reach another device: no remote copies, remote signals or barrier semaphores. Data moves between devices by JAX's collectives and lax.ppermute only.
A program may use at most 32 MiB of HBM per device.

v0:
```python
import math

import jax
import jax.numpy as jnp
from jax import lax
from jax.sharding import PartitionSpec as P


def with_halo(value, sides, width):
    for axis, dim in sides:
        count, length = (lax.axis_size(axis), value.shape[dim])
        up = [(i, (i + 1) % count) for i in range(count - 1)]
        down = [(j, i) for i, j in up]
        last = lax.slice_in_dim(value, length - width, length, axis=dim)
        first = lax.slice_in_dim(value, 0, width, axis=dim)
        before = lax.ppermute(last, axis, up)
        after = lax.ppermute(first, axis, down)
        value = jnp.concatenate([before, value, after], axis=dim)
    return value


def conv_forward(source, kernel, depth_pad):
    result = lax.conv_general_dilated(
        source[None],
        kernel,
        (1, 1, 1),
        ((depth_pad, depth_pad), (1, 1), (1, 1)),
        dimension_numbers=("NCDHW", "DHWIO", "NCDHW"),
        preferred_element_type=jnp.float32,
    )
    return result[0]


def correlate(left, right):
    return lax.conv_general_dilated(
        left[:, None],
        right[:, None],
        (1, 1, 1),
        ((0, 0), (1, 1), (1, 1)),
        dimension_numbers=("NCDHW", "OIDHW", "NCDHW"),
        preferred_element_type=jnp.float32,
    )


def on_device(volume, kernel, bias, out_grad):
    in_local = volume.shape[0]
    plane_count = volume.shape[1]
    row_count = volume.shape[2]
    col_count = volume.shape[3]
    cell_total = plane_count * lax.axis_size("slab") * row_count * col_count
    joined = jnp.concatenate([volume, out_grad], axis=0)
    rimmed = with_halo(joined, (("slab", 1),), 1)
    volume_rim = rimmed[:in_local]
    grad_rim = rimmed[in_local:]
    gathered = lax.all_gather(volume_rim, "chan", axis=0, tiled=True)
    feature_sum = conv_forward(gathered, kernel, 0)
    kernel_local = jnp.transpose(correlate(gathered, out_grad), (2, 3, 4, 0, 1))
    feature = (feature_sum + bias[:, None, None, None]).astype(jnp.bfloat16)
    flipped = jnp.flip(kernel, (0, 1, 2))
    result = lax.conv_general_dilated(
        grad_rim[None],
        flipped,
        (1, 1, 1),
        ((0, 0), (1, 1), (1, 1)),
        dimension_numbers=("NCDHW", "DHWOI", "NCDHW"),
        preferred_element_type=jnp.float32,
    )
    input_grad = lax.psum_scatter(result[0], "chan", scatter_dimension=0, tiled=True).astype(
        jnp.bfloat16
    )
    bias_local = jnp.sum(out_grad.astype(jnp.float32), axis=(1, 2, 3))
    kernel_sum, bias_sum = lax.psum((kernel_local, bias_local), "slab")
    factor = 1.0 / math.sqrt(cell_total)
    return (feature, input_grad, kernel_sum * factor, bias_sum * factor)


def solution(mesh):
    in_specs = (
        P("chan", "slab", None, None),
        P(None, None, None, None, "chan"),
        P("chan"),
        P("chan", "slab", None, None),
    )
    out_specs = (
        P("chan", "slab", None, None),
        P("chan", "slab", None, None),
        P(None, None, None, None, "chan"),
        P("chan"),
    )
    return jax.shard_map(
        on_device, mesh=mesh, in_specs=in_specs, out_specs=out_specs, check_vma=False
    )
```

profile of v0, /device:TPU:24, one launch (start us, length us, event | category | flops | bytes accessed | tf_op | source)
XLA Modules:
  0.0 847.8 jit_solution(13134298062972453266)
XLA Ops:
  8.1 0.8 constant_dynamic-update-slice_fusion.1
  8.8 0.9 constant_dynamic-update-slice_fusion
  9.7 3.8 collective-permute-start
  13.5 1.3 collective-permute-start.1
  14.8 1.0 convert_reduce_fusion
  15.8 294.3 %psum.15 = f32[16]{0:T(128)S(1)} all-reduce(f32[16]{0:T(128)S(1)} %convert_reduce_fusion), channel_id=1, replica_groups=mesh['slab'=128,'chan'=8] {'slab'}, use_global_device_ids=true, to_apply=%region_3.4 | all-reduce | flops 16 | bytes 128 | tf_op jit(solution)/shard_map/psum | solution.py:72
  310.2 2.5 copy.34
  312.7 13.5 %all_gather.3 = bf16[64,3,16,128]{3,2,1,0:T(8,128)(2,1)S(1)} all-gather(bf16[8,3,16,128]{3,2,1,0:T(8,128)(2,1)S(1)} %pad_maximum_fusion.2), channel_id=1, replica_groups=mesh['slab'=128,'chan'=8] {'chan'}, dimensions={0}, use_global_device_ids=true | all-gather | bytes 884736 | tf_op jit(solution)/shard_map/all_gather | solution.py:55
  326.2 0.2 pad.2
  326.4 1.1 reshape.36
  327.5 3.9 copy.30
  331.4 1.0 slice.14
  332.4 3.8 fusion.19
  336.2 0.2 copy.31
  336.4 3.7 copy.33
  340.1 19.0 %fusion.33 = f32[3,3,3,64,16]{3,4,2,1,0:T(8,128)} fusion(bf16[64,1,3,16,128]{0,1,4,3,2:T(2,128)(2,1)} %copy.33, bf16[16,1,1,16,128]{0,1,4,3,2:T(2,128)(2,1)S(1)} %copy-done.1), kind=kOutput, calls=%fused_computation.39 | convolution fusion | flops 107962368 | bytes 962560 | tf_op jit(solution)/shard_map/transpose | solution.py:57
  359.1 0.0 reduce-scatter.2.cloned.1.call-start
  359.2 0.1 slice_bitcast_fusion
  359.2 1.3 copy.32
  360.6 0.5 broadcast_multiply_fusion.1
  361.1 1.3 copy.25
  362.4 0.3 pad
  362.8 0.4 copy.27
  363.2 0.1 slice.12
  363.3 4.3 fusion.16
  367.6 0.8 copy.28
  368.4 0.3 reshape.33
  368.8 0.1 fusion.26
  368.8 0.6 copy.35
  369.5 467.8 %all-reduce.2.cloned.1.call-done = f32[3,3,3,64,16]{3,4,2,1,0:T(8,128)} async-done(((f32[3,3,3,64,16]{3,4,2,1,0:T(8,128)}), f32[3,3,3,64,16]{3,4,2,1,0:T(8,128)}) %all-reduce.2.cloned.1.call-update) | async-done | bytes 110608 | tf_op jit(solution)/shard_map/psum | solution.py:72
  837.2 1.6 broadcast_multiply_fusion
  838.9 1.5 convert_element_type.18
  (16 shorter events, 0.1 us)
Async XLA Ops:
  8.0 324.4 %copy-start = (bf16[3,3,3,64,16]{3,4,2,1,0:T(8,128)(2,1)S(1)}, bf16[3,3,3,64,16]{3,4,2,1,0:T(8,128)(2,1)}, u32[]{:S(2)}) copy-start(bf16[3,3,3,64,16]{3,4,2,1,0:T(8,128)(2,1)} %param.5) | copy-start | bytes 165892
  8.0 829.2 %all-reduce.2.cloned.1.call-start = ((), (), s32[]{:S(2)}) async-start(), calls=%async_computation.2 | async-start | bytes 442368 | tf_op jit(solution)/shard_map/psum | solution.py:72
  9.7 303.0 %collective-permute-start = (bf16[24,1,16,128]{3,2,1,0:T(8,128)(2,1)S(1)}, bf16[24,1,16,128]{3,2,1,0:T(8,128)(2,1)S(1)}, u32[]{:S(2)}, u32[]{:S(2)}) collective-permute-start(bf16[24,1,16,128]{3,2,1,0:T(8,128)(2,1)S(1)} %constant_dynamic-update-slice_fusion), channel_id=1, source_target_pairs={{0,8},{8,16},{16,24},{24,32},{32,40},{40,48},{48,56},{56,64},{64,7... | collective-permute-start | bytes 294920 | tf_op jit(solution)/shard_map/ppermute | solution.py:16
  13.5 299.1 %collective-permute-start.1 = (bf16[24,1,16,128]{3,2,1,0:T(8,128)(2,1)S(1)}, bf16[24,1,16,128]{3,2,1,0:T(8,128)(2,1)S(1)}, u32[]{:S(2)}, u32[]{:S(2)}) collective-permute-start(bf16[24,1,16,128]{3,2,1,0:T(8,128)(2,1)S(1)} %constant_dynamic-update-slice_fusion), channel_id=1, source_target_pairs={{8,0},{16,8},{24,16},{32,24},{40,32},{48,40},{56,48},{64,56},{72,6... | collective-permute-start | bytes 294920 | tf_op jit(solution)/shard_map/ppermute | solution.py:17
  327.5 4.9 copy-start.3
  336.4 3.7 copy-start.1
  359.1 479.8 %reduce-scatter.2.cloned.1.call-start = ((), (), s32[]{:S(2)}) async-start(), calls=%async_computation.1 | async-start | bytes 589824 | tf_op jit(solution)/shard_map/reduce_scatter | solution.py:68
  367.6 1.2 copy-start.2
Sparse Core Ops, SparseCore 0:
  359.2 477.9 all-reduce.1
Sparse Core Ops, SparseCore 1:
  363.0 24.2 reduce-scatter.1
where the time goes:
time: 849 us; the launch traced here: 848 us
  waiting for transfers between devices  468 us (55%)
  blocking collectives  308 us (36%)
  matrix products  27.1 us (3%)
  local copies, waits for them, and re-layouts  19.5 us (2%)
  between operations  15.6 us (2%)
    psum x1, waiting for transfers between devices, on_device(): kernel_sum, bias_sum = lax.psum((kernel_local, bias_local), 'slab')  468 us
    psum x1, blocking collectives, on_device(): kernel_sum, bias_sum = lax.psum((kernel_local, bias_local), 'slab')  294 us
    transpose x1, matrix products, on_device(): kernel_local = jnp.transpose(correlate(gathered, out_grad), (2, 3, 4, 0, 1))  19 us
  transfers between devices with their start and end apart: 4, of which 1 were waited for; matrix products, arithmetic and copies ran while one was open for 2% of the time, Pallas kernels for 0%

commit v1 on v0

v1 whole, which is shorter than its diff:
```python
import functools
import math

import jax
import jax.numpy as jnp
from jax import lax
from jax.experimental import pallas as pl
from jax.experimental.pallas import tpu as pltpu
from jax.sharding import Mesh, PartitionSpec as P

X, Z = 4, 32
ZL = 4
ZH = Z // ZL
SLAB = ("x", "zh", "zl")
NEAR = ("x", "zl")
ROWS, COLS = 16, 128
CELLS = ROWS * COLS
F32, BF16 = jnp.float32, jnp.bfloat16


def call(body, outs, args, scratch=(), flops=0):
    moved = sum(math.prod(a.shape) * a.dtype.itemsize for a in (*args, *outs))
    return pl.pallas_call(
        body,
        out_shape=tuple(outs),
        in_specs=[pl.BlockSpec(memory_space=pltpu.VMEM)] * len(args),
        out_specs=tuple(pl.BlockSpec(memory_space=pltpu.VMEM) for _ in outs),
        scratch_shapes=list(scratch),
        compiler_params=pltpu.CompilerParams(vmem_limit_bytes=24 << 20),
        cost_estimate=pl.CostEstimate(flops=flops, bytes_accessed=moved, transcendentals=0),
    )(*args)


def shape(dims, dtype):
    return jax.ShapeDtypeStruct(dims, dtype)


def cells_to_lanes(value, spare):
    count = value.shape[0]
    spare[...] = value.astype(F32).reshape(count * ROWS, COLS)
    rows = [spare[pl.ds(h, count, stride=ROWS), :] for h in range(ROWS)]
    return jnp.concatenate(rows, axis=1).astype(BF16)


def lanes_to_cells(value, spare):
    count = value.shape[0]
    for h in range(ROWS):
        spare[pl.ds(h, count, stride=ROWS), :] = value[:, h * COLS : (h + 1) * COLS]
    return spare[...].reshape(count, 1, ROWS, COLS).astype(BF16)


def from_row(value, step):
    if step == 0:
        return value
    gap = jnp.zeros((value.shape[0], COLS), value.dtype)
    if step > 0:
        return jnp.concatenate([value[:, COLS:], gap], axis=1)
    return jnp.concatenate([gap, value[:, :-COLS]], axis=1)


def from_col(value, step):
    if step == 0:
        return value
    lane = lax.broadcasted_iota(jnp.int32, (value.shape[0], COLS), 1)
    keep = lane != (COLS - 1 if step > 0 else 0)
    parts = []
    for h in range(ROWS):
        part = value[:, h * COLS : (h + 1) * COLS].astype(F32)
        part = pltpu.roll(part, (-step) % COLS, axis=1)
        parts.append(jnp.where(keep, part, 0.0).astype(value.dtype))
    return jnp.concatenate(parts, axis=1)


def pack_body(volume, grad, volume_out, grad_out, spare_v, spare_g):
    flat = cells_to_lanes(volume[...], spare_v)
    for k in range(volume_out.shape[0]):
        volume_out[k] = flat
    grad_out[...] = cells_to_lanes(grad[...], spare_g)


def kernel_grad_body(volume, after, here, before, out):
    left = jnp.concatenate(
        [from_row(g[...], 1 - b) for g in (after, here, before) for b in range(3)], axis=0
    )
    right = jnp.concatenate([from_col(volume[...], c - 1) for c in range(3)], axis=0)
    sums = lax.dot_general(left, right, (((1,), (1,)), ((), ())), preferred_element_type=F32)
    out[0:144] = sums[:, 0:128]
    out[144:216] = jnp.concatenate([sums[0:72, 128:192], sums[72:144, 128:192]], axis=1)
    total = jnp.sum(here[...].astype(F32), axis=1, keepdims=True)
    wide = jnp.broadcast_to(total, (16, 128))
    row = lax.broadcasted_iota(jnp.int32, (16, 128), 0)
    lane = lax.broadcasted_iota(jnp.int32, (16, 128), 1)
    across = jnp.sum(jnp.where(row == lane, wide, 0.0), axis=0, keepdims=True)
    out[216:224] = jnp.broadcast_to(across, (8, 128))
    out[224:] = jnp.zeros((out.shape[0] - 224, 128), F32)


def sum_body(factor, parts, out):
    total = parts[0]
    for k in range(1, parts.shape[0]):
        total = total + parts[k]
    if factor is not None:
        total = total * factor
    for k in range(out.shape[0]):
        out[k] = total


def unpack_body(flat, kernel_out, bias_out):
    for a in range(3):
        for b in range(3):
            for half in range(2):
                r = (a * 3 + b) * 16 + half * 8
                o = slice(half * 8, half * 8 + 8)
                pair = flat[r : r + 8]
                kernel_out[a, b, 0, o] = pair[:, 0:64]
                kernel_out[a, b, 1, o] = pair[:, 64:128]
                if r < 72:
                    kernel_out[a, b, 2, o] = flat[144 + r : 152 + r][:, 0:64]
                else:
                    kernel_out[a, b, 2, o] = flat[72 + r : 80 + r][:, 64:128]
    bias_out[...] = flat[216:217]


def input_grad_body(kernel, after, here, before, out):
    left = jnp.concatenate([kernel[:, b].reshape(144, 64) for b in range(3)], axis=1)
    right = jnp.concatenate(
        [from_col(g[...], 1 - c) for g in (after, here, before) for c in range(3)], axis=0
    )
    sums = lax.dot_general(left, right, (((0,), (0,)), ((), ())), preferred_element_type=F32)
    total = sums[64:128]
    total = total + from_row(sums[0:64], 1)
    out[...] = total + from_row(sums[128:192], -1)


def feature_body(kernel, bias, before, here, after, out, spare):
    left = jnp.concatenate([kernel[a].reshape(144, 64) for a in range(3)], axis=1)
    right = jnp.concatenate([before[...], here[...], after[...]], axis=0)
    sums = jnp.dot(left, right, preferred_element_type=F32)
    total = None
    for c in (1, 0, 2):
        part = None
        for b in range(3):
            r = (b * 3 + c) * 16
            term = from_row(sums[r : r + 16], b - 1)
            part = term if part is None else part + term
        part = from_col(part, c - 1)
        total = part if total is None else total + part
    row = lax.broadcasted_iota(jnp.int32, (16, 128), 0)
    lane = lax.broadcasted_iota(jnp.int32, (16, 128), 1)
    column = jnp.sum(jnp.where(row == lane, bias[...], 0.0), axis=1, keepdims=True)
    out[...] = lanes_to_cells(total + column, spare)


def narrow_body(value, out, spare):
    out[...] = lanes_to_cells(value[...], spare)


def on_device(volume, kernel, bias, out_grad):
    slabs = X * Z
    groups = lax.axis_size("chan")
    up = [(i, i + 1) for i in range(slabs - 1)]
    down = [(i + 1, i) for i in range(slabs - 1)]
    weights = jnp.transpose(kernel, (0, 1, 2, 4, 3))

    sent, here = call(
        pack_body,
        [shape((groups, 8, CELLS), BF16), shape((16, CELLS), BF16)],
        [volume, out_grad],
        [pltpu.VMEM((8 * ROWS, COLS), F32), pltpu.VMEM((16 * ROWS, COLS), F32)],
    )
    before = lax.ppermute(here, SLAB, up)
    after = lax.ppermute(here, SLAB, down)
    whole = lax.all_to_all(sent, "chan", 0, 0).reshape(64, CELLS)

    (partial,) = call(
        kernel_grad_body,
        [shape((256, 128), F32)],
        [whole, after, here, before],
        flops=2 * 144 * 192 * CELLS,
    )
    near = X * ZL
    rows = 256 // near
    parts = lax.all_to_all(partial.reshape(near, rows, 128), NEAR, 0, 0)
    (spread,) = call(
        functools.partial(sum_body, None), [shape((ZH, rows, 128), F32)], [parts]
    )
    parts = lax.all_to_all(spread, "zh", 0, 0)
    factor = 1.0 / math.sqrt(slabs * CELLS)
    (spread,) = call(
        functools.partial(sum_body, factor), [shape((near, rows, 128), F32)], [parts]
    )
    flat = lax.all_to_all(spread, NEAR, 0, 0).reshape(256, 128)
    kernel_out, bias_out = call(
        unpack_body, [shape((3, 3, 3, 16, 64), F32), shape((1, 128), F32)], [flat]
    )

    (share,) = call(
        input_grad_body,
        [shape((64, CELLS), F32)],
        [weights, after, here, before],
        flops=2 * 144 * 192 * CELLS,
    )
    mine = lax.psum_scatter(share, "chan", scatter_dimension=0, tiled=True)
    (input_grad,) = call(
        narrow_body,
        [shape((8, 1, ROWS, COLS), BF16)],
        [mine],
        [pltpu.VMEM((8 * ROWS, COLS), F32)],
    )

    whole_before = lax.ppermute(whole, SLAB, up)
    whole_after = lax.ppermute(whole, SLAB, down)
    (feature,) = call(
        feature_body,
        [shape((16, 1, ROWS, COLS), BF16)],
        [weights, jnp.pad(bias, (0, 112)).reshape(1, 128), whole_before, whole, whole_after],
        [pltpu.VMEM((16 * ROWS, COLS), F32)],
        flops=2 * 144 * 192 * CELLS,
    )
    return (
        feature,
        input_grad,
        jnp.transpose(kernel_out, (0, 1, 2, 4, 3)),
        bias_out[0, :16],
    )


def solution(mesh):
    split = Mesh(mesh.devices.reshape(X, ZH, ZL, -1), ("x", "zh", "zl", "chan"))
    in_specs = (
        P("chan", SLAB, None, None),
        P(None, None, None, None, "chan"),
        P("chan"),
        P("chan", SLAB, None, None),
    )
    out_specs = (
        P("chan", SLAB, None, None),
        P("chan", SLAB, None, None),
        P(None, None, None, None, "chan"),
        P("chan"),
    )
    return jax.shard_map(
        on_device, mesh=split, in_specs=in_specs, out_specs=out_specs, check_vma=False
    )
```

time: 849 us -> 130 us (0.15)
  the two profiles are of different devices: /device:TPU:24 before, /device:TPU:1 now
where the time goes in v1:
time: 130 us; the launch traced here: 129 us
  waiting for transfers between devices  44.5 us (34%)
  starting transfers between devices  42.8 us (33%)
  blocking collectives  18.7 us (14%)
  between operations  14.1 us (11%)
  Pallas kernels  6.44 us (5%)
  local copies, waits for them, and re-layouts  2.95 us (2%)
    all_to_all x1, waiting for transfers between devices, on_device(): parts = lax.all_to_all(spread, 'zh', 0, 0)  20.3 us
    all_to_all x1, blocking collectives, on_device(): parts = lax.all_to_all(partial.reshape(near, rows, 128), NEAR, 0, 0)  18.7 us
    all_to_all x1, starting transfers between devices, on_device(): whole = lax.all_to_all(sent, 'chan', 0, 0).reshape(64, CELLS)  17.5 us
    reduce_scatter x1, waiting for transfers between devices, on_device(): mine = lax.psum_scatter(share, 'chan', scatter_dimension=0, tiled=True)  15.9 us
    all_to_all x1, starting transfers between devices, on_device(): parts = lax.all_to_all(spread, 'zh', 0, 0)  11.8 us
    pallas_call x8, Pallas kernels, call(): pl.pallas_call(body, out_shape=tuple(outs), in_specs=[pl.BlockSpec(memory...  6.44 us
    ppermute x1, waiting for transfers between devices, on_device(): whole_after = lax.ppermute(whole, SLAB, down)  4.56 us
    ppermute x1, starting transfers between devices, on_device(): before = lax.ppermute(here, SLAB, up)  3.99 us
  transfers between devices with their start and end apart: 8, of which 6 were waited for; matrix products, arithmetic and copies ran while one was open for 0% of the time, Pallas kernels for 3%

profile of v1, /device:TPU:1, one launch (start us, length us, event | category | flops | bytes accessed | tf_op | source)
XLA Modules:
  0.0 129.5 jit_solution(6667109585412513983)
XLA Ops:
  7.2 0.0 copy-start.1
  7.2 0.8 copy-done.1
  8.0 0.8 copy-done.3
  8.8 0.8 shard_map.75
  9.5 17.5 %all-to-all-start = ((bf16[8,8,2048]{2,1,0:T(8,128)(2,1)}), bf16[8,8,2048]{2,1,0:T(8,128)(2,1)S(1)}, u32[]{:S(2)}, u32[]{:S(2)}) async-start(bf16[8,8,2048]{2,1,0:T(8,128)(2,1)} %get-tuple-element.8), calls=%async_computation | async-start | bytes 524288 | tf_op jit(solution)/shard_map/all_to_all | solution.py:173
  27.0 1.3 collective-permute-start.2
  28.3 4.0 %collective-permute-start.3 = (bf16[16,2048]{1,0:T(8,128)(2,1)S(1)}, bf16[16,2048]{1,0:T(8,128)(2,1)S(1)}, u32[]{:S(2)}, u32[]{:S(2)}) collective-permute-start(bf16[16,2048]{1,0:T(8,128)(2,1)S(1)} %get-tuple-element.9.here), channel_id=1, source_target_pairs={{0,8},{8,16},{16,24},{24,32},{32,40},{40,48},{48,56},{56,64},{64,7... | collective-permute-start | bytes 196616 | tf_op jit(solution)/shard_map/ppermute | solution.py:171
  32.3 0.2 collective-permute-done.2.after
  32.4 1.2 collective-permute-done.3.before
  33.6 0.0 all-to-all-done
  33.6 0.6 shard_map.79
  34.1 18.7 %all_to_all.20.parts = f32[16,16,128]{2,1,0:T(8,128)S(1)} all-to-all(f32[16,16,128]{2,1,0:T(8,128)S(1)} %bitcast.14), channel_id=1, replica_groups=mesh['x'=4,'zh'=8,'zl'=4,'chan'=8] {'x','zl'}, dimensions={0} | all-to-all | bytes 262144 | tf_op jit(solution)/shard_map/all_to_all | solution.py:183
  52.8 0.6 shard_map.80
  53.5 11.8 %all-to-all-start.2 = ((f32[8,16,128]{2,1,0:T(8,128)}), f32[8,16,128]{2,1,0:T(8,128)S(1)}, u32[]{:S(2)}, u32[]{:S(2)}) async-start(f32[8,16,128]{2,1,0:T(8,128)} %shard_map.80), calls=%async_computation.3 | async-start | bytes 131072 | tf_op jit(solution)/shard_map/all_to_all | solution.py:187
  65.3 0.0 reduce-scatter.2.cloned.1.call-start
  65.3 0.0 copy-done
  65.3 1.3 %shard_map.77 = f32[64,2048]{1,0:T(8,128)} custom-call(bf16[3,3,3,16,64]{4,3,2,1,0:T(8,128)(2,1)S(1)} %bitcast.15, bf16[16,2048]{1,0:T(8,128)(2,1)S(1)} %collective-permute-done.2.after, bf16[16,2048]{1,0:T(8,128)(2,1)S(1)} %get-tuple-element.9.here, bf16[16,2048]{1,0:T(8,128)(2,1)S(1)} %collective-permute-done.3.before), custom_call_target="tpu_custom_call" | custom-call | flops 113246208 | bytes 776192 | tf_op jit(solution)/shard_map/pallas_call | solution.py:23
  66.6 0.0 reduce-scatter.2.cloned.1.call-update
  66.7 20.3 %all-to-all-done.2.parts = f32[8,16,128]{2,1,0:T(8,128)S(1)} async-done(((f32[8,16,128]{2,1,0:T(8,128)}), f32[8,16,128]{2,1,0:T(8,128)S(1)}, u32[]{:S(2)}, u32[]{:S(2)}) %all-to-all-start.2) | async-done | bytes 65568 | tf_op jit(solution)/shard_map/all_to_all | solution.py:187
  86.9 0.7 shard_map.81
  87.6 3.7 %all-to-all-start.3 = ((f32[16,16,128]{2,1,0:T(8,128)}), f32[16,16,128]{2,1,0:T(8,128)S(1)}, u32[]{:S(2)}, u32[]{:S(2)}) async-start(f32[16,16,128]{2,1,0:T(8,128)} %shard_map.81), calls=%async_computation.4 | async-start | bytes 262144 | tf_op jit(solution)/shard_map/all_to_all | solution.py:192
  91.3 3.3 %collective-permute-start = (bf16[64,2048]{1,0:T(8,128)(2,1)S(1)}, bf16[64,2048]{1,0:T(8,128)(2,1)S(1)}, u32[]{:S(2)}, u32[]{:S(2)}) collective-permute-start(bf16[64,2048]{1,0:T(8,128)(2,1)S(1)} %bitcast.10), channel_id=1, source_target_pairs={{0,8},{8,16},{16,24},{24,32},{32,40},{40,48},{48,56},{56,64},{64,7... | collective-permute-start | bytes 786440 | tf_op jit(solution)/shard_map/ppermute | solution.py:211
  94.5 1.3 collective-permute-start.1
  95.9 2.5 %collective-permute-done.before = bf16[64,2048]{1,0:T(8,128)(2,1)S(1)} collective-permute-done((bf16[64,2048]{1,0:T(8,128)(2,1)S(1)}, bf16[64,2048]{1,0:T(8,128)(2,1)S(1)}, u32[]{:S(2)}, u32[]{:S(2)}) %collective-permute-start) | collective-permute-done | bytes 262176 | tf_op jit(solution)/shard_map/ppermute | solution.py:211
  98.3 4.6 %collective-permute-done.1.after = bf16[64,2048]{1,0:T(8,128)(2,1)S(1)} collective-permute-done((bf16[64,2048]{1,0:T(8,128)(2,1)S(1)}, bf16[64,2048]{1,0:T(8,128)(2,1)S(1)}, u32[]{:S(2)}, u32[]{:S(2)}) %collective-permute-start.1) | collective-permute-done | bytes 262176 | tf_op jit(solution)/shard_map/ppermute | solution.py:212
  102.9 1.1 shard_map.76
  104.0 15.9 %reduce-scatter.2.cloned.1.call-done.value = f32[8,2048]{1,0:T(8,128)} async-done(((f32[64,2048]{1,0:T(8,128)}), f32[8,2048]{1,0:T(8,128)}) %reduce-scatter.2.cloned.1.call-update) | async-done | bytes 65552 | tf_op jit(solution)/shard_map/reduce_scatter | solution.py:203
  119.8 0.8 copy-done.2
  120.7 0.6 shard_map.78
  121.3 0.0 all-to-all-done.3
  121.3 0.8 shard_map.82
  122.1 0.5 slice_bitcast_fusion
  (6 shorter events, 0.0 us)
Async XLA Ops:
  7.2 0.8 copy-start.1
  8.0 0.8 copy-start.3
  9.5 24.1 %all-to-all-start = ((bf16[8,8,2048]{2,1,0:T(8,128)(2,1)}), bf16[8,8,2048]{2,1,0:T(8,128)(2,1)S(1)}, u32[]{:S(2)}, u32[]{:S(2)}) async-start(bf16[8,8,2048]{2,1,0:T(8,128)(2,1)} %get-tuple-element.8), calls=%async_computation | async-start | bytes 524288 | tf_op jit(solution)/shard_map/all_to_all | solution.py:173
  27.0 5.4 %collective-permute-start.2 = (bf16[16,2048]{1,0:T(8,128)(2,1)S(1)}, bf16[16,2048]{1,0:T(8,128)(2,1)S(1)}, u32[]{:S(2)}, u32[]{:S(2)}) collective-permute-start(bf16[16,2048]{1,0:T(8,128)(2,1)S(1)} %get-tuple-element.9.here), channel_id=1, source_target_pairs={{8,0},{16,8},{24,16},{32,24},{40,32},{48,40},{56,48},{64,56},{72,6... | collective-permute-start | bytes 196616 | tf_op jit(solution)/shard_map/ppermute | solution.py:172
  28.3 5.3 %collective-permute-start.3 = (bf16[16,2048]{1,0:T(8,128)(2,1)S(1)}, bf16[16,2048]{1,0:T(8,128)(2,1)S(1)}, u32[]{:S(2)}, u32[]{:S(2)}) collective-permute-start(bf16[16,2048]{1,0:T(8,128)(2,1)S(1)} %get-tuple-element.9.here), channel_id=1, source_target_pairs={{0,8},{8,16},{16,24},{24,32},{32,40},{40,48},{48,56},{56,64},{64,7... | collective-permute-start | bytes 196616 | tf_op jit(solution)/shard_map/ppermute | solution.py:171
  53.5 11.8 %copy-start = (bf16[3,3,3,64,16]{3,4,2,1,0:T(8,128)(2,1)S(1)}, bf16[3,3,3,64,16]{3,4,2,1,0:T(8,128)(2,1)}, u32[]{:S(2)}) copy-start(bf16[3,3,3,64,16]{3,4,2,1,0:T(8,128)(2,1)} %param.5) | copy-start | bytes 165892
  53.5 33.4 %all-to-all-start.2 = ((f32[8,16,128]{2,1,0:T(8,128)}), f32[8,16,128]{2,1,0:T(8,128)S(1)}, u32[]{:S(2)}, u32[]{:S(2)}) async-start(f32[8,16,128]{2,1,0:T(8,128)} %shard_map.80), calls=%async_computation.3 | async-start | bytes 131072 | tf_op jit(solution)/shard_map/all_to_all | solution.py:187
  65.3 54.6 %reduce-scatter.2.cloned.1.call-start = ((), (), s32[]{:S(2)}) async-start(), calls=%async_computation.5 | async-start | bytes 589824 | tf_op jit(solution)/shard_map/reduce_scatter | solution.py:203
  87.6 8.3 %copy-start.4 = (f32[16]{0:T(128)S(1)}, f32[16]{0:T(128)}, u32[]{:S(2)}) copy-start(f32[16]{0:T(128)} %param.6) | copy-start | bytes 196
  87.6 33.8 %all-to-all-start.3 = ((f32[16,16,128]{2,1,0:T(8,128)}), f32[16,16,128]{2,1,0:T(8,128)S(1)}, u32[]{:S(2)}, u32[]{:S(2)}) async-start(f32[16,16,128]{2,1,0:T(8,128)} %shard_map.81), calls=%async_computation.4 | async-start | bytes 262144 | tf_op jit(solution)/shard_map/all_to_all | solution.py:192
  91.3 7.1 %collective-permute-start = (bf16[64,2048]{1,0:T(8,128)(2,1)S(1)}, bf16[64,2048]{1,0:T(8,128)(2,1)S(1)}, u32[]{:S(2)}, u32[]{:S(2)}) collective-permute-start(bf16[64,2048]{1,0:T(8,128)(2,1)S(1)} %bitcast.10), channel_id=1, source_target_pairs={{0,8},{8,16},{16,24},{24,32},{32,40},{40,48},{48,56},{56,64},{64,7... | collective-permute-start | bytes 786440 | tf_op jit(solution)/shard_map/ppermute | solution.py:211
  94.5 8.4 %collective-permute-start.1 = (bf16[64,2048]{1,0:T(8,128)(2,1)S(1)}, bf16[64,2048]{1,0:T(8,128)(2,1)S(1)}, u32[]{:S(2)}, u32[]{:S(2)}) collective-permute-start(bf16[64,2048]{1,0:T(8,128)(2,1)S(1)} %bitcast.11), channel_id=1, source_target_pairs={{8,0},{16,8},{24,16},{32,24},{40,32},{48,40},{56,48},{64,56},{72,6... | collective-permute-start | bytes 786440 | tf_op jit(solution)/shard_map/ppermute | solution.py:212
  119.8 0.8 copy-start.2
Sparse Core Ops, SparseCore 0:
  69.5 50.3 reduce-scatter.1

commit v2 on v1

--- a/solution.py
+++ b/solution.py
@@ -18,15 +18,23 @@
 F32, BF16 = jnp.float32, jnp.bfloat16
 
 
-def call(body, outs, args, scratch=(), flops=0):
+def call(body, outs, args, scratch=(), flops=0, after=(), anywhere=False, limit=24):
+    used, late = (len(args), len(after))
+    inner = body
+    if late:
+        def inner(*refs):
+            body(*refs[:used], *refs[used + late :])
+    args = [*args, *after]
+    space = pltpu.HBM if anywhere else pltpu.VMEM
     moved = sum(math.prod(a.shape) * a.dtype.itemsize for a in (*args, *outs))
     return pl.pallas_call(
-        body,
+        inner,
         out_shape=tuple(outs),
-        in_specs=[pl.BlockSpec(memory_space=pltpu.VMEM)] * len(args),
+        in_specs=[pl.BlockSpec(memory_space=space)] * used
+        + [pl.BlockSpec(memory_space=pl.ANY)] * late,
         out_specs=tuple(pl.BlockSpec(memory_space=pltpu.VMEM) for _ in outs),
         scratch_shapes=list(scratch),
-        compiler_params=pltpu.CompilerParams(vmem_limit_bytes=24 << 20),
+        compiler_params=pltpu.CompilerParams(vmem_limit_bytes=limit << 20),
         cost_estimate=pl.CostEstimate(flops=flops, bytes_accessed=moved, transcendentals=0),
     )(*args)
 
@@ -37,7 +45,7 @@
 
 def cells_to_lanes(value, spare):
     count = value.shape[0]
-    spare[...] = value.astype(F32).reshape(count * ROWS, COLS)
+    spare[...] = value[...].astype(F32).reshape(count * ROWS, COLS)
     rows = [spare[pl.ds(h, count, stride=ROWS), :] for h in range(ROWS)]
     return jnp.concatenate(rows, axis=1).astype(BF16)
 
@@ -71,22 +79,29 @@
     return jnp.concatenate(parts, axis=1)
 
 
-def pack_body(volume, grad, volume_out, grad_out, spare_v, spare_g):
-    flat = cells_to_lanes(volume[...], spare_v)
+def pack_body(volume, grad, volume_out, plane_out, here_v, here_g, spare_v, spare_g, sems):
+    copy_g = pltpu.make_async_copy(grad, here_g, sems.at[0])
+    copy_v = pltpu.make_async_copy(volume, here_v, sems.at[1])
+    copy_v.start()
+    copy_g.start()
+    copy_v.wait()
+    flat = cells_to_lanes(here_v, spare_v)
     for k in range(volume_out.shape[0]):
         volume_out[k] = flat
-    grad_out[...] = cells_to_lanes(grad[...], spare_g)
+    plane_out[16:24] = flat
+    copy_g.wait()
+    plane_out[0:16] = cells_to_lanes(here_g, spare_g)
 
 
 def kernel_grad_body(volume, after, here, before, out):
     left = jnp.concatenate(
-        [from_row(g[...], 1 - b) for g in (after, here, before) for b in range(3)], axis=0
+        [from_row(g[0:16], 1 - b) for g in (after, here, before) for b in range(3)], axis=0
     )
     right = jnp.concatenate([from_col(volume[...], c - 1) for c in range(3)], axis=0)
     sums = lax.dot_general(left, right, (((1,), (1,)), ((), ())), preferred_element_type=F32)
     out[0:144] = sums[:, 0:128]
     out[144:216] = jnp.concatenate([sums[0:72, 128:192], sums[72:144, 128:192]], axis=1)
-    total = jnp.sum(here[...].astype(F32), axis=1, keepdims=True)
+    total = jnp.sum(here[0:16].astype(F32), axis=1, keepdims=True)
     wide = jnp.broadcast_to(total, (16, 128))
     row = lax.broadcasted_iota(jnp.int32, (16, 128), 0)
     lane = lax.broadcasted_iota(jnp.int32, (16, 128), 1)
@@ -118,21 +133,57 @@
                     kernel_out[a, b, 2, o] = flat[144 + r : 152 + r][:, 0:64]
                 else:
                     kernel_out[a, b, 2, o] = flat[72 + r : 80 + r][:, 64:128]
-    bias_out[...] = flat[216:217]
-
-
-def input_grad_body(kernel, after, here, before, out):
+    bias_out[...] = flat[216:217, 0:16]
+
+
+def input_grad_body(kernel, after, here, before, kept, sent):
     left = jnp.concatenate([kernel[:, b].reshape(144, 64) for b in range(3)], axis=1)
     right = jnp.concatenate(
-        [from_col(g[...], 1 - c) for g in (after, here, before) for c in range(3)], axis=0
+        [from_col(g[0:16], 1 - c) for g in (after, here, before) for c in range(3)], axis=0
     )
     sums = lax.dot_general(left, right, (((0,), (0,)), ((), ())), preferred_element_type=F32)
     total = sums[64:128]
     total = total + from_row(sums[0:64], 1)
-    out[...] = total + from_row(sums[128:192], -1)
-
-
-def feature_body(kernel, bias, before, here, after, out, spare):
+    total = total + from_row(sums[128:192], -1)
+    odd = lax.rem(lax.axis_index("chan"), 2) == 1
+    for y in range(4):
+        first, second = total[16 * y : 16 * y + 8], total[16 * y + 8 : 16 * y + 16]
+        kept[y] = jnp.where(odd, second, first)
+        sent[y], sent[4 + y] = halves(jnp.where(odd, first, second))
+    sent[8] = before[16:24]
+    sent[9] = after[16:24]
+
+
+def halves(value):
+    high = value.astype(BF16)
+    return high, (value - high.astype(F32)).astype(BF16)
+
+
+def join_body(kept, got, before, after, own, *sent):
+    chan = lax.axis_index("chan")
+    y, odd = lax.div(chan, 2), lax.rem(chan, 2) == 1
+    for k, out in enumerate((own, *sent)):
+        block = lax.rem(y + k, 4)
+        total = kept[block] + got[block].astype(F32) + got[4 + block].astype(F32)
+        if k == 0:
+            out[...] = total
+        else:
+            out[0:8], out[8:16] = halves(total)
+    for row, mine, theirs in ((16, before, got[8]), (32, after, got[9])):
+        mine, theirs = mine[16:24].astype(F32), theirs.astype(F32)
+        first = jnp.where(odd, theirs, mine).astype(BF16)
+        second = jnp.where(odd, mine, theirs).astype(BF16)
+        for out in sent:
+            out[row : row + 8] = first
+            out[row + 8 : row + 16] = second
+
+
+def feature_body(kernel, bias, here, own, first, second, third, out, before, after, spare):
+    y = lax.div(lax.axis_index("chan"), 2)
+    for k, part in enumerate((own, first, second, third)):
+        place = pl.ds(pl.multiple_of(16 * lax.rem(y + 4 - k, 4), 16), 16)
+        before[place] = part[16:32]
+        after[place] = part[32:48]
     left = jnp.concatenate([kernel[a].reshape(144, 64) for a in range(3)], axis=1)
     right = jnp.concatenate([before[...], here[...], after[...]], axis=0)
     sums = jnp.dot(left, right, preferred_element_type=F32)
@@ -145,14 +196,17 @@
             part = term if part is None else part + term
         part = from_col(part, c - 1)
         total = part if total is None else total + part
-    row = lax.broadcasted_iota(jnp.int32, (16, 128), 0)
-    lane = lax.broadcasted_iota(jnp.int32, (16, 128), 1)
+    row = lax.broadcasted_iota(jnp.int32, (16, 16), 0)
+    lane = lax.broadcasted_iota(jnp.int32, (16, 16), 1)
     column = jnp.sum(jnp.where(row == lane, bias[...], 0.0), axis=1, keepdims=True)
     out[...] = lanes_to_cells(total + column, spare)
 
 
-def narrow_body(value, out, spare):
-    out[...] = lanes_to_cells(value[...], spare)
+def narrow_body(own, first, second, third, out, spare):
+    total = own[...]
+    for part in (first, second, third):
+        total = total + (part[0:8].astype(F32) + part[8:16].astype(F32))
+    out[...] = lanes_to_cells(total, spare)
 
 
 def on_device(volume, kernel, bias, out_grad):
@@ -164,9 +218,17 @@
 
     sent, here = call(
         pack_body,
-        [shape((groups, 8, CELLS), BF16), shape((16, CELLS), BF16)],
+        [shape((groups, 8, CELLS), BF16), shape((24, CELLS), BF16)],
         [volume, out_grad],
-        [pltpu.VMEM((8 * ROWS, COLS), F32), pltpu.VMEM((16 * ROWS, COLS), F32)],
+        [
+            pltpu.VMEM(volume.shape, BF16),
+            pltpu.VMEM(out_grad.shape, BF16),
+            pltpu.VMEM((8 * ROWS, COLS), F32),
+            pltpu.VMEM((16 * ROWS, COLS), F32),
+            pltpu.SemaphoreType.DMA((2,)),
+        ],
+        anywhere=True,
+        limit=60,
     )
     before = lax.ppermute(here, SLAB, up)
     after = lax.ppermute(here, SLAB, down)
@@ -178,50 +240,68 @@
         [whole, after, here, before],
         flops=2 * 144 * 192 * CELLS,
     )
+    kept, sent = call(
+        input_grad_body,
+        [shape((4, 8, CELLS), F32), shape((10, 8, CELLS), BF16)],
+        [weights, after, here, before],
+        flops=2 * 144 * 192 * CELLS,
+    )
+    got = lax.ppermute(sent, "chan", [(i, i ^ 1) for i in range(groups)])
     near = X * ZL
     rows = 256 // near
     parts = lax.all_to_all(partial.reshape(near, rows, 128), NEAR, 0, 0)
     (spread,) = call(
-        functools.partial(sum_body, None), [shape((ZH, rows, 128), F32)], [parts]
+        functools.partial(sum_body, None),
+        [shape((ZH, rows, 128), F32)],
+        [parts],
+        after=[got],
     )
     parts = lax.all_to_all(spread, "zh", 0, 0)
+    own, *joined = call(
+        join_body,
+        [shape((8, CELLS), F32)] + [shape((48, CELLS), BF16)] * 3,
+        [kept, got, before, after],
+        after=[spread],
+    )
+    others = [
+        lax.ppermute(part, "chan", [(i, (i + 2 * k + 2) % groups) for i in range(groups)])
+        for k, part in enumerate(joined)
+    ]
     factor = 1.0 / math.sqrt(slabs * CELLS)
     (spread,) = call(
-        functools.partial(sum_body, factor), [shape((near, rows, 128), F32)], [parts]
+        functools.partial(sum_body, factor),
+        [shape((near, rows, 128), F32)],
+        [parts],
+        after=[*others],
     )
     flat = lax.all_to_all(spread, NEAR, 0, 0).reshape(256, 128)
     kernel_out, bias_out = call(
-        unpack_body, [shape((3, 3, 3, 16, 64), F32), shape((1, 128), F32)], [flat]
-    )
-
-    (share,) = call(
-        input_grad_body,
-        [shape((64, CELLS), F32)],
-        [weights, after, here, before],
-        flops=2 * 144 * 192 * CELLS,
-    )
-    mine = lax.psum_scatter(share, "chan", scatter_dimension=0, tiled=True)
+        unpack_body, [shape((3, 3, 3, 16, 64), F32), shape((1, 16), F32)], [flat]
+    )
+
     (input_grad,) = call(
         narrow_body,
         [shape((8, 1, ROWS, COLS), BF16)],
-        [mine],
+        [own, *others],
         [pltpu.VMEM((8 * ROWS, COLS), F32)],
     )
 
-    whole_before = lax.ppermute(whole, SLAB, up)
-    whole_after = lax.ppermute(whole, SLAB, down)
     (feature,) = call(
         feature_body,
         [shape((16, 1, ROWS, COLS), BF16)],
-        [weights, jnp.pad(bias, (0, 112)).reshape(1, 128), whole_before, whole, whole_after],
-        [pltpu.VMEM((16 * ROWS, COLS), F32)],
+        [weights, bias.reshape(1, 16), whole, joined[0], *others],
+        [
+            pltpu.VMEM((64, CELLS), BF16),
+            pltpu.VMEM((64, CELLS), BF16),
+            pltpu.VMEM((16 * ROWS, COLS), F32),
+        ],
         flops=2 * 144 * 192 * CELLS,
     )
     return (
         feature,
         input_grad,
         jnp.transpose(kernel_out, (0, 1, 2, 4, 3)),
-        bias_out[0, :16],
+        bias_out.reshape(16),
     )
 
 

time: 130 us -> 102 us (0.78)
  the two profiles are of different devices: /device:TPU:1 before, /device:TPU:24 now
where the time goes in v2:
time: 102 us; the launch traced here: 101 us
  starting transfers between devices  62.7 us (61%)
  waiting for transfers between devices  29.5 us (29%)
  Pallas kernels  7.28 us (7%)
    all_to_all x1, starting transfers between devices, on_device(): parts = lax.all_to_all(spread, 'zh', 0, 0)  17.4 us
    all_to_all x1, starting transfers between devices, on_device(): whole = lax.all_to_all(sent, 'chan', 0, 0).reshape(64, CELLS)  16.4 us
    ppermute x3, starting transfers between devices, on_device(): lax.ppermute(part, 'chan', [(i, (i + 2 * k + 2) % groups) for i in range(...  10.4 us
    all_to_all x1, waiting for transfers between devices, on_device(): parts = lax.all_to_all(spread, 'zh', 0, 0)  8.95 us
    all_to_all x1, starting transfers between devices, on_device(): parts = lax.all_to_all(partial.reshape(near, rows, 128), NEAR, 0, 0)  7.93 us
    pallas_call x9, Pallas kernels, call(): pl.pallas_call(inner, out_shape=tuple(outs), in_specs=[pl.BlockSpec(memor...  7.28 us
    all_to_all x1, starting transfers between devices, on_device(): flat = lax.all_to_all(spread, NEAR, 0, 0).reshape(256, 128)  6.09 us
    all_to_all x1, waiting for transfers between devices, on_device(): flat = lax.all_to_all(spread, NEAR, 0, 0).reshape(256, 128)  6 us
  transfers between devices with their start and end apart: 10, of which 8 were waited for; matrix products, arithmetic and copies ran while one was open for 0% of the time, Pallas kernels for 2%

profile of v2, /device:TPU:24, one launch (start us, length us, event | category | flops | bytes accessed | tf_op | source)
XLA Modules:
  0.0 100.9 jit_solution(3067164044196161190)
XLA Ops:
  0.6 1.6 %shard_map.75 = (bf16[8,8,2048]{2,1,0:T(8,128)(2,1)}, bf16[24,2048]{1,0:T(8,128)(2,1)}) custom-call(bf16[8,1,16,128]{3,2,1,0:T(8,128)(2,1)} %volume.1, bf16[16,1,16,128]{3,2,1,0:T(8,128)(2,1)} %grad.1), custom_call_target="tpu_custom_call" | custom-call | bytes 458752 | tf_op jit(solution)/shard_map/pallas_call | solution.py:30
  2.2 0.0 copy-start.1
  2.3 16.4 %all-to-all-start = ((bf16[8,8,2048]{2,1,0:T(8,128)(2,1)}), bf16[8,8,2048]{2,1,0:T(8,128)(2,1)S(1)}, u32[]{:S(2)}, u32[]{:S(2)}) async-start(bf16[8,8,2048]{2,1,0:T(8,128)(2,1)} %get-tuple-element.14), calls=%async_computation | async-start | bytes 524288 | tf_op jit(solution)/shard_map/all_to_all | solution.py:235
  18.6 0.0 copy-done.1
  18.6 1.3 %collective-permute-start.1 = (bf16[24,2048]{1,0:T(8,128)(2,1)S(1)}, bf16[24,2048]{1,0:T(8,128)(2,1)S(1)}, u32[]{:S(2)}, u32[]{:S(2)}) collective-permute-start(bf16[24,2048]{1,0:T(8,128)(2,1)S(1)} %copy-done.1), channel_id=1, source_target_pairs={{0,8},{8,16},{16,24},{24,32},{32,40},{40,48},{48,56},{56,64},{64,7... | collective-permute-start | bytes 294920 | tf_op jit(solution)/shard_map/ppermute | solution.py:233
  19.9 1.3 %collective-permute-start = (bf16[24,2048]{1,0:T(8,128)(2,1)S(1)}, bf16[24,2048]{1,0:T(8,128)(2,1)S(1)}, u32[]{:S(2)}, u32[]{:S(2)}) collective-permute-start(bf16[24,2048]{1,0:T(8,128)(2,1)S(1)} %copy-done.1), channel_id=1, source_target_pairs={{8,0},{16,8},{24,16},{32,24},{40,32},{48,40},{56,48},{64,56},{72,6... | collective-permute-start | bytes 294920 | tf_op jit(solution)/shard_map/ppermute | solution.py:234
  21.2 1.3 %collective-permute-done.1.before.refs_2_ = bf16[24,2048]{1,0:T(8,128)(2,1)S(1)} collective-permute-done((bf16[24,2048]{1,0:T(8,128)(2,1)S(1)}, bf16[24,2048]{1,0:T(8,128)(2,1)S(1)}, u32[]{:S(2)}, u32[]{:S(2)}) %collective-permute-start.1) | collective-permute-done | bytes 98336 | tf_op jit(solution)/shard_map/ppermute | solution.py:233
  22.5 4.1 %collective-permute-done.after.refs_3_ = bf16[24,2048]{1,0:T(8,128)(2,1)S(1)} collective-permute-done((bf16[24,2048]{1,0:T(8,128)(2,1)S(1)}, bf16[24,2048]{1,0:T(8,128)(2,1)S(1)}, u32[]{:S(2)}, u32[]{:S(2)}) %collective-permute-start) | collective-permute-done | bytes 98336 | tf_op jit(solution)/shard_map/ppermute | solution.py:234
  26.7 0.0 all-to-all-done
  26.7 1.2 %shard_map.77 = f32[256,128]{1,0:T(8,128)} custom-call(bf16[64,2048]{1,0:T(8,128)(2,1)S(1)} %bitcast.7, bf16[24,2048]{1,0:T(8,128)(2,1)S(1)} %collective-permute-done.after.refs_3_, bf16[24,2048]{1,0:T(8,128)(2,1)S(1)} %copy-done.1, bf16[24,2048]{1,0:T(8,128)(2,1)S(1)} %collective-permute-done.1.before.refs_2_), custom_call_target="tpu_custom_call" | custom-call | flops 113246208 | bytes 688128 | tf_op jit(solution)/shard_map/pallas_call | solution.py:30
  27.9 7.9 %all-to-all-start.1 = ((f32[16,16,128]{2,1,0:T(8,128)}), f32[16,16,128]{2,1,0:T(8,128)S(1)}, u32[]{:S(2)}, u32[]{:S(2)}) async-start(f32[16,16,128]{2,1,0:T(8,128)} %bitcast.3), calls=%async_computation.1 | async-start | bytes 262144 | tf_op jit(solution)/shard_map/all_to_all | solution.py:252
  35.8 0.5 shard_map.76
  36.3 1.9 %collective-permute-start.2 = (bf16[10,8,2048]{2,1,0:T(8,128)(2,1)S(1)}, bf16[10,8,2048]{2,1,0:T(8,128)(2,1)S(1)}, u32[]{:S(2)}, u32[]{:S(2)}) collective-permute-start(bf16[10,8,2048]{2,1,0:T(8,128)(2,1)S(1)} %get-tuple-element.17), channel_id=1, source_target_pairs={{0,1},{1,0},{2,3},{3,2},{4,5},{5,4},{6,7},{7,6},{8,9},{9,8},{10,11... | collective-permute-start | bytes 983048 | tf_op jit(solution)/shard_map/ppermute | solution.py:249
  38.3 1.6 %collective-permute-done.2.refs_1_ = bf16[10,8,2048]{2,1,0:T(8,128)(2,1)S(1)} collective-permute-done((bf16[10,8,2048]{2,1,0:T(8,128)(2,1)S(1)}, bf16[10,8,2048]{2,1,0:T(8,128)(2,1)S(1)}, u32[]{:S(2)}, u32[]{:S(2)}) %collective-permute-start.2) | collective-permute-done | bytes 327712 | tf_op jit(solution)/shard_map/ppermute | solution.py:249
  39.9 4.3 %all-to-all-done.1.refs_0_ = f32[16,16,128]{2,1,0:T(8,128)S(1)} async-done(((f32[16,16,128]{2,1,0:T(8,128)}), f32[16,16,128]{2,1,0:T(8,128)S(1)}, u32[]{:S(2)}, u32[]{:S(2)}) %all-to-all-start.1) | async-done | bytes 131104 | tf_op jit(solution)/shard_map/all_to_all | solution.py:252
  44.2 0.6 shard_map.78.refs_4_
  44.8 17.4 %all-to-all-start.2 = ((f32[8,16,128]{2,1,0:T(8,128)}), f32[8,16,128]{2,1,0:T(8,128)S(1)}, u32[]{:S(2)}, u32[]{:S(2)}) async-start(f32[8,16,128]{2,1,0:T(8,128)} %shard_map.78.refs_4_), calls=%async_computation.2 | async-start | bytes 131072 | tf_op jit(solution)/shard_map/all_to_all | solution.py:259
  62.2 0.1 shard_map.79
  62.4 3.4 %collective-permute-start.4 = (bf16[48,2048]{1,0:T(8,128)(2,1)S(1)}, bf16[48,2048]{1,0:T(8,128)(2,1)S(1)}, u32[]{:S(2)}, u32[]{:S(2)}) collective-permute-start(bf16[48,2048]{1,0:T(8,128)(2,1)S(1)} %get-tuple-element.19), channel_id=1, source_target_pairs={{0,4},{1,5},{2,6},{3,7},{4,0},{5,1},{6,2},{7,3},{8,12},{9,13},{10,... | collective-permute-start | bytes 589832 | tf_op jit(solution)/shard_map/ppermute | solution.py:267
  65.7 1.9 %collective-permute-start.5 = (bf16[48,2048]{1,0:T(8,128)(2,1)S(1)}, bf16[48,2048]{1,0:T(8,128)(2,1)S(1)}, u32[]{:S(2)}, u32[]{:S(2)}) collective-permute-start(bf16[48,2048]{1,0:T(8,128)(2,1)S(1)} %get-tuple-element.20), channel_id=1, source_target_pairs={{0,6},{1,7},{2,0},{3,1},{4,2},{5,3},{6,4},{7,5},{8,14},{9,15},{10,... | collective-permute-start | bytes 589832 | tf_op jit(solution)/shard_map/ppermute | solution.py:267
  67.7 5.1 %collective-permute-start.3 = (bf16[48,2048]{1,0:T(8,128)(2,1)S(1)}, bf16[48,2048]{1,0:T(8,128)(2,1)S(1)}, u32[]{:S(2)}, u32[]{:S(2)}) collective-permute-start(bf16[48,2048]{1,0:T(8,128)(2,1)S(1)} %get-tuple-element.18.own), channel_id=1, source_target_pairs={{0,2},{1,3},{2,4},{3,5},{4,6},{5,7},{6,0},{7,1},{8,10},{9,11},{10,... | collective-permute-start | bytes 589832 | tf_op jit(solution)/shard_map/ppermute | solution.py:267
  72.8 0.0 collective-permute-done.4.second.refs_2_
  72.8 2.0 %collective-permute-done.5.third.refs_3_ = bf16[48,2048]{1,0:T(8,128)(2,1)S(1)} collective-permute-done((bf16[48,2048]{1,0:T(8,128)(2,1)S(1)}, bf16[48,2048]{1,0:T(8,128)(2,1)S(1)}, u32[]{:S(2)}, u32[]{:S(2)}) %collective-permute-start.5) | collective-permute-done | bytes 196640 | tf_op jit(solution)/shard_map/ppermute | solution.py:267
  74.8 1.1 %collective-permute-done.3.first.refs_1_ = bf16[48,2048]{1,0:T(8,128)(2,1)S(1)} collective-permute-done((bf16[48,2048]{1,0:T(8,128)(2,1)S(1)}, bf16[48,2048]{1,0:T(8,128)(2,1)S(1)}, u32[]{:S(2)}, u32[]{:S(2)}) %collective-permute-start.3) | collective-permute-done | bytes 196640 | tf_op jit(solution)/shard_map/ppermute | solution.py:267
  76.0 9.0 %all-to-all-done.2.refs_0_ = f32[8,16,128]{2,1,0:T(8,128)S(1)} async-done(((f32[8,16,128]{2,1,0:T(8,128)}), f32[8,16,128]{2,1,0:T(8,128)S(1)}, u32[]{:S(2)}, u32[]{:S(2)}) %all-to-all-start.2) | async-done | bytes 65568 | tf_op jit(solution)/shard_map/all_to_all | solution.py:259
  84.9 0.7 shard_map.82
  85.6 6.1 %all-to-all-start.3 = ((f32[16,16,128]{2,1,0:T(8,128)}), f32[16,16,128]{2,1,0:T(8,128)S(1)}, u32[]{:S(2)}, u32[]{:S(2)}) async-start(f32[16,16,128]{2,1,0:T(8,128)} %shard_map.82), calls=%async_computation.3 | async-start | bytes 262144 | tf_op jit(solution)/shard_map/all_to_all | solution.py:277
  91.7 0.7 shard_map.81
  92.4 0.7 copy-done.2
  93.0 1.1 %shard_map.80 = bf16[16,1,16,128]{3,2,1,0:T(8,128)(2,1)} custom-call(bf16[3,3,3,16,64]{4,3,2,1,0:T(8,128)(2,1)S(1)} %bitcast.11, f32[1,16]{1,0:T(1,128)S(1)} %bitcast.12, bf16[64,2048]{1,0:T(8,128)(2,1)S(1)} %bitcast.8, bf16[48,2048]{1,0:T(8,128)(2,1)S(1)} %get-tuple-element.18.own, bf16[48,2048]{1,0:T(8,128)(2,1)S(1)} %collective-permute-done.3.first.refs_1_, ...), custom_call_target="tpu_custom_call" | custom-call | flops 113246208 | bytes 1169472 | tf_op jit(solution)/shard_map/pallas_call | solution.py:30
  94.1 6.0 %all-to-all-done.3 = f32[16,16,128]{2,1,0:T(8,128)S(1)} async-done(((f32[16,16,128]{2,1,0:T(8,128)}), f32[16,16,128]{2,1,0:T(8,128)S(1)}, u32[]{:S(2)}, u32[]{:S(2)}) %all-to-all-start.3) | async-done | bytes 131104 | tf_op jit(solution)/shard_map/all_to_all | solution.py:277
  100.1 0.8 shard_map.83
  (3 shorter events, 0.0 us)
Async XLA Ops:
  2.2 16.4 %copy-start.1 = (bf16[24,2048]{1,0:T(8,128)(2,1)S(1)}, bf16[24,2048]{1,0:T(8,128)(2,1)}, u32[]{:S(2)}) copy-start(bf16[24,2048]{1,0:T(8,128)(2,1)} %get-tuple-element.15.here) | copy-start | bytes 294916
  2.3 24.4 %all-to-all-start = ((bf16[8,8,2048]{2,1,0:T(8,128)(2,1)}), bf16[8,8,2048]{2,1,0:T(8,128)(2,1)S(1)}, u32[]{:S(2)}, u32[]{:S(2)}) async-start(bf16[8,8,2048]{2,1,0:T(8,128)(2,1)} %get-tuple-element.14), calls=%async_computation | async-start | bytes 524288 | tf_op jit(solution)/shard_map/all_to_all | solution.py:235
  18.6 3.9 %collective-permute-start.1 = (bf16[24,2048]{1,0:T(8,128)(2,1)S(1)}, bf16[24,2048]{1,0:T(8,128)(2,1)S(1)}, u32[]{:S(2)}, u32[]{:S(2)}) collective-permute-start(bf16[24,2048]{1,0:T(8,128)(2,1)S(1)} %copy-done.1), channel_id=1, source_target_pairs={{0,8},{8,16},{16,24},{24,32},{32,40},{40,48},{48,56},{56,64},{64,7... | collective-permute-start | bytes 294920 | tf_op jit(solution)/shard_map/ppermute | solution.py:233
  19.9 6.7 %collective-permute-start = (bf16[24,2048]{1,0:T(8,128)(2,1)S(1)}, bf16[24,2048]{1,0:T(8,128)(2,1)S(1)}, u32[]{:S(2)}, u32[]{:S(2)}) collective-permute-start(bf16[24,2048]{1,0:T(8,128)(2,1)S(1)} %copy-done.1), channel_id=1, source_target_pairs={{8,0},{16,8},{24,16},{32,24},{40,32},{48,40},{56,48},{64,56},{72,6... | collective-permute-start | bytes 294920 | tf_op jit(solution)/shard_map/ppermute | solution.py:234
  27.9 7.9 %copy-start = (bf16[3,3,3,64,16]{3,4,2,1,0:T(8,128)(2,1)S(1)}, bf16[3,3,3,64,16]{3,4,2,1,0:T(8,128)(2,1)}, u32[]{:S(2)}) copy-start(bf16[3,3,3,64,16]{3,4,2,1,0:T(8,128)(2,1)} %param.5) | copy-start | bytes 165892
  27.9 16.3 %all-to-all-start.1 = ((f32[16,16,128]{2,1,0:T(8,128)}), f32[16,16,128]{2,1,0:T(8,128)S(1)}, u32[]{:S(2)}, u32[]{:S(2)}) async-start(f32[16,16,128]{2,1,0:T(8,128)} %bitcast.3), calls=%async_computation.1 | async-start | bytes 262144 | tf_op jit(solution)/shard_map/all_to_all | solution.py:252
  36.3 3.5 %collective-permute-start.2 = (bf16[10,8,2048]{2,1,0:T(8,128)(2,1)S(1)}, bf16[10,8,2048]{2,1,0:T(8,128)(2,1)S(1)}, u32[]{:S(2)}, u32[]{:S(2)}) collective-permute-start(bf16[10,8,2048]{2,1,0:T(8,128)(2,1)S(1)} %get-tuple-element.17), channel_id=1, source_target_pairs={{0,1},{1,0},{2,3},{3,2},{4,5},{5,4},{6,7},{7,6},{8,9},{9,8},{10,11... | collective-permute-start | bytes 983048 | tf_op jit(solution)/shard_map/ppermute | solution.py:249
  44.8 40.1 %all-to-all-start.2 = ((f32[8,16,128]{2,1,0:T(8,128)}), f32[8,16,128]{2,1,0:T(8,128)S(1)}, u32[]{:S(2)}, u32[]{:S(2)}) async-start(f32[8,16,128]{2,1,0:T(8,128)} %shard_map.78.refs_4_), calls=%async_computation.2 | async-start | bytes 131072 | tf_op jit(solution)/shard_map/all_to_all | solution.py:259
  62.4 10.4 %collective-permute-start.4 = (bf16[48,2048]{1,0:T(8,128)(2,1)S(1)}, bf16[48,2048]{1,0:T(8,128)(2,1)S(1)}, u32[]{:S(2)}, u32[]{:S(2)}) collective-permute-start(bf16[48,2048]{1,0:T(8,128)(2,1)S(1)} %get-tuple-element.19), channel_id=1, source_target_pairs={{0,4},{1,5},{2,6},{3,7},{4,0},{5,1},{6,2},{7,3},{8,12},{9,13},{10,... | collective-permute-start | bytes 589832 | tf_op jit(solution)/shard_map/ppermute | solution.py:267
  65.7 9.1 %collective-permute-start.5 = (bf16[48,2048]{1,0:T(8,128)(2,1)S(1)}, bf16[48,2048]{1,0:T(8,128)(2,1)S(1)}, u32[]{:S(2)}, u32[]{:S(2)}) collective-permute-start(bf16[48,2048]{1,0:T(8,128)(2,1)S(1)} %get-tuple-element.20), channel_id=1, source_target_pairs={{0,6},{1,7},{2,0},{3,1},{4,2},{5,3},{6,4},{7,5},{8,14},{9,15},{10,... | collective-permute-start | bytes 589832 | tf_op jit(solution)/shard_map/ppermute | solution.py:267
  67.7 8.3 %collective-permute-start.3 = (bf16[48,2048]{1,0:T(8,128)(2,1)S(1)}, bf16[48,2048]{1,0:T(8,128)(2,1)S(1)}, u32[]{:S(2)}, u32[]{:S(2)}) collective-permute-start(bf16[48,2048]{1,0:T(8,128)(2,1)S(1)} %get-tuple-element.18.own), channel_id=1, source_target_pairs={{0,2},{1,3},{2,4},{3,5},{4,6},{5,7},{6,0},{7,1},{8,10},{9,11},{10,... | collective-permute-start | bytes 589832 | tf_op jit(solution)/shard_map/ppermute | solution.py:267
  85.6 14.5 %all-to-all-start.3 = ((f32[16,16,128]{2,1,0:T(8,128)}), f32[16,16,128]{2,1,0:T(8,128)S(1)}, u32[]{:S(2)}, u32[]{:S(2)}) async-start(f32[16,16,128]{2,1,0:T(8,128)} %shard_map.82), calls=%async_computation.3 | async-start | bytes 262144 | tf_op jit(solution)/shard_map/all_to_all | solution.py:277
  92.4 0.7 copy-start.2

commit v3 on v2

--- a/solution.py
+++ b/solution.py
@@ -79,11 +79,15 @@
     return jnp.concatenate(parts, axis=1)
 
 
-def pack_body(volume, grad, volume_out, plane_out, here_v, here_g, spare_v, spare_g, sems):
+def pack_body(
+    volume, grad, bias, volume_out, plane_out, bias_out, here_v, here_g, here_b, spare_v, spare_g, sems
+):
     copy_g = pltpu.make_async_copy(grad, here_g, sems.at[0])
     copy_v = pltpu.make_async_copy(volume, here_v, sems.at[1])
+    copy_b = pltpu.make_async_copy(bias, here_b, sems.at[2])
     copy_v.start()
     copy_g.start()
+    copy_b.start()
     copy_v.wait()
     flat = cells_to_lanes(here_v, spare_v)
     for k in range(volume_out.shape[0]):
@@ -91,6 +95,11 @@
     plane_out[16:24] = flat
     copy_g.wait()
     plane_out[0:16] = cells_to_lanes(here_g, spare_g)
+    copy_b.wait()
+    row = lax.broadcasted_iota(jnp.int32, (16, 16), 0)
+    lane = lax.broadcasted_iota(jnp.int32, (16, 16), 1)
+    column = jnp.sum(jnp.where(row == lane, here_b[...], 0.0), axis=1, keepdims=True)
+    bias_out[...] = jnp.broadcast_to(column, (16, COLS))
 
 
 def kernel_grad_body(volume, after, here, before, out):
@@ -136,7 +145,7 @@
     bias_out[...] = flat[216:217, 0:16]
 
 
-def input_grad_body(kernel, after, here, before, kept, sent):
+def input_grad_body(kernel, after, here, before, own, first, second, third, blocks):
     left = jnp.concatenate([kernel[:, b].reshape(144, 64) for b in range(3)], axis=1)
     right = jnp.concatenate(
         [from_col(g[0:16], 1 - c) for g in (after, here, before) for c in range(3)], axis=0
@@ -145,13 +154,14 @@
     total = sums[64:128]
     total = total + from_row(sums[0:64], 1)
     total = total + from_row(sums[128:192], -1)
-    odd = lax.rem(lax.axis_index("chan"), 2) == 1
     for y in range(4):
-        first, second = total[16 * y : 16 * y + 8], total[16 * y + 8 : 16 * y + 16]
-        kept[y] = jnp.where(odd, second, first)
-        sent[y], sent[4 + y] = halves(jnp.where(odd, first, second))
-    sent[8] = before[16:24]
-    sent[9] = after[16:24]
+        blocks[y] = total[16 * y : 16 * y + 16]
+    y = lax.div(lax.axis_index("chan"), 2)
+    own[...] = blocks[y]
+    for k, out in enumerate((first, second, third)):
+        out[0:16], out[16:32] = halves(blocks[lax.rem(y + k + 1, 4)])
+        out[32:40] = before[16:24]
+        out[40:48] = after[16:24]
 
 
 def halves(value):
@@ -159,53 +169,45 @@
     return high, (value - high.astype(F32)).astype(BF16)
 
 
-def join_body(kept, got, before, after, own, *sent):
+def join_body(own, first, second, third, before, after, kept, sent):
     chan = lax.axis_index("chan")
     y, odd = lax.div(chan, 2), lax.rem(chan, 2) == 1
-    for k, out in enumerate((own, *sent)):
-        block = lax.rem(y + k, 4)
-        total = kept[block] + got[block].astype(F32) + got[4 + block].astype(F32)
-        if k == 0:
-            out[...] = total
-        else:
-            out[0:8], out[8:16] = halves(total)
-    for row, mine, theirs in ((16, before, got[8]), (32, after, got[9])):
-        mine, theirs = mine[16:24].astype(F32), theirs.astype(F32)
-        first = jnp.where(odd, theirs, mine).astype(BF16)
-        second = jnp.where(odd, mine, theirs).astype(BF16)
-        for out in sent:
-            out[row : row + 8] = first
-            out[row + 8 : row + 16] = second
-
-
-def feature_body(kernel, bias, here, own, first, second, third, out, before, after, spare):
-    y = lax.div(lax.axis_index("chan"), 2)
-    for k, part in enumerate((own, first, second, third)):
-        place = pl.ds(pl.multiple_of(16 * lax.rem(y + 4 - k, 4), 16), 16)
-        before[place] = part[16:32]
-        after[place] = part[32:48]
+    total = own[...]
+    for part in (first, second, third):
+        total = total + (part[0:16].astype(F32) + part[16:32].astype(F32))
+    kept[...] = jnp.where(odd, total[8:16], total[0:8])
+    sent[0], sent[1] = halves(jnp.where(odd, total[0:8], total[8:16]))
+    sent[2 + 2 * y] = before[16:24]
+    sent[3 + 2 * y] = after[16:24]
+    for k, part in enumerate((first, second, third)):
+        source = lax.rem(y + 3 - k, 4)
+        sent[2 + 2 * source] = part[32:40]
+        sent[3 + 2 * source] = part[40:48]
+
+
+def narrow_body(kept, got, out, spare):
+    total = kept[...] + (got[0].astype(F32) + got[1].astype(F32))
+    out[...] = lanes_to_cells(total, spare)
+
+
+def feature_body(kernel, bias, here, mine, theirs, out, before, after, spare):
+    odd = lax.rem(lax.axis_index("chan"), 2) == 1
+    for side, plane in enumerate((before, after)):
+        for y in range(4):
+            a, b = mine[2 + 2 * y + side].astype(F32), theirs[2 + 2 * y + side].astype(F32)
+            plane[16 * y : 16 * y + 8] = jnp.where(odd, b, a).astype(BF16)
+            plane[16 * y + 8 : 16 * y + 16] = jnp.where(odd, a, b).astype(BF16)
     left = jnp.concatenate([kernel[a].reshape(144, 64) for a in range(3)], axis=1)
     right = jnp.concatenate([before[...], here[...], after[...]], axis=0)
     sums = jnp.dot(left, right, preferred_element_type=F32)
-    total = None
-    for c in (1, 0, 2):
+    total = jnp.concatenate([bias[...]] * ROWS, axis=1)
+    for c in range(3):
         part = None
         for b in range(3):
             r = (b * 3 + c) * 16
             term = from_row(sums[r : r + 16], b - 1)
             part = term if part is None else part + term
-        part = from_col(part, c - 1)
-        total = part if total is None else total + part
-    row = lax.broadcasted_iota(jnp.int32, (16, 16), 0)
-    lane = lax.broadcasted_iota(jnp.int32, (16, 16), 1)
-    column = jnp.sum(jnp.where(row == lane, bias[...], 0.0), axis=1, keepdims=True)
-    out[...] = lanes_to_cells(total + column, spare)
-
-
-def narrow_body(own, first, second, third, out, spare):
-    total = own[...]
-    for part in (first, second, third):
-        total = total + (part[0:8].astype(F32) + part[8:16].astype(F32))
+        total = total + from_col(part, c - 1)
     out[...] = lanes_to_cells(total, spare)
 
 
@@ -216,16 +218,17 @@
     down = [(i + 1, i) for i in range(slabs - 1)]
     weights = jnp.transpose(kernel, (0, 1, 2, 4, 3))
 
-    sent, here = call(
+    sent, here, column = call(
         pack_body,
-        [shape((groups, 8, CELLS), BF16), shape((24, CELLS), BF16)],
-        [volume, out_grad],
+        [shape((groups, 8, CELLS), BF16), shape((24, CELLS), BF16), shape((16, COLS), F32)],
+        [volume, out_grad, bias.reshape(1, 16)],
         [
             pltpu.VMEM(volume.shape, BF16),
             pltpu.VMEM(out_grad.shape, BF16),
+            pltpu.VMEM((1, 16), F32),
             pltpu.VMEM((8 * ROWS, COLS), F32),
             pltpu.VMEM((16 * ROWS, COLS), F32),
-            pltpu.SemaphoreType.DMA((2,)),
+            pltpu.SemaphoreType.DMA((3,)),
         ],
         anywhere=True,
         limit=60,
@@ -240,13 +243,17 @@
         [whole, after, here, before],
         flops=2 * 144 * 192 * CELLS,
     )
-    kept, sent = call(
+    own, *shares = call(
         input_grad_body,
-        [shape((4, 8, CELLS), F32), shape((10, 8, CELLS), BF16)],
+        [shape((16, CELLS), F32)] + [shape((48, CELLS), BF16)] * 3,
         [weights, after, here, before],
+        [pltpu.VMEM((4, 16, CELLS), F32)],
         flops=2 * 144 * 192 * CELLS,
     )
-    got = lax.ppermute(sent, "chan", [(i, i ^ 1) for i in range(groups)])
+    others = [
+        lax.ppermute(part, "chan", [(i, (i + 2 * k + 2) % groups) for i in range(groups)])
+        for k, part in enumerate(shares)
+    ]
     near = X * ZL
     rows = 256 // near
     parts = lax.all_to_all(partial.reshape(near, rows, 128), NEAR, 0, 0)
@@ -254,25 +261,22 @@
         functools.partial(sum_body, None),
         [shape((ZH, rows, 128), F32)],
         [parts],
-        after=[got],
+        after=[others[0]],
     )
     parts = lax.all_to_all(spread, "zh", 0, 0)
-    own, *joined = call(
+    kept, sent = call(
         join_body,
-        [shape((8, CELLS), F32)] + [shape((48, CELLS), BF16)] * 3,
-        [kept, got, before, after],
+        [shape((8, CELLS), F32), shape((10, 8, CELLS), BF16)],
+        [own, *others, before, after],
         after=[spread],
     )
-    others = [
-        lax.ppermute(part, "chan", [(i, (i + 2 * k + 2) % groups) for i in range(groups)])
-        for k, part in enumerate(joined)
-    ]
+    got = lax.ppermute(sent, "chan", [(i, i ^ 1) for i in range(groups)])
     factor = 1.0 / math.sqrt(slabs * CELLS)
     (spread,) = call(
         functools.partial(sum_body, factor),
         [shape((near, rows, 128), F32)],
         [parts],
-        after=[*others],
+        after=[kept],
     )
     flat = lax.all_to_all(spread, NEAR, 0, 0).reshape(256, 128)
     kernel_out, bias_out = call(
@@ -282,14 +286,14 @@
     (input_grad,) = call(
         narrow_body,
         [shape((8, 1, ROWS, COLS), BF16)],
-        [own, *others],
+        [kept, got],
         [pltpu.VMEM((8 * ROWS, COLS), F32)],
     )
 
     (feature,) = call(
         feature_body,
         [shape((16, 1, ROWS, COLS), BF16)],
-        [weights, bias.reshape(1, 16), whole, joined[0], *others],
+        [weights, column, whole, sent, got],
         [
             pltpu.VMEM((64, CELLS), BF16),
             pltpu.VMEM((64, CELLS), BF16),

time: 102 us -> 103 us (level)
  waiting for transfers between devices: 29.5 us -> 31.1 us
    ppermute x3, waiting for transfers between devices: 3.16 us -> 11.7 us  [on_device(): lax.ppermute(part, 'chan', [(i, (i + 2 * k + 2) % groups) for i in range(...]
    all_to_all x1, starting transfers between devices: 17.4 us -> 11.8 us  [on_device(): parts = lax.all_to_all(spread, 'zh', 0, 0)]
    all_to_all x1, starting transfers between devices: 7.93 us -> 12.3 us  [on_device(): parts = lax.all_to_all(partial.reshape(near, rows, 128), NEAR, 0, 0)]
    all_to_all x1, waiting for transfers between devices: 4.34 us -> 0.26 us  [on_device(): parts = lax.all_to_all(partial.reshape(near, rows, 128), NEAR, 0, 0)]
    all_to_all x1, waiting for transfers between devices: 8.95 us -> 12.2 us  [on_device(): parts = lax.all_to_all(spread, 'zh', 0, 0)]
    ppermute x1, starting transfers between devices: 1.28 us -> 4.55 us  [on_device(): before = lax.ppermute(here, SLAB, up)]
    ppermute x1, waiting for transfers between devices: 4.12 us -> 0.88 us  [on_device(): after = lax.ppermute(here, SLAB, down)]
    all_to_all x1, waiting for transfers between devices: 6 us -> 3.14 us  [on_device(): flat = lax.all_to_all(spread, NEAR, 0, 0).reshape(256, 128)]
  transfers between devices with their start and end apart: 10 -> 10, of which waited for: 8 -> 9; matrix products, arithmetic and copies ran while one was open for 0% -> 0% of each run, Pallas kernels for 2% -> 2%
where the time goes in v3:
time: 103 us; the launch traced here: 101 us
  starting transfers between devices  62.1 us (60%)
  waiting for transfers between devices  31.1 us (30%)
  Pallas kernels  7.36 us (7%)
    all_to_all x1, starting transfers between devices, on_device(): whole = lax.all_to_all(sent, 'chan', 0, 0).reshape(64, CELLS)  16.4 us
    all_to_all x1, starting transfers between devices, on_device(): parts = lax.all_to_all(partial.reshape(near, rows, 128), NEAR, 0, 0)  12.3 us
    all_to_all x1, waiting for transfers between devices, on_device(): parts = lax.all_to_all(spread, 'zh', 0, 0)  12.2 us
    all_to_all x1, starting transfers between devices, on_device(): parts = lax.all_to_all(spread, 'zh', 0, 0)  11.8 us
    ppermute x3, waiting for transfers between devices, on_device(): lax.ppermute(part, 'chan', [(i, (i + 2 * k + 2) % groups) for i in range(...  11.7 us
    ppermute x3, starting transfers between devices, on_device(): lax.ppermute(part, 'chan', [(i, (i + 2 * k + 2) % groups) for i in range(...  8.39 us
    pallas_call x9, Pallas kernels, call(): pl.pallas_call(inner, out_shape=tuple(outs), in_specs=[pl.BlockSpec(memor...  7.36 us
    all_to_all x1, starting transfers between devices, on_device(): flat = lax.all_to_all(spread, NEAR, 0, 0).reshape(256, 128)  5.49 us
  transfers between devices with their start and end apart: 10, of which 9 were waited for; matrix products, arithmetic and copies ran while one was open for 0% of the time, Pallas kernels for 2%

profile of v3, /device:TPU:24, one launch (start us, length us, event | category | flops | bytes accessed | tf_op | source)
XLA Modules:
  0.0 101.4 jit_solution(15374413730058027917)
XLA Ops:
  0.6 1.7 %shard_map.75 = (bf16[8,8,2048]{2,1,0:T(8,128)(2,1)}, bf16[24,2048]{1,0:T(8,128)(2,1)}, f32[16,128]{1,0:T(8,128)}) custom-call(bf16[8,1,16,128]{3,2,1,0:T(8,128)(2,1)} %volume.1, bf16[16,1,16,128]{3,2,1,0:T(8,128)(2,1)} %grad.1, f32[1,16]{1,0:T(1,128)} %bitcast.12), custom_call_target="tpu_custom_call" | custom-call | bytes 467008 | tf_op jit(solution)/shard_map/pallas_call | solution.py:30
  2.3 0.0 copy-start.1
  2.3 16.4 %all-to-all-start = ((bf16[8,8,2048]{2,1,0:T(8,128)(2,1)}), bf16[8,8,2048]{2,1,0:T(8,128)(2,1)S(1)}, u32[]{:S(2)}, u32[]{:S(2)}) async-start(bf16[8,8,2048]{2,1,0:T(8,128)(2,1)} %get-tuple-element.16), calls=%async_computation | async-start | bytes 524288 | tf_op jit(solution)/shard_map/all_to_all | solution.py:238
  18.7 0.0 copy-done.1
  18.7 1.3 %collective-permute-start = (bf16[24,2048]{1,0:T(8,128)(2,1)S(1)}, bf16[24,2048]{1,0:T(8,128)(2,1)S(1)}, u32[]{:S(2)}, u32[]{:S(2)}) collective-permute-start(bf16[24,2048]{1,0:T(8,128)(2,1)S(1)} %copy-done.1), channel_id=1, source_target_pairs={{8,0},{16,8},{24,16},{32,24},{40,32},{48,40},{56,48},{64,56},{72,6... | collective-permute-start | bytes 294920 | tf_op jit(solution)/shard_map/ppermute | solution.py:237
  20.0 4.6 %collective-permute-start.1 = (bf16[24,2048]{1,0:T(8,128)(2,1)S(1)}, bf16[24,2048]{1,0:T(8,128)(2,1)S(1)}, u32[]{:S(2)}, u32[]{:S(2)}) collective-permute-start(bf16[24,2048]{1,0:T(8,128)(2,1)S(1)} %copy-done.1), channel_id=1, source_target_pairs={{0,8},{8,16},{16,24},{24,32},{32,40},{40,48},{48,56},{56,64},{64,7... | collective-permute-start | bytes 294920 | tf_op jit(solution)/shard_map/ppermute | solution.py:236
  24.5 0.9 collective-permute-done.after.refs_5_
  25.4 1.3 %collective-permute-done.1.before.refs_4_ = bf16[24,2048]{1,0:T(8,128)(2,1)S(1)} collective-permute-done((bf16[24,2048]{1,0:T(8,128)(2,1)S(1)}, bf16[24,2048]{1,0:T(8,128)(2,1)S(1)}, u32[]{:S(2)}, u32[]{:S(2)}) %collective-permute-start.1) | collective-permute-done | bytes 98336 | tf_op jit(solution)/shard_map/ppermute | solution.py:236
  26.7 0.0 all-to-all-done
  26.7 1.2 %shard_map.77 = f32[256,128]{1,0:T(8,128)} custom-call(bf16[64,2048]{1,0:T(8,128)(2,1)S(1)} %bitcast.7, bf16[24,2048]{1,0:T(8,128)(2,1)S(1)} %collective-permute-done.after.refs_5_, bf16[24,2048]{1,0:T(8,128)(2,1)S(1)} %copy-done.1, bf16[24,2048]{1,0:T(8,128)(2,1)S(1)} %collective-permute-done.1.before.refs_4_), custom_call_target="tpu_custom_call" | custom-call | flops 113246208 | bytes 688128 | tf_op jit(solution)/shard_map/pallas_call | solution.py:30
  27.9 12.3 %all-to-all-start.1 = ((f32[16,16,128]{2,1,0:T(8,128)}), f32[16,16,128]{2,1,0:T(8,128)S(1)}, u32[]{:S(2)}, u32[]{:S(2)}) async-start(f32[16,16,128]{2,1,0:T(8,128)} %bitcast.3), calls=%async_computation.1 | async-start | bytes 262144 | tf_op jit(solution)/shard_map/all_to_all | solution.py:259
  40.2 0.0 copy-done
  40.2 0.6 shard_map.76
  40.8 2.2 %collective-permute-start.2 = (bf16[48,2048]{1,0:T(8,128)(2,1)S(1)}, bf16[48,2048]{1,0:T(8,128)(2,1)S(1)}, u32[]{:S(2)}, u32[]{:S(2)}) collective-permute-start(bf16[48,2048]{1,0:T(8,128)(2,1)S(1)} %get-tuple-element.19), channel_id=1, source_target_pairs={{0,2},{1,3},{2,4},{3,5},{4,6},{5,7},{6,0},{7,1},{8,10},{9,11},{10,... | collective-permute-start | bytes 589832 | tf_op jit(solution)/shard_map/ppermute | solution.py:254
  43.0 5.3 %collective-permute-done.2.refs_1_ = bf16[48,2048]{1,0:T(8,128)(2,1)S(1)} collective-permute-done((bf16[48,2048]{1,0:T(8,128)(2,1)S(1)}, bf16[48,2048]{1,0:T(8,128)(2,1)S(1)}, u32[]{:S(2)}, u32[]{:S(2)}) %collective-permute-start.2) | collective-permute-done | bytes 196640 | tf_op jit(solution)/shard_map/ppermute | solution.py:254
  48.4 0.3 all-to-all-done.1.refs_0_
  48.6 0.6 shard_map.78.refs_6_
  49.3 11.8 %all-to-all-start.2 = ((f32[8,16,128]{2,1,0:T(8,128)}), f32[8,16,128]{2,1,0:T(8,128)S(1)}, u32[]{:S(2)}, u32[]{:S(2)}) async-start(f32[8,16,128]{2,1,0:T(8,128)} %shard_map.78.refs_6_), calls=%async_computation.2 | async-start | bytes 131072 | tf_op jit(solution)/shard_map/all_to_all | solution.py:266
  61.1 3.4 %collective-permute-start.3 = (bf16[48,2048]{1,0:T(8,128)(2,1)S(1)}, bf16[48,2048]{1,0:T(8,128)(2,1)S(1)}, u32[]{:S(2)}, u32[]{:S(2)}) collective-permute-start(bf16[48,2048]{1,0:T(8,128)(2,1)S(1)} %get-tuple-element.20), channel_id=1, source_target_pairs={{0,4},{1,5},{2,6},{3,7},{4,0},{5,1},{6,2},{7,3},{8,12},{9,13},{10,... | collective-permute-start | bytes 589832 | tf_op jit(solution)/shard_map/ppermute | solution.py:254
  64.5 2.8 %collective-permute-start.4 = (bf16[48,2048]{1,0:T(8,128)(2,1)S(1)}, bf16[48,2048]{1,0:T(8,128)(2,1)S(1)}, u32[]{:S(2)}, u32[]{:S(2)}) collective-permute-start(bf16[48,2048]{1,0:T(8,128)(2,1)S(1)} %get-tuple-element.21), channel_id=1, source_target_pairs={{0,6},{1,7},{2,0},{3,1},{4,2},{5,3},{6,4},{7,5},{8,14},{9,15},{10,... | collective-permute-start | bytes 589832 | tf_op jit(solution)/shard_map/ppermute | solution.py:254
  67.3 4.3 %collective-permute-done.3.refs_2_ = bf16[48,2048]{1,0:T(8,128)(2,1)S(1)} collective-permute-done((bf16[48,2048]{1,0:T(8,128)(2,1)S(1)}, bf16[48,2048]{1,0:T(8,128)(2,1)S(1)}, u32[]{:S(2)}, u32[]{:S(2)}) %collective-permute-start.3) | collective-permute-done | bytes 196640 | tf_op jit(solution)/shard_map/ppermute | solution.py:254
  71.6 2.1 %collective-permute-done.4.refs_3_ = bf16[48,2048]{1,0:T(8,128)(2,1)S(1)} collective-permute-done((bf16[48,2048]{1,0:T(8,128)(2,1)S(1)}, bf16[48,2048]{1,0:T(8,128)(2,1)S(1)}, u32[]{:S(2)}, u32[]{:S(2)}) %collective-permute-start.4) | collective-permute-done | bytes 196640 | tf_op jit(solution)/shard_map/ppermute | solution.py:254
  73.7 0.1 shard_map.79
  73.8 12.2 %all-to-all-done.2.refs_0_ = f32[8,16,128]{2,1,0:T(8,128)S(1)} async-done(((f32[8,16,128]{2,1,0:T(8,128)}), f32[8,16,128]{2,1,0:T(8,128)S(1)}, u32[]{:S(2)}, u32[]{:S(2)}) %all-to-all-start.2) | async-done | bytes 65568 | tf_op jit(solution)/shard_map/all_to_all | solution.py:266
  86.0 0.7 shard_map.82
  86.7 5.5 %all-to-all-start.3 = ((f32[16,16,128]{2,1,0:T(8,128)}), f32[16,16,128]{2,1,0:T(8,128)S(1)}, u32[]{:S(2)}, u32[]{:S(2)}) async-start(f32[16,16,128]{2,1,0:T(8,128)} %shard_map.82), calls=%async_computation.3 | async-start | bytes 262144 | tf_op jit(solution)/shard_map/all_to_all | solution.py:281
  92.2 1.9 %collective-permute-start.5 = (bf16[10,8,2048]{2,1,0:T(8,128)(2,1)S(1)}, bf16[10,8,2048]{2,1,0:T(8,128)(2,1)S(1)}, u32[]{:S(2)}, u32[]{:S(2)}) collective-permute-start(bf16[10,8,2048]{2,1,0:T(8,128)(2,1)S(1)} %get-tuple-element.22.mine), channel_id=1, source_target_pairs={{0,1},{1,0},{2,3},{3,2},{4,5},{5,4},{6,7},{7,6},{8,9},{9,8},{10,11... | collective-permute-start | bytes 983048 | tf_op jit(solution)/shard_map/ppermute | solution.py:273
  94.1 1.6 %collective-permute-done.5.theirs.got = bf16[10,8,2048]{2,1,0:T(8,128)(2,1)S(1)} collective-permute-done((bf16[10,8,2048]{2,1,0:T(8,128)(2,1)S(1)}, bf16[10,8,2048]{2,1,0:T(8,128)(2,1)S(1)}, u32[]{:S(2)}, u32[]{:S(2)}) %collective-permute-start.5) | collective-permute-done | bytes 327712 | tf_op jit(solution)/shard_map/ppermute | solution.py:273
  95.7 0.6 shard_map.81
  96.4 1.1 %shard_map.80 = bf16[16,1,16,128]{3,2,1,0:T(8,128)(2,1)} custom-call(bf16[3,3,3,16,64]{4,3,2,1,0:T(8,128)(2,1)S(1)} %bitcast.11, f32[16,128]{1,0:T(8,128)S(1)} %copy-done.2, bf16[64,2048]{1,0:T(8,128)(2,1)S(1)} %bitcast.8, bf16[10,8,2048]{2,1,0:T(8,128)(2,1)S(1)} %get-tuple-element.22.mine, bf16[10,8,2048]{2,1,0:T(8,128)(2,1)S(1)} %collective-permute-done.5.theirs.got), custom_call_target="tpu_custom_call" | custom-call | flops 113246208 | bytes 1046528 | tf_op jit(solution)/shard_map/pallas_call | solution.py:30
  97.4 3.1 %all-to-all-done.3 = f32[16,16,128]{2,1,0:T(8,128)S(1)} async-done(((f32[16,16,128]{2,1,0:T(8,128)}), f32[16,16,128]{2,1,0:T(8,128)S(1)}, u32[]{:S(2)}, u32[]{:S(2)}) %all-to-all-start.3) | async-done | bytes 131104 | tf_op jit(solution)/shard_map/all_to_all | solution.py:281
  100.6 0.8 shard_map.83
  (3 shorter events, 0.0 us)
Async XLA Ops:
  2.3 16.4 %copy-start.1 = (bf16[24,2048]{1,0:T(8,128)(2,1)S(1)}, bf16[24,2048]{1,0:T(8,128)(2,1)}, u32[]{:S(2)}) copy-start(bf16[24,2048]{1,0:T(8,128)(2,1)} %get-tuple-element.17.here) | copy-start | bytes 294916
  2.3 24.4 %all-to-all-start = ((bf16[8,8,2048]{2,1,0:T(8,128)(2,1)}), bf16[8,8,2048]{2,1,0:T(8,128)(2,1)S(1)}, u32[]{:S(2)}, u32[]{:S(2)}) async-start(bf16[8,8,2048]{2,1,0:T(8,128)(2,1)} %get-tuple-element.16), calls=%async_computation | async-start | bytes 524288 | tf_op jit(solution)/shard_map/all_to_all | solution.py:238
  18.7 6.7 %collective-permute-start = (bf16[24,2048]{1,0:T(8,128)(2,1)S(1)}, bf16[24,2048]{1,0:T(8,128)(2,1)S(1)}, u32[]{:S(2)}, u32[]{:S(2)}) collective-permute-start(bf16[24,2048]{1,0:T(8,128)(2,1)S(1)} %copy-done.1), channel_id=1, source_target_pairs={{8,0},{16,8},{24,16},{32,24},{40,32},{48,40},{56,48},{64,56},{72,6... | collective-permute-start | bytes 294920 | tf_op jit(solution)/shard_map/ppermute | solution.py:237
  20.0 6.8 %collective-permute-start.1 = (bf16[24,2048]{1,0:T(8,128)(2,1)S(1)}, bf16[24,2048]{1,0:T(8,128)(2,1)S(1)}, u32[]{:S(2)}, u32[]{:S(2)}) collective-permute-start(bf16[24,2048]{1,0:T(8,128)(2,1)S(1)} %copy-done.1), channel_id=1, source_target_pairs={{0,8},{8,16},{16,24},{24,32},{32,40},{40,48},{48,56},{56,64},{64,7... | collective-permute-start | bytes 294920 | tf_op jit(solution)/shard_map/ppermute | solution.py:236
  27.9 12.3 %copy-start = (bf16[3,3,3,64,16]{3,4,2,1,0:T(8,128)(2,1)S(1)}, bf16[3,3,3,64,16]{3,4,2,1,0:T(8,128)(2,1)}, u32[]{:S(2)}) copy-start(bf16[3,3,3,64,16]{3,4,2,1,0:T(8,128)(2,1)} %param.5) | copy-start | bytes 165892
  27.9 20.7 %all-to-all-start.1 = ((f32[16,16,128]{2,1,0:T(8,128)}), f32[16,16,128]{2,1,0:T(8,128)S(1)}, u32[]{:S(2)}, u32[]{:S(2)}) async-start(f32[16,16,128]{2,1,0:T(8,128)} %bitcast.3), calls=%async_computation.1 | async-start | bytes 262144 | tf_op jit(solution)/shard_map/all_to_all | solution.py:259
  40.8 7.6 %collective-permute-start.2 = (bf16[48,2048]{1,0:T(8,128)(2,1)S(1)}, bf16[48,2048]{1,0:T(8,128)(2,1)S(1)}, u32[]{:S(2)}, u32[]{:S(2)}) collective-permute-start(bf16[48,2048]{1,0:T(8,128)(2,1)S(1)} %get-tuple-element.19), channel_id=1, source_target_pairs={{0,2},{1,3},{2,4},{3,5},{4,6},{5,7},{6,0},{7,1},{8,10},{9,11},{10,... | collective-permute-start | bytes 589832 | tf_op jit(solution)/shard_map/ppermute | solution.py:254
  49.3 36.7 %all-to-all-start.2 = ((f32[8,16,128]{2,1,0:T(8,128)}), f32[8,16,128]{2,1,0:T(8,128)S(1)}, u32[]{:S(2)}, u32[]{:S(2)}) async-start(f32[8,16,128]{2,1,0:T(8,128)} %shard_map.78.refs_6_), calls=%async_computation.2 | async-start | bytes 131072 | tf_op jit(solution)/shard_map/all_to_all | solution.py:266
  61.1 10.5 %collective-permute-start.3 = (bf16[48,2048]{1,0:T(8,128)(2,1)S(1)}, bf16[48,2048]{1,0:T(8,128)(2,1)S(1)}, u32[]{:S(2)}, u32[]{:S(2)}) collective-permute-start(bf16[48,2048]{1,0:T(8,128)(2,1)S(1)} %get-tuple-element.20), channel_id=1, source_target_pairs={{0,4},{1,5},{2,6},{3,7},{4,0},{5,1},{6,2},{7,3},{8,12},{9,13},{10,... | collective-permute-start | bytes 589832 | tf_op jit(solution)/shard_map/ppermute | solution.py:254
  64.5 9.2 %collective-permute-start.4 = (bf16[48,2048]{1,0:T(8,128)(2,1)S(1)}, bf16[48,2048]{1,0:T(8,128)(2,1)S(1)}, u32[]{:S(2)}, u32[]{:S(2)}) collective-permute-start(bf16[48,2048]{1,0:T(8,128)(2,1)S(1)} %get-tuple-element.21), channel_id=1, source_target_pairs={{0,6},{1,7},{2,0},{3,1},{4,2},{5,3},{6,4},{7,5},{8,14},{9,15},{10,... | collective-permute-start | bytes 589832 | tf_op jit(solution)/shard_map/ppermute | solution.py:254
  86.7 13.9 %all-to-all-start.3 = ((f32[16,16,128]{2,1,0:T(8,128)}), f32[16,16,128]{2,1,0:T(8,128)S(1)}, u32[]{:S(2)}, u32[]{:S(2)}) async-start(f32[16,16,128]{2,1,0:T(8,128)} %shard_map.82), calls=%async_computation.3 | async-start | bytes 262144 | tf_op jit(solution)/shard_map/all_to_all | solution.py:281
  92.2 4.2 %copy-start.2 = (f32[16,128]{1,0:T(8,128)S(1)}, f32[16,128]{1,0:T(8,128)}, u32[]{:S(2)}) copy-start(f32[16,128]{1,0:T(8,128)} %get-tuple-element.15.bias) | copy-start | bytes 24580
  92.2 3.5 %collective-permute-start.5 = (bf16[10,8,2048]{2,1,0:T(8,128)(2,1)S(1)}, bf16[10,8,2048]{2,1,0:T(8,128)(2,1)S(1)}, u32[]{:S(2)}, u32[]{:S(2)}) collective-permute-start(bf16[10,8,2048]{2,1,0:T(8,128)(2,1)S(1)} %get-tuple-element.22.mine), channel_id=1, source_target_pairs={{0,1},{1,0},{2,3},{3,2},{4,5},{5,4},{6,7},{7,6},{8,9},{9,8},{10,11... | collective-permute-start | bytes 983048 | tf_op jit(solution)/shard_map/ppermute | solution.py:273

commit v4 on v3

--- a/solution.py
+++ b/solution.py
@@ -261,7 +261,6 @@
         functools.partial(sum_body, None),
         [shape((ZH, rows, 128), F32)],
         [parts],
-        after=[others[0]],
     )
     parts = lax.all_to_all(spread, "zh", 0, 0)
     kept, sent = call(

time: 103 us -> 98.4 us (0.955)
  blocking collectives: 0 us -> 20.3 us
  starting transfers between devices: 62.1 us -> 49.1 us
  waiting for transfers between devices: 31.1 us -> 20.6 us
    all_to_all x0 -> x1, blocking collectives: none -> 20.3 us  [on_device(): parts = lax.all_to_all(partial.reshape(near, rows, 128), NEAR, 0, 0)]
    all_to_all x1 -> x0, starting transfers between devices: 12.3 us -> none  [on_device(): parts = lax.all_to_all(partial.reshape(near, rows, 128), NEAR, 0, 0)]
    all_to_all x1, waiting for transfers between devices: 12.2 us -> 6.81 us  [on_device(): parts = lax.all_to_all(spread, 'zh', 0, 0)]
    ppermute x3, waiting for transfers between devices: 11.7 us -> 6.84 us  [on_device(): lax.ppermute(part, 'chan', [(i, (i + 2 * k + 2) % groups) for i in range(...]
    all_to_all x1, starting transfers between devices: 5.49 us -> 4.36 us  [on_device(): flat = lax.all_to_all(spread, NEAR, 0, 0).reshape(256, 128)]
  transfers between devices with their start and end apart: 10 -> 9, of which waited for: 9 -> 7; matrix products, arithmetic and copies ran while one was open for 0% -> 0% of each run, Pallas kernels for 2% -> 2%
where the time goes in v4:
time: 98.4 us; the launch traced here: 97.5 us
  starting transfers between devices  49.1 us (50%)
  waiting for transfers between devices  20.6 us (21%)
  blocking collectives  20.3 us (21%)
  Pallas kernels  6.71 us (7%)
    all_to_all x1, blocking collectives, on_device(): parts = lax.all_to_all(partial.reshape(near, rows, 128), NEAR, 0, 0)  20.3 us
    all_to_all x1, starting transfers between devices, on_device(): whole = lax.all_to_all(sent, 'chan', 0, 0).reshape(64, CELLS)  16.4 us
    all_to_all x1, starting transfers between devices, on_device(): parts = lax.all_to_all(spread, 'zh', 0, 0)  12 us
    ppermute x3, starting transfers between devices, on_device(): lax.ppermute(part, 'chan', [(i, (i + 2 * k + 2) % groups) for i in range(...  8.67 us
    ppermute x3, waiting for transfers between devices, on_device(): lax.ppermute(part, 'chan', [(i, (i + 2 * k + 2) % groups) for i in range(...  6.84 us
    all_to_all x1, waiting for transfers between devices, on_device(): parts = lax.all_to_all(spread, 'zh', 0, 0)  6.81 us
    pallas_call x9, Pallas kernels, call(): pl.pallas_call(inner, out_shape=tuple(outs), in_specs=[pl.BlockSpec(memor...  6.71 us
    ppermute x1, starting transfers between devices, on_device(): before = lax.ppermute(here, SLAB, up)  4.55 us
  transfers between devices with their start and end apart: 9, of which 7 were waited for; matrix products, arithmetic and copies ran while one was open for 0% of the time, Pallas kernels for 2%

profile of v4, /device:TPU:24, one launch (start us, length us, event | category | flops | bytes accessed | tf_op | source)
XLA Modules:
  0.0 97.5 jit_solution(9438988791543825261)
XLA Ops:
  0.6 1.7 %shard_map.75 = (bf16[8,8,2048]{2,1,0:T(8,128)(2,1)}, bf16[24,2048]{1,0:T(8,128)(2,1)}, f32[16,128]{1,0:T(8,128)}) custom-call(bf16[8,1,16,128]{3,2,1,0:T(8,128)(2,1)} %volume.1, bf16[16,1,16,128]{3,2,1,0:T(8,128)(2,1)} %grad.1, f32[1,16]{1,0:T(1,128)} %bitcast.13), custom_call_target="tpu_custom_call" | custom-call | bytes 467008 | tf_op jit(solution)/shard_map/pallas_call | solution.py:30
  2.3 0.0 copy-start.1
  2.3 16.4 %all-to-all-start = ((bf16[8,8,2048]{2,1,0:T(8,128)(2,1)}), bf16[8,8,2048]{2,1,0:T(8,128)(2,1)S(1)}, u32[]{:S(2)}, u32[]{:S(2)}) async-start(bf16[8,8,2048]{2,1,0:T(8,128)(2,1)} %get-tuple-element.16), calls=%async_computation | async-start | bytes 524288 | tf_op jit(solution)/shard_map/all_to_all | solution.py:238
  18.7 0.0 copy-done.1
  18.7 1.3 %collective-permute-start = (bf16[24,2048]{1,0:T(8,128)(2,1)S(1)}, bf16[24,2048]{1,0:T(8,128)(2,1)S(1)}, u32[]{:S(2)}, u32[]{:S(2)}) collective-permute-start(bf16[24,2048]{1,0:T(8,128)(2,1)S(1)} %copy-done.1), channel_id=1, source_target_pairs={{8,0},{16,8},{24,16},{32,24},{40,32},{48,40},{56,48},{64,56},{72,6... | collective-permute-start | bytes 294920 | tf_op jit(solution)/shard_map/ppermute | solution.py:237
  20.0 4.6 %collective-permute-start.1 = (bf16[24,2048]{1,0:T(8,128)(2,1)S(1)}, bf16[24,2048]{1,0:T(8,128)(2,1)S(1)}, u32[]{:S(2)}, u32[]{:S(2)}) collective-permute-start(bf16[24,2048]{1,0:T(8,128)(2,1)S(1)} %copy-done.1), channel_id=1, source_target_pairs={{0,8},{8,16},{16,24},{24,32},{32,40},{40,48},{48,56},{56,64},{64,7... | collective-permute-start | bytes 294920 | tf_op jit(solution)/shard_map/ppermute | solution.py:236
  24.5 0.9 collective-permute-done.after.refs_5_
  25.4 1.3 %collective-permute-done.1.before.refs_4_ = bf16[24,2048]{1,0:T(8,128)(2,1)S(1)} collective-permute-done((bf16[24,2048]{1,0:T(8,128)(2,1)S(1)}, bf16[24,2048]{1,0:T(8,128)(2,1)S(1)}, u32[]{:S(2)}, u32[]{:S(2)}) %collective-permute-start.1) | collective-permute-done | bytes 98336 | tf_op jit(solution)/shard_map/ppermute | solution.py:236
  26.7 0.0 all-to-all-done
  26.7 0.6 shard_map.77
  27.3 20.3 %all_to_all.20.parts = f32[16,16,128]{2,1,0:T(8,128)S(1)} all-to-all(f32[16,16,128]{2,1,0:T(8,128)S(1)} %bitcast.10), channel_id=1, replica_groups=mesh['x'=4,'zh'=8,'zl'=4,'chan'=8] {'x','zl'}, dimensions={0} | all-to-all | bytes 262144 | tf_op jit(solution)/shard_map/all_to_all | solution.py:259
  47.6 0.6 shard_map.78.refs_6_
  48.3 12.0 %all-to-all-start.2 = ((f32[8,16,128]{2,1,0:T(8,128)}), f32[8,16,128]{2,1,0:T(8,128)S(1)}, u32[]{:S(2)}, u32[]{:S(2)}) async-start(f32[8,16,128]{2,1,0:T(8,128)} %shard_map.78.refs_6_), calls=%async_computation.2 | async-start | bytes 131072 | tf_op jit(solution)/shard_map/all_to_all | solution.py:265
  60.2 0.0 copy-done
  60.3 0.6 shard_map.76
  60.8 2.2 %collective-permute-start.2 = (bf16[48,2048]{1,0:T(8,128)(2,1)S(1)}, bf16[48,2048]{1,0:T(8,128)(2,1)S(1)}, u32[]{:S(2)}, u32[]{:S(2)}) collective-permute-start(bf16[48,2048]{1,0:T(8,128)(2,1)S(1)} %get-tuple-element.19), channel_id=1, source_target_pairs={{0,2},{1,3},{2,4},{3,5},{4,6},{5,7},{6,0},{7,1},{8,10},{9,11},{10,... | collective-permute-start | bytes 589832 | tf_op jit(solution)/shard_map/ppermute | solution.py:254
  63.0 4.5 %collective-permute-start.3 = (bf16[48,2048]{1,0:T(8,128)(2,1)S(1)}, bf16[48,2048]{1,0:T(8,128)(2,1)S(1)}, u32[]{:S(2)}, u32[]{:S(2)}) collective-permute-start(bf16[48,2048]{1,0:T(8,128)(2,1)S(1)} %get-tuple-element.20), channel_id=1, source_target_pairs={{0,4},{1,5},{2,6},{3,7},{4,0},{5,1},{6,2},{7,3},{8,12},{9,13},{10,... | collective-permute-start | bytes 589832 | tf_op jit(solution)/shard_map/ppermute | solution.py:254
  67.6 1.9 %collective-permute-start.4 = (bf16[48,2048]{1,0:T(8,128)(2,1)S(1)}, bf16[48,2048]{1,0:T(8,128)(2,1)S(1)}, u32[]{:S(2)}, u32[]{:S(2)}) collective-permute-start(bf16[48,2048]{1,0:T(8,128)(2,1)S(1)} %get-tuple-element.21), channel_id=1, source_target_pairs={{0,6},{1,7},{2,0},{3,1},{4,2},{5,3},{6,4},{7,5},{8,14},{9,15},{10,... | collective-permute-start | bytes 589832 | tf_op jit(solution)/shard_map/ppermute | solution.py:254
  69.5 0.0 collective-permute-done.2.refs_1_
  69.5 4.6 %collective-permute-done.3.refs_2_ = bf16[48,2048]{1,0:T(8,128)(2,1)S(1)} collective-permute-done((bf16[48,2048]{1,0:T(8,128)(2,1)S(1)}, bf16[48,2048]{1,0:T(8,128)(2,1)S(1)}, u32[]{:S(2)}, u32[]{:S(2)}) %collective-permute-start.3) | collective-permute-done | bytes 196640 | tf_op jit(solution)/shard_map/ppermute | solution.py:254
  74.1 2.2 %collective-permute-done.4.refs_3_ = bf16[48,2048]{1,0:T(8,128)(2,1)S(1)} collective-permute-done((bf16[48,2048]{1,0:T(8,128)(2,1)S(1)}, bf16[48,2048]{1,0:T(8,128)(2,1)S(1)}, u32[]{:S(2)}, u32[]{:S(2)}) %collective-permute-start.4) | collective-permute-done | bytes 196640 | tf_op jit(solution)/shard_map/ppermute | solution.py:254
  76.4 0.1 shard_map.79
  76.4 6.8 %all-to-all-done.2.refs_0_ = f32[8,16,128]{2,1,0:T(8,128)S(1)} async-done(((f32[8,16,128]{2,1,0:T(8,128)}), f32[8,16,128]{2,1,0:T(8,128)S(1)}, u32[]{:S(2)}, u32[]{:S(2)}) %all-to-all-start.2) | async-done | bytes 65568 | tf_op jit(solution)/shard_map/all_to_all | solution.py:265
  83.3 0.7 shard_map.82
  83.9 4.4 %all-to-all-start.3 = ((f32[16,16,128]{2,1,0:T(8,128)}), f32[16,16,128]{2,1,0:T(8,128)S(1)}, u32[]{:S(2)}, u32[]{:S(2)}) async-start(f32[16,16,128]{2,1,0:T(8,128)} %shard_map.82), calls=%async_computation.3 | async-start | bytes 262144 | tf_op jit(solution)/shard_map/all_to_all | solution.py:280
  88.3 0.0 copy-start.2
  88.3 1.9 %collective-permute-start.5 = (bf16[10,8,2048]{2,1,0:T(8,128)(2,1)S(1)}, bf16[10,8,2048]{2,1,0:T(8,128)(2,1)S(1)}, u32[]{:S(2)}, u32[]{:S(2)}) collective-permute-start(bf16[10,8,2048]{2,1,0:T(8,128)(2,1)S(1)} %get-tuple-element.22.mine), channel_id=1, source_target_pairs={{0,1},{1,0},{2,3},{3,2},{4,5},{5,4},{6,7},{7,6},{8,9},{9,8},{10,11... | collective-permute-start | bytes 983048 | tf_op jit(solution)/shard_map/ppermute | solution.py:272
  90.2 1.6 %collective-permute-done.5.theirs.got = bf16[10,8,2048]{2,1,0:T(8,128)(2,1)S(1)} collective-permute-done((bf16[10,8,2048]{2,1,0:T(8,128)(2,1)S(1)}, bf16[10,8,2048]{2,1,0:T(8,128)(2,1)S(1)}, u32[]{:S(2)}, u32[]{:S(2)}) %collective-permute-start.5) | collective-permute-done | bytes 327712 | tf_op jit(solution)/shard_map/ppermute | solution.py:272
  91.8 0.6 shard_map.81
  92.5 1.1 %shard_map.80 = bf16[16,1,16,128]{3,2,1,0:T(8,128)(2,1)} custom-call(bf16[3,3,3,16,64]{4,3,2,1,0:T(8,128)(2,1)S(1)} %bitcast.12, f32[16,128]{1,0:T(8,128)S(1)} %copy-done.2, bf16[64,2048]{1,0:T(8,128)(2,1)S(1)} %bitcast.8, bf16[10,8,2048]{2,1,0:T(8,128)(2,1)S(1)} %get-tuple-element.22.mine, bf16[10,8,2048]{2,1,0:T(8,128)(2,1)S(1)} %collective-permute-done.5.theirs.got), custom_call_target="tpu_custom_call" | custom-call | flops 113246208 | bytes 1046528 | tf_op jit(solution)/shard_map/pallas_call | solution.py:30
  93.6 3.1 %all-to-all-done.3 = f32[16,16,128]{2,1,0:T(8,128)S(1)} async-done(((f32[16,16,128]{2,1,0:T(8,128)}), f32[16,16,128]{2,1,0:T(8,128)S(1)}, u32[]{:S(2)}, u32[]{:S(2)}) %all-to-all-start.3) | async-done | bytes 131104 | tf_op jit(solution)/shard_map/all_to_all | solution.py:280
  96.7 0.8 shard_map.83
  (2 shorter events, 0.0 us)
Async XLA Ops:
  2.3 16.4 %copy-start.1 = (bf16[24,2048]{1,0:T(8,128)(2,1)S(1)}, bf16[24,2048]{1,0:T(8,128)(2,1)}, u32[]{:S(2)}) copy-start(bf16[24,2048]{1,0:T(8,128)(2,1)} %get-tuple-element.17.here) | copy-start | bytes 294916
  2.3 24.4 %all-to-all-start = ((bf16[8,8,2048]{2,1,0:T(8,128)(2,1)}), bf16[8,8,2048]{2,1,0:T(8,128)(2,1)S(1)}, u32[]{:S(2)}, u32[]{:S(2)}) async-start(bf16[8,8,2048]{2,1,0:T(8,128)(2,1)} %get-tuple-element.16), calls=%async_computation | async-start | bytes 524288 | tf_op jit(solution)/shard_map/all_to_all | solution.py:238
  18.7 6.7 %collective-permute-start = (bf16[24,2048]{1,0:T(8,128)(2,1)S(1)}, bf16[24,2048]{1,0:T(8,128)(2,1)S(1)}, u32[]{:S(2)}, u32[]{:S(2)}) collective-permute-start(bf16[24,2048]{1,0:T(8,128)(2,1)S(1)} %copy-done.1), channel_id=1, source_target_pairs={{8,0},{16,8},{24,16},{32,24},{40,32},{48,40},{56,48},{64,56},{72,6... | collective-permute-start | bytes 294920 | tf_op jit(solution)/shard_map/ppermute | solution.py:237
  20.0 6.8 %collective-permute-start.1 = (bf16[24,2048]{1,0:T(8,128)(2,1)S(1)}, bf16[24,2048]{1,0:T(8,128)(2,1)S(1)}, u32[]{:S(2)}, u32[]{:S(2)}) collective-permute-start(bf16[24,2048]{1,0:T(8,128)(2,1)S(1)} %copy-done.1), channel_id=1, source_target_pairs={{0,8},{8,16},{16,24},{24,32},{32,40},{40,48},{48,56},{56,64},{64,7... | collective-permute-start | bytes 294920 | tf_op jit(solution)/shard_map/ppermute | solution.py:236
  48.3 12.0 %copy-start = (bf16[3,3,3,64,16]{3,4,2,1,0:T(8,128)(2,1)S(1)}, bf16[3,3,3,64,16]{3,4,2,1,0:T(8,128)(2,1)}, u32[]{:S(2)}) copy-start(bf16[3,3,3,64,16]{3,4,2,1,0:T(8,128)(2,1)} %param.5) | copy-start | bytes 165892
  48.3 35.0 %all-to-all-start.2 = ((f32[8,16,128]{2,1,0:T(8,128)}), f32[8,16,128]{2,1,0:T(8,128)S(1)}, u32[]{:S(2)}, u32[]{:S(2)}) async-start(f32[8,16,128]{2,1,0:T(8,128)} %shard_map.78.refs_6_), calls=%async_computation.2 | async-start | bytes 131072 | tf_op jit(solution)/shard_map/all_to_all | solution.py:265
  60.8 8.7 %collective-permute-start.2 = (bf16[48,2048]{1,0:T(8,128)(2,1)S(1)}, bf16[48,2048]{1,0:T(8,128)(2,1)S(1)}, u32[]{:S(2)}, u32[]{:S(2)}) collective-permute-start(bf16[48,2048]{1,0:T(8,128)(2,1)S(1)} %get-tuple-element.19), channel_id=1, source_target_pairs={{0,2},{1,3},{2,4},{3,5},{4,6},{5,7},{6,0},{7,1},{8,10},{9,11},{10,... | collective-permute-start | bytes 589832 | tf_op jit(solution)/shard_map/ppermute | solution.py:254
  63.0 11.1 %collective-permute-start.3 = (bf16[48,2048]{1,0:T(8,128)(2,1)S(1)}, bf16[48,2048]{1,0:T(8,128)(2,1)S(1)}, u32[]{:S(2)}, u32[]{:S(2)}) collective-permute-start(bf16[48,2048]{1,0:T(8,128)(2,1)S(1)} %get-tuple-element.20), channel_id=1, source_target_pairs={{0,4},{1,5},{2,6},{3,7},{4,0},{5,1},{6,2},{7,3},{8,12},{9,13},{10,... | collective-permute-start | bytes 589832 | tf_op jit(solution)/shard_map/ppermute | solution.py:254
  67.6 8.8 %collective-permute-start.4 = (bf16[48,2048]{1,0:T(8,128)(2,1)S(1)}, bf16[48,2048]{1,0:T(8,128)(2,1)S(1)}, u32[]{:S(2)}, u32[]{:S(2)}) collective-permute-start(bf16[48,2048]{1,0:T(8,128)(2,1)S(1)} %get-tuple-element.21), channel_id=1, source_target_pairs={{0,6},{1,7},{2,0},{3,1},{4,2},{5,3},{6,4},{7,5},{8,14},{9,15},{10,... | collective-permute-start | bytes 589832 | tf_op jit(solution)/shard_map/ppermute | solution.py:254
  83.9 12.8 %all-to-all-start.3 = ((f32[16,16,128]{2,1,0:T(8,128)}), f32[16,16,128]{2,1,0:T(8,128)S(1)}, u32[]{:S(2)}, u32[]{:S(2)}) async-start(f32[16,16,128]{2,1,0:T(8,128)} %shard_map.82), calls=%async_computation.3 | async-start | bytes 262144 | tf_op jit(solution)/shard_map/all_to_all | solution.py:280
  88.3 4.2 %copy-start.2 = (f32[16,128]{1,0:T(8,128)S(1)}, f32[16,128]{1,0:T(8,128)}, u32[]{:S(2)}) copy-start(f32[16,128]{1,0:T(8,128)} %get-tuple-element.15.bias) | copy-start | bytes 24580
  88.3 3.5 %collective-permute-start.5 = (bf16[10,8,2048]{2,1,0:T(8,128)(2,1)S(1)}, bf16[10,8,2048]{2,1,0:T(8,128)(2,1)S(1)}, u32[]{:S(2)}, u32[]{:S(2)}) collective-permute-start(bf16[10,8,2048]{2,1,0:T(8,128)(2,1)S(1)} %get-tuple-element.22.mine), channel_id=1, source_target_pairs={{0,1},{1,0},{2,3},{3,2},{4,5},{5,4},{6,7},{7,6},{8,9},{9,8},{10,11... | collective-permute-start | bytes 983048 | tf_op jit(solution)/shard_map/ppermute | solution.py:272

commit v5 on v4

--- a/solution.py
+++ b/solution.py
@@ -6,13 +6,16 @@
 from jax import lax
 from jax.experimental import pallas as pl
 from jax.experimental.pallas import tpu as pltpu
-from jax.sharding import Mesh, PartitionSpec as P
+from jax.sharding import PartitionSpec as P
 
 X, Z = 4, 32
 ZL = 4
 ZH = Z // ZL
-SLAB = ("x", "zh", "zl")
-NEAR = ("x", "zl")
+SLAB = "slab"
+FAR_ORDER = [(h + ZH // 2) % ZH for h in range(ZH)]
+NEAR_ORDER = [(k + ZL // 2) % ZL for k in range(ZL)]
+FAR = [[x * Z + h * ZL + k for h in FAR_ORDER] for x in range(X) for k in range(ZL)]
+NEAR = [[x * Z + h * ZL + k for k in NEAR_ORDER for x in range(X)] for h in range(ZH)]
 ROWS, COLS = 16, 128
 CELLS = ROWS * COLS
 F32, BF16 = jnp.float32, jnp.bfloat16
@@ -256,13 +259,15 @@
     ]
     near = X * ZL
     rows = 256 // near
-    parts = lax.all_to_all(partial.reshape(near, rows, 128), NEAR, 0, 0)
+    parts = lax.all_to_all(
+        partial.reshape(near, rows, 128), SLAB, 0, 0, axis_index_groups=NEAR
+    )
     (spread,) = call(
         functools.partial(sum_body, None),
         [shape((ZH, rows, 128), F32)],
         [parts],
     )
-    parts = lax.all_to_all(spread, "zh", 0, 0)
+    parts = lax.all_to_all(spread, SLAB, 0, 0, axis_index_groups=FAR)
     kept, sent = call(
         join_body,
         [shape((8, CELLS), F32), shape((10, 8, CELLS), BF16)],
@@ -277,7 +282,7 @@
         [parts],
         after=[kept],
     )
-    flat = lax.all_to_all(spread, NEAR, 0, 0).reshape(256, 128)
+    flat = lax.all_to_all(spread, SLAB, 0, 0, axis_index_groups=NEAR).reshape(256, 128)
     kernel_out, bias_out = call(
         unpack_body, [shape((3, 3, 3, 16, 64), F32), shape((1, 16), F32)], [flat]
     )
@@ -309,7 +314,6 @@
 
 
 def solution(mesh):
-    split = Mesh(mesh.devices.reshape(X, ZH, ZL, -1), ("x", "zh", "zl", "chan"))
     in_specs = (
         P("chan", SLAB, None, None),
         P(None, None, None, None, "chan"),
@@ -323,5 +327,5 @@
         P("chan"),
     )
     return jax.shard_map(
-        on_device, mesh=split, in_specs=in_specs, out_specs=out_specs, check_vma=False
-    )
+        on_device, mesh=mesh, in_specs=in_specs, out_specs=out_specs, check_vma=False
+    )

time: 98.4 us -> 100 us (1.016)
  starting transfers between devices: 49.1 us -> 59.3 us
  waiting for transfers between devices: 20.6 us -> 12 us
    all_to_all x2, starting transfers between devices: 16.3 us -> 26.5 us  [the longest x1 21.8 us: on_device(): parts = lax.all_to_all(spread, SLAB, 0, 0, axis_index_groups=FAR)]
    all_to_all x2, waiting for transfers between devices: 9.94 us -> 1.41 us  [the longest x1 1.4 us: on_device(): lax.all_to_all(spread, SLAB, 0, 0, axis_index_groups=NEAR).reshape(256, 128)]
  transfers between devices with their start and end apart: 9 -> 9, of which waited for: 7 -> 6; matrix products, arithmetic and copies ran while one was open for 0% -> 0% of each run, Pallas kernels for 2% -> 2%
where the time goes in v5:
time: 100 us; the launch traced here: 99.6 us
  starting transfers between devices  59.3 us (59%)
  blocking collectives  20.9 us (21%)
  waiting for transfers between devices  12 us (12%)
  Pallas kernels  6.7 us (7%)
    all_to_all x1, starting transfers between devices, on_device(): parts = lax.all_to_all(spread, SLAB, 0, 0, axis_index_groups=FAR)  21.8 us
    all_to_all x1, blocking collectives, on_device(): lax.all_to_all(partial.reshape(near, rows, 128), SLAB, 0, 0, axis_index_g...  20.9 us
    all_to_all x1, starting transfers between devices, on_device(): whole = lax.all_to_all(sent, 'chan', 0, 0).reshape(64, CELLS)  16.4 us
    ppermute x3, starting transfers between devices, on_device(): lax.ppermute(part, 'chan', [(i, (i + 2 * k + 2) % groups) for i in range(...  8.67 us
    ppermute x3, waiting for transfers between devices, on_device(): lax.ppermute(part, 'chan', [(i, (i + 2 * k + 2) % groups) for i in range(...  6.84 us
    pallas_call x9, Pallas kernels, call(): pl.pallas_call(inner, out_shape=tuple(outs), in_specs=[pl.BlockSpec(memor...  6.7 us
    all_to_all x1, starting transfers between devices, on_device(): lax.all_to_all(spread, SLAB, 0, 0, axis_index_groups=NEAR).reshape(256, 128)  4.74 us
    ppermute x1, starting transfers between devices, on_device(): before = lax.ppermute(here, SLAB, up)  4.55 us
  transfers between devices with their start and end apart: 9, of which 6 were waited for; matrix products, arithmetic and copies ran while one was open for 0% of the time, Pallas kernels for 2%

profile of v5, /device:TPU:24, one launch (start us, length us, event | category | flops | bytes accessed | tf_op | source)
XLA Modules:
  0.0 99.6 jit_solution(7665028235059353795)
XLA Ops:
  0.6 1.7 %shard_map.75 = (bf16[8,8,2048]{2,1,0:T(8,128)(2,1)}, bf16[24,2048]{1,0:T(8,128)(2,1)}, f32[16,128]{1,0:T(8,128)}) custom-call(bf16[8,1,16,128]{3,2,1,0:T(8,128)(2,1)} %volume.1, bf16[16,1,16,128]{3,2,1,0:T(8,128)(2,1)} %grad.1, f32[1,16]{1,0:T(1,128)} %bitcast.13), custom_call_target="tpu_custom_call" | custom-call | bytes 467008 | tf_op jit(solution)/shard_map/pallas_call | solution.py:33
  2.3 0.0 copy-start.1
  2.3 16.4 %all-to-all-start = ((bf16[8,8,2048]{2,1,0:T(8,128)(2,1)}), bf16[8,8,2048]{2,1,0:T(8,128)(2,1)S(1)}, u32[]{:S(2)}, u32[]{:S(2)}) async-start(bf16[8,8,2048]{2,1,0:T(8,128)(2,1)} %get-tuple-element.16), calls=%async_computation | async-start | bytes 524288 | tf_op jit(solution)/shard_map/all_to_all | solution.py:241
  18.7 0.0 copy-done.1
  18.7 1.3 %collective-permute-start = (bf16[24,2048]{1,0:T(8,128)(2,1)S(1)}, bf16[24,2048]{1,0:T(8,128)(2,1)S(1)}, u32[]{:S(2)}, u32[]{:S(2)}) collective-permute-start(bf16[24,2048]{1,0:T(8,128)(2,1)S(1)} %copy-done.1), channel_id=1, source_target_pairs={{8,0},{16,8},{24,16},{32,24},{40,32},{48,40},{56,48},{64,56},{72,6... | collective-permute-start | bytes 294920 | tf_op jit(solution)/shard_map/ppermute | solution.py:240
  20.0 4.6 %collective-permute-start.1 = (bf16[24,2048]{1,0:T(8,128)(2,1)S(1)}, bf16[24,2048]{1,0:T(8,128)(2,1)S(1)}, u32[]{:S(2)}, u32[]{:S(2)}) collective-permute-start(bf16[24,2048]{1,0:T(8,128)(2,1)S(1)} %copy-done.1), channel_id=1, source_target_pairs={{0,8},{8,16},{16,24},{24,32},{32,40},{40,48},{48,56},{56,64},{64,7... | collective-permute-start | bytes 294920 | tf_op jit(solution)/shard_map/ppermute | solution.py:239
  24.5 0.9 collective-permute-done.after.refs_5_
  25.4 1.3 %collective-permute-done.1.before.refs_4_ = bf16[24,2048]{1,0:T(8,128)(2,1)S(1)} collective-permute-done((bf16[24,2048]{1,0:T(8,128)(2,1)S(1)}, bf16[24,2048]{1,0:T(8,128)(2,1)S(1)}, u32[]{:S(2)}, u32[]{:S(2)}) %collective-permute-start.1) | collective-permute-done | bytes 98336 | tf_op jit(solution)/shard_map/ppermute | solution.py:239
  26.7 0.0 all-to-all-done
  26.7 0.6 shard_map.77
  27.3 20.9 %all_to_all.20.parts = f32[16,16,128]{2,1,0:T(8,128)S(1)} all-to-all(f32[16,16,128]{2,1,0:T(8,128)S(1)} %bitcast.10), channel_id=1, replica_groups={{16,272,528,784,24,280,536,792,0,256,512,768,8,264,520,776},{48,304,560..., dimensions={0} | all-to-all | bytes 262144 | tf_op jit(solution)/shard_map/all_to_all | solution.py:262
  48.1 0.6 shard_map.78.refs_6_
  48.8 21.8 %all-to-all-start.2 = ((f32[8,16,128]{2,1,0:T(8,128)}), f32[8,16,128]{2,1,0:T(8,128)S(1)}, u32[]{:S(2)}, u32[]{:S(2)}) async-start(f32[8,16,128]{2,1,0:T(8,128)} %shard_map.78.refs_6_), calls=%async_computation.2 | async-start | bytes 131072 | tf_op jit(solution)/shard_map/all_to_all | solution.py:270
  70.6 0.0 copy-done
  70.6 0.6 shard_map.76
  71.1 2.2 %collective-permute-start.2 = (bf16[48,2048]{1,0:T(8,128)(2,1)S(1)}, bf16[48,2048]{1,0:T(8,128)(2,1)S(1)}, u32[]{:S(2)}, u32[]{:S(2)}) collective-permute-start(bf16[48,2048]{1,0:T(8,128)(2,1)S(1)} %get-tuple-element.19), channel_id=1, source_target_pairs={{0,2},{1,3},{2,4},{3,5},{4,6},{5,7},{6,0},{7,1},{8,10},{9,11},{10,... | collective-permute-start | bytes 589832 | tf_op jit(solution)/shard_map/ppermute | solution.py:257
  73.4 4.5 %collective-permute-start.3 = (bf16[48,2048]{1,0:T(8,128)(2,1)S(1)}, bf16[48,2048]{1,0:T(8,128)(2,1)S(1)}, u32[]{:S(2)}, u32[]{:S(2)}) collective-permute-start(bf16[48,2048]{1,0:T(8,128)(2,1)S(1)} %get-tuple-element.20), channel_id=1, source_target_pairs={{0,4},{1,5},{2,6},{3,7},{4,0},{5,1},{6,2},{7,3},{8,12},{9,13},{10,... | collective-permute-start | bytes 589832 | tf_op jit(solution)/shard_map/ppermute | solution.py:257
  77.9 1.9 %collective-permute-start.4 = (bf16[48,2048]{1,0:T(8,128)(2,1)S(1)}, bf16[48,2048]{1,0:T(8,128)(2,1)S(1)}, u32[]{:S(2)}, u32[]{:S(2)}) collective-permute-start(bf16[48,2048]{1,0:T(8,128)(2,1)S(1)} %get-tuple-element.21), channel_id=1, source_target_pairs={{0,6},{1,7},{2,0},{3,1},{4,2},{5,3},{6,4},{7,5},{8,14},{9,15},{10,... | collective-permute-start | bytes 589832 | tf_op jit(solution)/shard_map/ppermute | solution.py:257
  79.8 0.0 collective-permute-done.2.refs_1_
  79.8 4.1 %collective-permute-done.3.refs_2_ = bf16[48,2048]{1,0:T(8,128)(2,1)S(1)} collective-permute-done((bf16[48,2048]{1,0:T(8,128)(2,1)S(1)}, bf16[48,2048]{1,0:T(8,128)(2,1)S(1)}, u32[]{:S(2)}, u32[]{:S(2)}) %collective-permute-start.3) | collective-permute-done | bytes 196640 | tf_op jit(solution)/shard_map/ppermute | solution.py:257
  84.0 2.7 %collective-permute-done.4.refs_3_ = bf16[48,2048]{1,0:T(8,128)(2,1)S(1)} collective-permute-done((bf16[48,2048]{1,0:T(8,128)(2,1)S(1)}, bf16[48,2048]{1,0:T(8,128)(2,1)S(1)}, u32[]{:S(2)}, u32[]{:S(2)}) %collective-permute-start.4) | collective-permute-done | bytes 196640 | tf_op jit(solution)/shard_map/ppermute | solution.py:257
  86.7 0.1 shard_map.79
  86.8 0.0 all-to-all-done.2.refs_0_
  86.8 0.7 shard_map.82
  87.4 4.7 %all-to-all-start.3 = ((f32[16,16,128]{2,1,0:T(8,128)}), f32[16,16,128]{2,1,0:T(8,128)S(1)}, u32[]{:S(2)}, u32[]{:S(2)}) async-start(f32[16,16,128]{2,1,0:T(8,128)} %shard_map.82), calls=%async_computation.3 | async-start | bytes 262144 | tf_op jit(solution)/shard_map/all_to_all | solution.py:285
  92.2 1.9 %collective-permute-start.5 = (bf16[10,8,2048]{2,1,0:T(8,128)(2,1)S(1)}, bf16[10,8,2048]{2,1,0:T(8,128)(2,1)S(1)}, u32[]{:S(2)}, u32[]{:S(2)}) collective-permute-start(bf16[10,8,2048]{2,1,0:T(8,128)(2,1)S(1)} %get-tuple-element.22.mine), channel_id=1, source_target_pairs={{0,1},{1,0},{2,3},{3,2},{4,5},{5,4},{6,7},{7,6},{8,9},{9,8},{10,11... | collective-permute-start | bytes 983048 | tf_op jit(solution)/shard_map/ppermute | solution.py:277
  94.1 1.6 %collective-permute-done.5.theirs.got = bf16[10,8,2048]{2,1,0:T(8,128)(2,1)S(1)} collective-permute-done((bf16[10,8,2048]{2,1,0:T(8,128)(2,1)S(1)}, bf16[10,8,2048]{2,1,0:T(8,128)(2,1)S(1)}, u32[]{:S(2)}, u32[]{:S(2)}) %collective-permute-start.5) | collective-permute-done | bytes 327712 | tf_op jit(solution)/shard_map/ppermute | solution.py:277
  95.7 0.6 shard_map.81
  96.4 0.0 copy-done.2
  96.4 1.1 %shard_map.80 = bf16[16,1,16,128]{3,2,1,0:T(8,128)(2,1)} custom-call(bf16[3,3,3,16,64]{4,3,2,1,0:T(8,128)(2,1)S(1)} %bitcast.12, f32[16,128]{1,0:T(8,128)S(1)} %copy-done.2, bf16[64,2048]{1,0:T(8,128)(2,1)S(1)} %bitcast.8, bf16[10,8,2048]{2,1,0:T(8,128)(2,1)S(1)} %get-tuple-element.22.mine, bf16[10,8,2048]{2,1,0:T(8,128)(2,1)S(1)} %collective-permute-done.5.theirs.got), custom_call_target="tpu_custom_call" | custom-call | flops 113246208 | bytes 1046528 | tf_op jit(solution)/shard_map/pallas_call | solution.py:33
  97.4 1.4 %all-to-all-done.3 = f32[16,16,128]{2,1,0:T(8,128)S(1)} async-done(((f32[16,16,128]{2,1,0:T(8,128)}), f32[16,16,128]{2,1,0:T(8,128)S(1)}, u32[]{:S(2)}, u32[]{:S(2)}) %all-to-all-start.3) | async-done | bytes 131104 | tf_op jit(solution)/shard_map/all_to_all | solution.py:285
  98.8 0.8 shard_map.83
  (2 shorter events, 0.0 us)
Async XLA Ops:
  2.3 16.4 %copy-start.1 = (bf16[24,2048]{1,0:T(8,128)(2,1)S(1)}, bf16[24,2048]{1,0:T(8,128)(2,1)}, u32[]{:S(2)}) copy-start(bf16[24,2048]{1,0:T(8,128)(2,1)} %get-tuple-element.17.here) | copy-start | bytes 294916
  2.3 24.4 %all-to-all-start = ((bf16[8,8,2048]{2,1,0:T(8,128)(2,1)}), bf16[8,8,2048]{2,1,0:T(8,128)(2,1)S(1)}, u32[]{:S(2)}, u32[]{:S(2)}) async-start(bf16[8,8,2048]{2,1,0:T(8,128)(2,1)} %get-tuple-element.16), calls=%async_computation | async-start | bytes 524288 | tf_op jit(solution)/shard_map/all_to_all | solution.py:241
  18.7 6.7 %collective-permute-start = (bf16[24,2048]{1,0:T(8,128)(2,1)S(1)}, bf16[24,2048]{1,0:T(8,128)(2,1)S(1)}, u32[]{:S(2)}, u32[]{:S(2)}) collective-permute-start(bf16[24,2048]{1,0:T(8,128)(2,1)S(1)} %copy-done.1), channel_id=1, source_target_pairs={{8,0},{16,8},{24,16},{32,24},{40,32},{48,40},{56,48},{64,56},{72,6... | collective-permute-start | bytes 294920 | tf_op jit(solution)/shard_map/ppermute | solution.py:240
  20.0 6.8 %collective-permute-start.1 = (bf16[24,2048]{1,0:T(8,128)(2,1)S(1)}, bf16[24,2048]{1,0:T(8,128)(2,1)S(1)}, u32[]{:S(2)}, u32[]{:S(2)}) collective-permute-start(bf16[24,2048]{1,0:T(8,128)(2,1)S(1)} %copy-done.1), channel_id=1, source_target_pairs={{0,8},{8,16},{16,24},{24,32},{32,40},{40,48},{48,56},{56,64},{64,7... | collective-permute-start | bytes 294920 | tf_op jit(solution)/shard_map/ppermute | solution.py:239
  48.8 21.8 %copy-start = (bf16[3,3,3,64,16]{3,4,2,1,0:T(8,128)(2,1)S(1)}, bf16[3,3,3,64,16]{3,4,2,1,0:T(8,128)(2,1)}, u32[]{:S(2)}) copy-start(bf16[3,3,3,64,16]{3,4,2,1,0:T(8,128)(2,1)} %param.5) | copy-start | bytes 165892
  48.8 38.0 %all-to-all-start.2 = ((f32[8,16,128]{2,1,0:T(8,128)}), f32[8,16,128]{2,1,0:T(8,128)S(1)}, u32[]{:S(2)}, u32[]{:S(2)}) async-start(f32[8,16,128]{2,1,0:T(8,128)} %shard_map.78.refs_6_), calls=%async_computation.2 | async-start | bytes 131072 | tf_op jit(solution)/shard_map/all_to_all | solution.py:270
  71.1 8.7 %collective-permute-start.2 = (bf16[48,2048]{1,0:T(8,128)(2,1)S(1)}, bf16[48,2048]{1,0:T(8,128)(2,1)S(1)}, u32[]{:S(2)}, u32[]{:S(2)}) collective-permute-start(bf16[48,2048]{1,0:T(8,128)(2,1)S(1)} %get-tuple-element.19), channel_id=1, source_target_pairs={{0,2},{1,3},{2,4},{3,5},{4,6},{5,7},{6,0},{7,1},{8,10},{9,11},{10,... | collective-permute-start | bytes 589832 | tf_op jit(solution)/shard_map/ppermute | solution.py:257
  73.4 10.6 %collective-permute-start.3 = (bf16[48,2048]{1,0:T(8,128)(2,1)S(1)}, bf16[48,2048]{1,0:T(8,128)(2,1)S(1)}, u32[]{:S(2)}, u32[]{:S(2)}) collective-permute-start(bf16[48,2048]{1,0:T(8,128)(2,1)S(1)} %get-tuple-element.20), channel_id=1, source_target_pairs={{0,4},{1,5},{2,6},{3,7},{4,0},{5,1},{6,2},{7,3},{8,12},{9,13},{10,... | collective-permute-start | bytes 589832 | tf_op jit(solution)/shard_map/ppermute | solution.py:257
  77.9 8.8 %collective-permute-start.4 = (bf16[48,2048]{1,0:T(8,128)(2,1)S(1)}, bf16[48,2048]{1,0:T(8,128)(2,1)S(1)}, u32[]{:S(2)}, u32[]{:S(2)}) collective-permute-start(bf16[48,2048]{1,0:T(8,128)(2,1)S(1)} %get-tuple-element.21), channel_id=1, source_target_pairs={{0,6},{1,7},{2,0},{3,1},{4,2},{5,3},{6,4},{7,5},{8,14},{9,15},{10,... | collective-permute-start | bytes 589832 | tf_op jit(solution)/shard_map/ppermute | solution.py:257
  87.4 11.4 %all-to-all-start.3 = ((f32[16,16,128]{2,1,0:T(8,128)}), f32[16,16,128]{2,1,0:T(8,128)S(1)}, u32[]{:S(2)}, u32[]{:S(2)}) async-start(f32[16,16,128]{2,1,0:T(8,128)} %shard_map.82), calls=%async_computation.3 | async-start | bytes 262144 | tf_op jit(solution)/shard_map/all_to_all | solution.py:285
  92.2 4.2 %copy-start.2 = (f32[16,128]{1,0:T(8,128)S(1)}, f32[16,128]{1,0:T(8,128)}, u32[]{:S(2)}) copy-start(f32[16,128]{1,0:T(8,128)} %get-tuple-element.15.bias) | copy-start | bytes 24580
  92.2 3.5 %collective-permute-start.5 = (bf16[10,8,2048]{2,1,0:T(8,128)(2,1)S(1)}, bf16[10,8,2048]{2,1,0:T(8,128)(2,1)S(1)}, u32[]{:S(2)}, u32[]{:S(2)}) collective-permute-start(bf16[10,8,2048]{2,1,0:T(8,128)(2,1)S(1)} %get-tuple-element.22.mine), channel_id=1, source_target_pairs={{0,1},{1,0},{2,3},{3,2},{4,5},{5,4},{6,7},{7,6},{8,9},{9,8},{10,11... | collective-permute-start | bytes 983048 | tf_op jit(solution)/shard_map/ppermute | solution.py:277

commit v6 on v5

--- a/solution.py
+++ b/solution.py
@@ -12,7 +12,7 @@
 ZL = 4
 ZH = Z // ZL
 SLAB = "slab"
-FAR_ORDER = [(h + ZH // 2) % ZH for h in range(ZH)]
+FAR_ORDER = [(h + ZH * 3 // 4) % ZH for h in range(ZH)]
 NEAR_ORDER = [(k + ZL // 2) % ZL for k in range(ZL)]
 FAR = [[x * Z + h * ZL + k for h in FAR_ORDER] for x in range(X) for k in range(ZL)]
 NEAR = [[x * Z + h * ZL + k for k in NEAR_ORDER for x in range(X)] for h in range(ZH)]

time: 100 us -> 90.7 us (0.907)
  starting transfers between devices: 59.3 us -> 49.7 us
    all_to_all x1, starting transfers between devices: 21.8 us -> 12.1 us  [on_device(): parts = lax.all_to_all(spread, SLAB, 0, 0, axis_index_groups=FAR)]
  transfers between devices with their start and end apart: 9 -> 9, of which waited for: 6 -> 6; matrix products, arithmetic and copies ran while one was open for 0% -> 0% of each run, Pallas kernels for 2% -> 3%
where the time goes in v6:
time: 90.7 us; the launch traced here: 90 us
  starting transfers between devices  49.7 us (55%)
  blocking collectives  20.9 us (23%)
  waiting for transfers between devices  12 us (13%)
  Pallas kernels  6.71 us (7%)
    all_to_all x1, blocking collectives, on_device(): lax.all_to_all(partial.reshape(near, rows, 128), SLAB, 0, 0, axis_index_g...  20.9 us
    all_to_all x1, starting transfers between devices, on_device(): whole = lax.all_to_all(sent, 'chan', 0, 0).reshape(64, CELLS)  16.4 us
    all_to_all x1, starting transfers between devices, on_device(): parts = lax.all_to_all(spread, SLAB, 0, 0, axis_index_groups=FAR)  12.1 us
    ppermute x3, starting transfers between devices, on_device(): lax.ppermute(part, 'chan', [(i, (i + 2 * k + 2) % groups) for i in range(...  8.66 us
    ppermute x3, waiting for transfers between devices, on_device(): lax.ppermute(part, 'chan', [(i, (i + 2 * k + 2) % groups) for i in range(...  6.84 us
    pallas_call x9, Pallas kernels, call(): pl.pallas_call(inner, out_shape=tuple(outs), in_specs=[pl.BlockSpec(memor...  6.71 us
    all_to_all x1, starting transfers between devices, on_device(): lax.all_to_all(spread, SLAB, 0, 0, axis_index_groups=NEAR).reshape(256, 128)  4.73 us
    ppermute x1, starting transfers between devices, on_device(): before = lax.ppermute(here, SLAB, up)  4.55 us
  transfers between devices with their start and end apart: 9, of which 6 were waited for; matrix products, arithmetic and copies ran while one was open for 0% of the time, Pallas kernels for 3%

profile of v6, /device:TPU:24, one launch (start us, length us, event | category | flops | bytes accessed | tf_op | source)
XLA Modules:
  0.0 90.0 jit_solution(1858065172583062811)
XLA Ops:
  0.6 1.7 %shard_map.75 = (bf16[8,8,2048]{2,1,0:T(8,128)(2,1)}, bf16[24,2048]{1,0:T(8,128)(2,1)}, f32[16,128]{1,0:T(8,128)}) custom-call(bf16[8,1,16,128]{3,2,1,0:T(8,128)(2,1)} %volume.1, bf16[16,1,16,128]{3,2,1,0:T(8,128)(2,1)} %grad.1, f32[1,16]{1,0:T(1,128)} %bitcast.13), custom_call_target="tpu_custom_call" | custom-call | bytes 467008 | tf_op jit(solution)/shard_map/pallas_call | solution.py:33
  2.3 0.0 copy-start.1
  2.3 16.4 %all-to-all-start = ((bf16[8,8,2048]{2,1,0:T(8,128)(2,1)}), bf16[8,8,2048]{2,1,0:T(8,128)(2,1)S(1)}, u32[]{:S(2)}, u32[]{:S(2)}) async-start(bf16[8,8,2048]{2,1,0:T(8,128)(2,1)} %get-tuple-element.16), calls=%async_computation | async-start | bytes 524288 | tf_op jit(solution)/shard_map/all_to_all | solution.py:241
  18.7 0.0 copy-done.1
  18.7 1.3 %collective-permute-start = (bf16[24,2048]{1,0:T(8,128)(2,1)S(1)}, bf16[24,2048]{1,0:T(8,128)(2,1)S(1)}, u32[]{:S(2)}, u32[]{:S(2)}) collective-permute-start(bf16[24,2048]{1,0:T(8,128)(2,1)S(1)} %copy-done.1), channel_id=1, source_target_pairs={{8,0},{16,8},{24,16},{32,24},{40,32},{48,40},{56,48},{64,56},{72,6... | collective-permute-start | bytes 294920 | tf_op jit(solution)/shard_map/ppermute | solution.py:240
  20.0 4.6 %collective-permute-start.1 = (bf16[24,2048]{1,0:T(8,128)(2,1)S(1)}, bf16[24,2048]{1,0:T(8,128)(2,1)S(1)}, u32[]{:S(2)}, u32[]{:S(2)}) collective-permute-start(bf16[24,2048]{1,0:T(8,128)(2,1)S(1)} %copy-done.1), channel_id=1, source_target_pairs={{0,8},{8,16},{16,24},{24,32},{32,40},{40,48},{48,56},{56,64},{64,7... | collective-permute-start | bytes 294920 | tf_op jit(solution)/shard_map/ppermute | solution.py:239
  24.5 0.9 collective-permute-done.after.refs_5_
  25.4 1.3 %collective-permute-done.1.before.refs_4_ = bf16[24,2048]{1,0:T(8,128)(2,1)S(1)} collective-permute-done((bf16[24,2048]{1,0:T(8,128)(2,1)S(1)}, bf16[24,2048]{1,0:T(8,128)(2,1)S(1)}, u32[]{:S(2)}, u32[]{:S(2)}) %collective-permute-start.1) | collective-permute-done | bytes 98336 | tf_op jit(solution)/shard_map/ppermute | solution.py:239
  26.7 0.0 all-to-all-done
  26.7 0.6 shard_map.77
  27.3 20.9 %all_to_all.20.parts = f32[16,16,128]{2,1,0:T(8,128)S(1)} all-to-all(f32[16,16,128]{2,1,0:T(8,128)S(1)} %bitcast.10), channel_id=1, replica_groups={{16,272,528,784,24,280,536,792,0,256,512,768,8,264,520,776},{48,304,560..., dimensions={0} | all-to-all | bytes 262144 | tf_op jit(solution)/shard_map/all_to_all | solution.py:262
  48.1 0.6 shard_map.78.refs_6_
  48.8 12.1 %all-to-all-start.2 = ((f32[8,16,128]{2,1,0:T(8,128)}), f32[8,16,128]{2,1,0:T(8,128)S(1)}, u32[]{:S(2)}, u32[]{:S(2)}) async-start(f32[8,16,128]{2,1,0:T(8,128)} %shard_map.78.refs_6_), calls=%async_computation.2 | async-start | bytes 131072 | tf_op jit(solution)/shard_map/all_to_all | solution.py:270
  60.9 0.0 copy-done
  60.9 0.6 shard_map.76
  61.5 2.2 %collective-permute-start.2 = (bf16[48,2048]{1,0:T(8,128)(2,1)S(1)}, bf16[48,2048]{1,0:T(8,128)(2,1)S(1)}, u32[]{:S(2)}, u32[]{:S(2)}) collective-permute-start(bf16[48,2048]{1,0:T(8,128)(2,1)S(1)} %get-tuple-element.19), channel_id=1, source_target_pairs={{0,2},{1,3},{2,4},{3,5},{4,6},{5,7},{6,0},{7,1},{8,10},{9,11},{10,... | collective-permute-start | bytes 589832 | tf_op jit(solution)/shard_map/ppermute | solution.py:257
  63.7 4.5 %collective-permute-start.3 = (bf16[48,2048]{1,0:T(8,128)(2,1)S(1)}, bf16[48,2048]{1,0:T(8,128)(2,1)S(1)}, u32[]{:S(2)}, u32[]{:S(2)}) collective-permute-start(bf16[48,2048]{1,0:T(8,128)(2,1)S(1)} %get-tuple-element.20), channel_id=1, source_target_pairs={{0,4},{1,5},{2,6},{3,7},{4,0},{5,1},{6,2},{7,3},{8,12},{9,13},{10,... | collective-permute-start | bytes 589832 | tf_op jit(solution)/shard_map/ppermute | solution.py:257
  68.3 1.9 %collective-permute-start.4 = (bf16[48,2048]{1,0:T(8,128)(2,1)S(1)}, bf16[48,2048]{1,0:T(8,128)(2,1)S(1)}, u32[]{:S(2)}, u32[]{:S(2)}) collective-permute-start(bf16[48,2048]{1,0:T(8,128)(2,1)S(1)} %get-tuple-element.21), channel_id=1, source_target_pairs={{0,6},{1,7},{2,0},{3,1},{4,2},{5,3},{6,4},{7,5},{8,14},{9,15},{10,... | collective-permute-start | bytes 589832 | tf_op jit(solution)/shard_map/ppermute | solution.py:257
  70.2 0.0 collective-permute-done.2.refs_1_
  70.2 4.1 %collective-permute-done.3.refs_2_ = bf16[48,2048]{1,0:T(8,128)(2,1)S(1)} collective-permute-done((bf16[48,2048]{1,0:T(8,128)(2,1)S(1)}, bf16[48,2048]{1,0:T(8,128)(2,1)S(1)}, u32[]{:S(2)}, u32[]{:S(2)}) %collective-permute-start.3) | collective-permute-done | bytes 196640 | tf_op jit(solution)/shard_map/ppermute | solution.py:257
  74.3 2.7 %collective-permute-done.4.refs_3_ = bf16[48,2048]{1,0:T(8,128)(2,1)S(1)} collective-permute-done((bf16[48,2048]{1,0:T(8,128)(2,1)S(1)}, bf16[48,2048]{1,0:T(8,128)(2,1)S(1)}, u32[]{:S(2)}, u32[]{:S(2)}) %collective-permute-start.4) | collective-permute-done | bytes 196640 | tf_op jit(solution)/shard_map/ppermute | solution.py:257
  77.0 0.1 shard_map.79
  77.1 0.0 all-to-all-done.2.refs_0_
  77.2 0.7 shard_map.82
  77.8 4.7 %all-to-all-start.3 = ((f32[16,16,128]{2,1,0:T(8,128)}), f32[16,16,128]{2,1,0:T(8,128)S(1)}, u32[]{:S(2)}, u32[]{:S(2)}) async-start(f32[16,16,128]{2,1,0:T(8,128)} %shard_map.82), calls=%async_computation.3 | async-start | bytes 262144 | tf_op jit(solution)/shard_map/all_to_all | solution.py:285
  82.6 1.9 %collective-permute-start.5 = (bf16[10,8,2048]{2,1,0:T(8,128)(2,1)S(1)}, bf16[10,8,2048]{2,1,0:T(8,128)(2,1)S(1)}, u32[]{:S(2)}, u32[]{:S(2)}) collective-permute-start(bf16[10,8,2048]{2,1,0:T(8,128)(2,1)S(1)} %get-tuple-element.22.mine), channel_id=1, source_target_pairs={{0,1},{1,0},{2,3},{3,2},{4,5},{5,4},{6,7},{7,6},{8,9},{9,8},{10,11... | collective-permute-start | bytes 983048 | tf_op jit(solution)/shard_map/ppermute | solution.py:277
  84.5 1.6 %collective-permute-done.5.theirs.got = bf16[10,8,2048]{2,1,0:T(8,128)(2,1)S(1)} collective-permute-done((bf16[10,8,2048]{2,1,0:T(8,128)(2,1)S(1)}, bf16[10,8,2048]{2,1,0:T(8,128)(2,1)S(1)}, u32[]{:S(2)}, u32[]{:S(2)}) %collective-permute-start.5) | collective-permute-done | bytes 327712 | tf_op jit(solution)/shard_map/ppermute | solution.py:277
  86.1 0.6 shard_map.81
  86.7 0.0 copy-done.2
  86.7 1.1 %shard_map.80 = bf16[16,1,16,128]{3,2,1,0:T(8,128)(2,1)} custom-call(bf16[3,3,3,16,64]{4,3,2,1,0:T(8,128)(2,1)S(1)} %bitcast.12, f32[16,128]{1,0:T(8,128)S(1)} %copy-done.2, bf16[64,2048]{1,0:T(8,128)(2,1)S(1)} %bitcast.8, bf16[10,8,2048]{2,1,0:T(8,128)(2,1)S(1)} %get-tuple-element.22.mine, bf16[10,8,2048]{2,1,0:T(8,128)(2,1)S(1)} %collective-permute-done.5.theirs.got), custom_call_target="tpu_custom_call" | custom-call | flops 113246208 | bytes 1046528 | tf_op jit(solution)/shard_map/pallas_call | solution.py:33
  87.8 1.4 %all-to-all-done.3 = f32[16,16,128]{2,1,0:T(8,128)S(1)} async-done(((f32[16,16,128]{2,1,0:T(8,128)}), f32[16,16,128]{2,1,0:T(8,128)S(1)}, u32[]{:S(2)}, u32[]{:S(2)}) %all-to-all-start.3) | async-done | bytes 131104 | tf_op jit(solution)/shard_map/all_to_all | solution.py:285
  89.2 0.8 shard_map.83
  (2 shorter events, 0.0 us)
Async XLA Ops:
  2.3 16.4 %copy-start.1 = (bf16[24,2048]{1,0:T(8,128)(2,1)S(1)}, bf16[24,2048]{1,0:T(8,128)(2,1)}, u32[]{:S(2)}) copy-start(bf16[24,2048]{1,0:T(8,128)(2,1)} %get-tuple-element.17.here) | copy-start | bytes 294916
  2.3 24.4 %all-to-all-start = ((bf16[8,8,2048]{2,1,0:T(8,128)(2,1)}), bf16[8,8,2048]{2,1,0:T(8,128)(2,1)S(1)}, u32[]{:S(2)}, u32[]{:S(2)}) async-start(bf16[8,8,2048]{2,1,0:T(8,128)(2,1)} %get-tuple-element.16), calls=%async_computation | async-start | bytes 524288 | tf_op jit(solution)/shard_map/all_to_all | solution.py:241
  18.7 6.7 %collective-permute-start = (bf16[24,2048]{1,0:T(8,128)(2,1)S(1)}, bf16[24,2048]{1,0:T(8,128)(2,1)S(1)}, u32[]{:S(2)}, u32[]{:S(2)}) collective-permute-start(bf16[24,2048]{1,0:T(8,128)(2,1)S(1)} %copy-done.1), channel_id=1, source_target_pairs={{8,0},{16,8},{24,16},{32,24},{40,32},{48,40},{56,48},{64,56},{72,6... | collective-permute-start | bytes 294920 | tf_op jit(solution)/shard_map/ppermute | solution.py:240
  20.0 6.8 %collective-permute-start.1 = (bf16[24,2048]{1,0:T(8,128)(2,1)S(1)}, bf16[24,2048]{1,0:T(8,128)(2,1)S(1)}, u32[]{:S(2)}, u32[]{:S(2)}) collective-permute-start(bf16[24,2048]{1,0:T(8,128)(2,1)S(1)} %copy-done.1), channel_id=1, source_target_pairs={{0,8},{8,16},{16,24},{24,32},{32,40},{40,48},{48,56},{56,64},{64,7... | collective-permute-start | bytes 294920 | tf_op jit(solution)/shard_map/ppermute | solution.py:239
  48.8 12.1 %copy-start = (bf16[3,3,3,64,16]{3,4,2,1,0:T(8,128)(2,1)S(1)}, bf16[3,3,3,64,16]{3,4,2,1,0:T(8,128)(2,1)}, u32[]{:S(2)}) copy-start(bf16[3,3,3,64,16]{3,4,2,1,0:T(8,128)(2,1)} %param.5) | copy-start | bytes 165892
  48.8 28.3 %all-to-all-start.2 = ((f32[8,16,128]{2,1,0:T(8,128)}), f32[8,16,128]{2,1,0:T(8,128)S(1)}, u32[]{:S(2)}, u32[]{:S(2)}) async-start(f32[8,16,128]{2,1,0:T(8,128)} %shard_map.78.refs_6_), calls=%async_computation.2 | async-start | bytes 131072 | tf_op jit(solution)/shard_map/all_to_all | solution.py:270
  61.5 8.7 %collective-permute-start.2 = (bf16[48,2048]{1,0:T(8,128)(2,1)S(1)}, bf16[48,2048]{1,0:T(8,128)(2,1)S(1)}, u32[]{:S(2)}, u32[]{:S(2)}) collective-permute-start(bf16[48,2048]{1,0:T(8,128)(2,1)S(1)} %get-tuple-element.19), channel_id=1, source_target_pairs={{0,2},{1,3},{2,4},{3,5},{4,6},{5,7},{6,0},{7,1},{8,10},{9,11},{10,... | collective-permute-start | bytes 589832 | tf_op jit(solution)/shard_map/ppermute | solution.py:257
  63.7 10.6 %collective-permute-start.3 = (bf16[48,2048]{1,0:T(8,128)(2,1)S(1)}, bf16[48,2048]{1,0:T(8,128)(2,1)S(1)}, u32[]{:S(2)}, u32[]{:S(2)}) collective-permute-start(bf16[48,2048]{1,0:T(8,128)(2,1)S(1)} %get-tuple-element.20), channel_id=1, source_target_pairs={{0,4},{1,5},{2,6},{3,7},{4,0},{5,1},{6,2},{7,3},{8,12},{9,13},{10,... | collective-permute-start | bytes 589832 | tf_op jit(solution)/shard_map/ppermute | solution.py:257
  68.3 8.8 %collective-permute-start.4 = (bf16[48,2048]{1,0:T(8,128)(2,1)S(1)}, bf16[48,2048]{1,0:T(8,128)(2,1)S(1)}, u32[]{:S(2)}, u32[]{:S(2)}) collective-permute-start(bf16[48,2048]{1,0:T(8,128)(2,1)S(1)} %get-tuple-element.21), channel_id=1, source_target_pairs={{0,6},{1,7},{2,0},{3,1},{4,2},{5,3},{6,4},{7,5},{8,14},{9,15},{10,... | collective-permute-start | bytes 589832 | tf_op jit(solution)/shard_map/ppermute | solution.py:257
  77.8 11.4 %all-to-all-start.3 = ((f32[16,16,128]{2,1,0:T(8,128)}), f32[16,16,128]{2,1,0:T(8,128)S(1)}, u32[]{:S(2)}, u32[]{:S(2)}) async-start(f32[16,16,128]{2,1,0:T(8,128)} %shard_map.82), calls=%async_computation.3 | async-start | bytes 262144 | tf_op jit(solution)/shard_map/all_to_all | solution.py:285
  82.6 4.2 %copy-start.2 = (f32[16,128]{1,0:T(8,128)S(1)}, f32[16,128]{1,0:T(8,128)}, u32[]{:S(2)}) copy-start(f32[16,128]{1,0:T(8,128)} %get-tuple-element.15.bias) | copy-start | bytes 24580
  82.6 3.5 %collective-permute-start.5 = (bf16[10,8,2048]{2,1,0:T(8,128)(2,1)S(1)}, bf16[10,8,2048]{2,1,0:T(8,128)(2,1)S(1)}, u32[]{:S(2)}, u32[]{:S(2)}) collective-permute-start(bf16[10,8,2048]{2,1,0:T(8,128)(2,1)S(1)} %get-tuple-element.22.mine), channel_id=1, source_target_pairs={{0,1},{1,0},{2,3},{3,2},{4,5},{5,4},{6,7},{7,6},{8,9},{9,8},{10,11... | collective-permute-start | bytes 983048 | tf_op jit(solution)/shard_map/ppermute | solution.py:277

commit v7 on v6

--- a/solution.py
+++ b/solution.py
@@ -17,6 +17,7 @@
 FAR = [[x * Z + h * ZL + k for h in FAR_ORDER] for x in range(X) for k in range(ZL)]
 NEAR = [[x * Z + h * ZL + k for k in NEAR_ORDER for x in range(X)] for h in range(ZH)]
 ROWS, COLS = 16, 128
+FL = 1 << 34
 CELLS = ROWS * COLS
 F32, BF16 = jnp.float32, jnp.bfloat16
 
@@ -188,12 +189,11 @@
         sent[3 + 2 * source] = part[40:48]
 
 
-def narrow_body(kept, got, out, spare):
-    total = kept[...] + (got[0].astype(F32) + got[1].astype(F32))
-    out[...] = lanes_to_cells(total, spare)
-
-
-def feature_body(kernel, bias, here, mine, theirs, out, before, after, spare):
+def feature_body(
+    kernel, bias, here, kept, mine, theirs, out, grad_out, before, after, spare, spare_g
+):
+    total = kept[...] + (theirs[0].astype(F32) + theirs[1].astype(F32))
+    grad_out[...] = lanes_to_cells(total, spare_g)
     odd = lax.rem(lax.axis_index("chan"), 2) == 1
     for side, plane in enumerate((before, after)):
         for y in range(4):
@@ -268,40 +268,36 @@
         [parts],
     )
     parts = lax.all_to_all(spread, SLAB, 0, 0, axis_index_groups=FAR)
+    factor = 1.0 / math.sqrt(slabs * CELLS)
+    (spread,) = call(
+        functools.partial(sum_body, factor),
+        [shape((near, rows, 128), F32)],
+        [parts],
+        flops=FL,
+        after=[own],
+    )
     kept, sent = call(
         join_body,
         [shape((8, CELLS), F32), shape((10, 8, CELLS), BF16)],
         [own, *others, before, after],
         after=[spread],
+        flops=FL,
     )
     got = lax.ppermute(sent, "chan", [(i, i ^ 1) for i in range(groups)])
-    factor = 1.0 / math.sqrt(slabs * CELLS)
-    (spread,) = call(
-        functools.partial(sum_body, factor),
-        [shape((near, rows, 128), F32)],
-        [parts],
-        after=[kept],
-    )
     flat = lax.all_to_all(spread, SLAB, 0, 0, axis_index_groups=NEAR).reshape(256, 128)
     kernel_out, bias_out = call(
         unpack_body, [shape((3, 3, 3, 16, 64), F32), shape((1, 16), F32)], [flat]
     )
 
-    (input_grad,) = call(
-        narrow_body,
-        [shape((8, 1, ROWS, COLS), BF16)],
-        [kept, got],
-        [pltpu.VMEM((8 * ROWS, COLS), F32)],
-    )
-
-    (feature,) = call(
+    feature, input_grad = call(
         feature_body,
-        [shape((16, 1, ROWS, COLS), BF16)],
-        [weights, column, whole, sent, got],
+        [shape((16, 1, ROWS, COLS), BF16), shape((8, 1, ROWS, COLS), BF16)],
+        [weights, column, whole, kept, sent, got],
         [
             pltpu.VMEM((64, CELLS), BF16),
             pltpu.VMEM((64, CELLS), BF16),
             pltpu.VMEM((16 * ROWS, COLS), F32),
+            pltpu.VMEM((8 * ROWS, COLS), F32),
         ],
         flops=2 * 144 * 192 * CELLS,
     )

time: 90.7 us -> 88.5 us (0.976)
  waiting for transfers between devices: 12 us -> 9.61 us
    ppermute x3, waiting for transfers between devices: 6.84 us -> 0.01 us  [on_device(): lax.ppermute(part, 'chan', [(i, (i + 2 * k + 2) % groups) for i in range(...]
    all_to_all x1, waiting for transfers between devices: 0.01 us -> 3.91 us  [on_device(): parts = lax.all_to_all(spread, SLAB, 0, 0, axis_index_groups=FAR)]
    pallas_call x9 -> x8, Pallas kernels: 6.71 us -> 6.04 us  [call(): pl.pallas_call(inner, out_shape=tuple(outs), in_specs=[pl.BlockSpec(memor...]
  transfers between devices with their start and end apart: 9 -> 9, of which waited for: 6 -> 5; matrix products, arithmetic and copies ran while one was open for 0% -> 0% of each run, Pallas kernels for 3% -> 3%
where the time goes in v7:
time: 88.5 us; the launch traced here: 87.6 us
  starting transfers between devices  50.3 us (57%)
  blocking collectives  20.9 us (24%)
  waiting for transfers between devices  9.61 us (11%)
  Pallas kernels  6.04 us (7%)
    all_to_all x1, blocking collectives, on_device(): lax.all_to_all(partial.reshape(near, rows, 128), SLAB, 0, 0, axis_index_g...  20.9 us
    all_to_all x1, starting transfers between devices, on_device(): whole = lax.all_to_all(sent, 'chan', 0, 0).reshape(64, CELLS)  16.4 us
    all_to_all x1, starting transfers between devices, on_device(): parts = lax.all_to_all(spread, SLAB, 0, 0, axis_index_groups=FAR)  12.1 us
    ppermute x3, starting transfers between devices, on_device(): lax.ppermute(part, 'chan', [(i, (i + 2 * k + 2) % groups) for i in range(...  8.67 us
    pallas_call x8, Pallas kernels, call(): pl.pallas_call(inner, out_shape=tuple(outs), in_specs=[pl.BlockSpec(memor...  6.04 us
    all_to_all x1, starting transfers between devices, on_device(): lax.all_to_all(spread, SLAB, 0, 0, axis_index_groups=NEAR).reshape(256, 128)  5.37 us
    ppermute x1, starting transfers between devices, on_device(): before = lax.ppermute(here, SLAB, up)  4.55 us
    all_to_all x1, waiting for transfers between devices, on_device(): parts = lax.all_to_all(spread, SLAB, 0, 0, axis_index_groups=FAR)  3.91 us
  transfers between devices with their start and end apart: 9, of which 5 were waited for; matrix products, arithmetic and copies ran while one was open for 0% of the time, Pallas kernels for 3%

profile of v7, /device:TPU:24, one launch (start us, length us, event | category | flops | bytes accessed | tf_op | source)
XLA Modules:
  0.0 87.6 jit_solution(14824231243782208133)
XLA Ops:
  0.6 1.7 %shard_map.75 = (bf16[8,8,2048]{2,1,0:T(8,128)(2,1)}, bf16[24,2048]{1,0:T(8,128)(2,1)}, f32[16,128]{1,0:T(8,128)}) custom-call(bf16[8,1,16,128]{3,2,1,0:T(8,128)(2,1)} %volume.1, bf16[16,1,16,128]{3,2,1,0:T(8,128)(2,1)} %grad.1, f32[1,16]{1,0:T(1,128)} %bitcast.13), custom_call_target="tpu_custom_call" | custom-call | bytes 467008 | tf_op jit(solution)/shard_map/pallas_call | solution.py:34
  2.3 0.0 copy-start.1
  2.3 16.4 %all-to-all-start = ((bf16[8,8,2048]{2,1,0:T(8,128)(2,1)}), bf16[8,8,2048]{2,1,0:T(8,128)(2,1)S(1)}, u32[]{:S(2)}, u32[]{:S(2)}) async-start(bf16[8,8,2048]{2,1,0:T(8,128)(2,1)} %get-tuple-element.18), calls=%async_computation | async-start | bytes 524288 | tf_op jit(solution)/shard_map/all_to_all | solution.py:241
  18.7 0.0 copy-done.1
  18.7 1.3 %collective-permute-start = (bf16[24,2048]{1,0:T(8,128)(2,1)S(1)}, bf16[24,2048]{1,0:T(8,128)(2,1)S(1)}, u32[]{:S(2)}, u32[]{:S(2)}) collective-permute-start(bf16[24,2048]{1,0:T(8,128)(2,1)S(1)} %copy-done.1), channel_id=1, source_target_pairs={{8,0},{16,8},{24,16},{32,24},{40,32},{48,40},{56,48},{64,56},{72,6... | collective-permute-start | bytes 294920 | tf_op jit(solution)/shard_map/ppermute | solution.py:240
  20.0 4.6 %collective-permute-start.1 = (bf16[24,2048]{1,0:T(8,128)(2,1)S(1)}, bf16[24,2048]{1,0:T(8,128)(2,1)S(1)}, u32[]{:S(2)}, u32[]{:S(2)}) collective-permute-start(bf16[24,2048]{1,0:T(8,128)(2,1)S(1)} %copy-done.1), channel_id=1, source_target_pairs={{0,8},{8,16},{16,24},{24,32},{32,40},{40,48},{48,56},{56,64},{64,7... | collective-permute-start | bytes 294920 | tf_op jit(solution)/shard_map/ppermute | solution.py:239
  24.5 0.9 %collective-permute-done.after.refs_5_ = bf16[24,2048]{1,0:T(8,128)(2,1)S(1)} collective-permute-done((bf16[24,2048]{1,0:T(8,128)(2,1)S(1)}, bf16[24,2048]{1,0:T(8,128)(2,1)S(1)}, u32[]{:S(2)}, u32[]{:S(2)}) %collective-permute-start) | collective-permute-done | bytes 98336 | tf_op jit(solution)/shard_map/ppermute | solution.py:240
  25.4 1.3 %collective-permute-done.1.before.refs_4_ = bf16[24,2048]{1,0:T(8,128)(2,1)S(1)} collective-permute-done((bf16[24,2048]{1,0:T(8,128)(2,1)S(1)}, bf16[24,2048]{1,0:T(8,128)(2,1)S(1)}, u32[]{:S(2)}, u32[]{:S(2)}) %collective-permute-start.1) | collective-permute-done | bytes 98336 | tf_op jit(solution)/shard_map/ppermute | solution.py:239
  26.7 0.0 all-to-all-done
  26.7 0.6 shard_map.77
  27.3 20.9 %all_to_all.20.parts = f32[16,16,128]{2,1,0:T(8,128)S(1)} all-to-all(f32[16,16,128]{2,1,0:T(8,128)S(1)} %bitcast.10), channel_id=1, replica_groups={{16,272,528,784,24,280,536,792,0,256,512,768,8,264,520,776},{48,304,560..., dimensions={0} | all-to-all | bytes 262144 | tf_op jit(solution)/shard_map/all_to_all | solution.py:262
  48.1 0.6 shard_map.78
  48.8 12.1 %all-to-all-start.2 = ((f32[8,16,128]{2,1,0:T(8,128)}), f32[8,16,128]{2,1,0:T(8,128)S(1)}, u32[]{:S(2)}, u32[]{:S(2)}) async-start(f32[8,16,128]{2,1,0:T(8,128)} %shard_map.78), calls=%async_computation.2 | async-start | bytes 131072 | tf_op jit(solution)/shard_map/all_to_all | solution.py:270
  60.9 0.0 copy-done
  60.9 0.6 shard_map.76
  61.5 2.2 %collective-permute-start.2 = (bf16[48,2048]{1,0:T(8,128)(2,1)S(1)}, bf16[48,2048]{1,0:T(8,128)(2,1)S(1)}, u32[]{:S(2)}, u32[]{:S(2)}) collective-permute-start(bf16[48,2048]{1,0:T(8,128)(2,1)S(1)} %get-tuple-element.21), channel_id=1, source_target_pairs={{0,2},{1,3},{2,4},{3,5},{4,6},{5,7},{6,0},{7,1},{8,10},{9,11},{10,... | collective-permute-start | bytes 589832 | tf_op jit(solution)/shard_map/ppermute | solution.py:257
  63.7 4.5 %collective-permute-start.3 = (bf16[48,2048]{1,0:T(8,128)(2,1)S(1)}, bf16[48,2048]{1,0:T(8,128)(2,1)S(1)}, u32[]{:S(2)}, u32[]{:S(2)}) collective-permute-start(bf16[48,2048]{1,0:T(8,128)(2,1)S(1)} %get-tuple-element.22), channel_id=1, source_target_pairs={{0,4},{1,5},{2,6},{3,7},{4,0},{5,1},{6,2},{7,3},{8,12},{9,13},{10,... | collective-permute-start | bytes 589832 | tf_op jit(solution)/shard_map/ppermute | solution.py:257
  68.3 1.9 %collective-permute-start.4 = (bf16[48,2048]{1,0:T(8,128)(2,1)S(1)}, bf16[48,2048]{1,0:T(8,128)(2,1)S(1)}, u32[]{:S(2)}, u32[]{:S(2)}) collective-permute-start(bf16[48,2048]{1,0:T(8,128)(2,1)S(1)} %get-tuple-element.23), channel_id=1, source_target_pairs={{0,6},{1,7},{2,0},{3,1},{4,2},{5,3},{6,4},{7,5},{8,14},{9,15},{10,... | collective-permute-start | bytes 589832 | tf_op jit(solution)/shard_map/ppermute | solution.py:257
  70.2 3.9 %all-to-all-done.2.refs_0_ = f32[8,16,128]{2,1,0:T(8,128)S(1)} async-done(((f32[8,16,128]{2,1,0:T(8,128)}), f32[8,16,128]{2,1,0:T(8,128)S(1)}, u32[]{:S(2)}, u32[]{:S(2)}) %all-to-all-start.2) | async-done | bytes 65568 | tf_op jit(solution)/shard_map/all_to_all | solution.py:270
  74.1 0.7 shard_map.79.refs_6_
  74.8 5.4 %all-to-all-start.3 = ((f32[16,16,128]{2,1,0:T(8,128)}), f32[16,16,128]{2,1,0:T(8,128)S(1)}, u32[]{:S(2)}, u32[]{:S(2)}) async-start(f32[16,16,128]{2,1,0:T(8,128)} %shard_map.79.refs_6_), calls=%async_computation.3 | async-start | bytes 262144 | tf_op jit(solution)/shard_map/all_to_all | solution.py:287
  80.1 0.0 collective-permute-done.2.refs_1_
  80.1 0.0 collective-permute-done.3.refs_2_
  80.2 0.0 collective-permute-done.4.refs_3_
  80.2 0.0 copy-start.2
  80.2 0.1 shard_map.80
  80.3 1.9 %collective-permute-start.5 = (bf16[10,8,2048]{2,1,0:T(8,128)(2,1)S(1)}, bf16[10,8,2048]{2,1,0:T(8,128)(2,1)S(1)}, u32[]{:S(2)}, u32[]{:S(2)}) collective-permute-start(bf16[10,8,2048]{2,1,0:T(8,128)(2,1)S(1)} %get-tuple-element.25.mine), channel_id=1, source_target_pairs={{0,1},{1,0},{2,3},{3,2},{4,5},{5,4},{6,7},{7,6},{8,9},{9,8},{10,11... | collective-permute-start | bytes 983048 | tf_op jit(solution)/shard_map/ppermute | solution.py:286
  82.2 1.6 %collective-permute-done.5.theirs = bf16[10,8,2048]{2,1,0:T(8,128)(2,1)S(1)} collective-permute-done((bf16[10,8,2048]{2,1,0:T(8,128)(2,1)S(1)}, bf16[10,8,2048]{2,1,0:T(8,128)(2,1)S(1)}, u32[]{:S(2)}, u32[]{:S(2)}) %collective-permute-start.5) | collective-permute-done | bytes 327712 | tf_op jit(solution)/shard_map/ppermute | solution.py:286
  83.8 0.0 copy-done.2
  83.8 1.1 %shard_map.81 = (bf16[16,1,16,128]{3,2,1,0:T(8,128)(2,1)}, bf16[8,1,16,128]{3,2,1,0:T(8,128)(2,1)}) custom-call(bf16[3,3,3,16,64]{4,3,2,1,0:T(8,128)(2,1)S(1)} %bitcast.12, f32[16,128]{1,0:T(8,128)S(1)} %copy-done.2, bf16[64,2048]{1,0:T(8,128)(2,1)S(1)} %bitcast.8, f32[8,2048]{1,0:T(8,128)S(1)} %get-tuple-element.24.kept, ...), custom_call_target="tpu_custom_call" | custom-call | flops 113246208 | bytes 1144832 | tf_op jit(solution)/shard_map/pallas_call | solution.py:34
  84.9 1.9 %all-to-all-done.3 = f32[16,16,128]{2,1,0:T(8,128)S(1)} async-done(((f32[16,16,128]{2,1,0:T(8,128)}), f32[16,16,128]{2,1,0:T(8,128)S(1)}, u32[]{:S(2)}, u32[]{:S(2)}) %all-to-all-start.3) | async-done | bytes 131104 | tf_op jit(solution)/shard_map/all_to_all | solution.py:287
  86.8 0.8 shard_map.82
  (1 shorter events, 0.0 us)
Async XLA Ops:
  2.3 16.4 %copy-start.1 = (bf16[24,2048]{1,0:T(8,128)(2,1)S(1)}, bf16[24,2048]{1,0:T(8,128)(2,1)}, u32[]{:S(2)}) copy-start(bf16[24,2048]{1,0:T(8,128)(2,1)} %get-tuple-element.19.here) | copy-start | bytes 294916
  2.3 24.4 %all-to-all-start = ((bf16[8,8,2048]{2,1,0:T(8,128)(2,1)}), bf16[8,8,2048]{2,1,0:T(8,128)(2,1)S(1)}, u32[]{:S(2)}, u32[]{:S(2)}) async-start(bf16[8,8,2048]{2,1,0:T(8,128)(2,1)} %get-tuple-element.18), calls=%async_computation | async-start | bytes 524288 | tf_op jit(solution)/shard_map/all_to_all | solution.py:241
  18.7 6.7 %collective-permute-start = (bf16[24,2048]{1,0:T(8,128)(2,1)S(1)}, bf16[24,2048]{1,0:T(8,128)(2,1)S(1)}, u32[]{:S(2)}, u32[]{:S(2)}) collective-permute-start(bf16[24,2048]{1,0:T(8,128)(2,1)S(1)} %copy-done.1), channel_id=1, source_target_pairs={{8,0},{16,8},{24,16},{32,24},{40,32},{48,40},{56,48},{64,56},{72,6... | collective-permute-start | bytes 294920 | tf_op jit(solution)/shard_map/ppermute | solution.py:240
  20.0 6.8 %collective-permute-start.1 = (bf16[24,2048]{1,0:T(8,128)(2,1)S(1)}, bf16[24,2048]{1,0:T(8,128)(2,1)S(1)}, u32[]{:S(2)}, u32[]{:S(2)}) collective-permute-start(bf16[24,2048]{1,0:T(8,128)(2,1)S(1)} %copy-done.1), channel_id=1, source_target_pairs={{0,8},{8,16},{16,24},{24,32},{32,40},{40,48},{48,56},{56,64},{64,7... | collective-permute-start | bytes 294920 | tf_op jit(solution)/shard_map/ppermute | solution.py:239
  48.8 12.1 %copy-start = (bf16[3,3,3,64,16]{3,4,2,1,0:T(8,128)(2,1)S(1)}, bf16[3,3,3,64,16]{3,4,2,1,0:T(8,128)(2,1)}, u32[]{:S(2)}) copy-start(bf16[3,3,3,64,16]{3,4,2,1,0:T(8,128)(2,1)} %param.5) | copy-start | bytes 165892
  48.8 25.3 %all-to-all-start.2 = ((f32[8,16,128]{2,1,0:T(8,128)}), f32[8,16,128]{2,1,0:T(8,128)S(1)}, u32[]{:S(2)}, u32[]{:S(2)}) async-start(f32[8,16,128]{2,1,0:T(8,128)} %shard_map.78), calls=%async_computation.2 | async-start | bytes 131072 | tf_op jit(solution)/shard_map/all_to_all | solution.py:270
  61.5 18.7 %collective-permute-start.2 = (bf16[48,2048]{1,0:T(8,128)(2,1)S(1)}, bf16[48,2048]{1,0:T(8,128)(2,1)S(1)}, u32[]{:S(2)}, u32[]{:S(2)}) collective-permute-start(bf16[48,2048]{1,0:T(8,128)(2,1)S(1)} %get-tuple-element.21), channel_id=1, source_target_pairs={{0,2},{1,3},{2,4},{3,5},{4,6},{5,7},{6,0},{7,1},{8,10},{9,11},{10,... | collective-permute-start | bytes 589832 | tf_op jit(solution)/shard_map/ppermute | solution.py:257
  63.7 16.4 %collective-permute-start.3 = (bf16[48,2048]{1,0:T(8,128)(2,1)S(1)}, bf16[48,2048]{1,0:T(8,128)(2,1)S(1)}, u32[]{:S(2)}, u32[]{:S(2)}) collective-permute-start(bf16[48,2048]{1,0:T(8,128)(2,1)S(1)} %get-tuple-element.22), channel_id=1, source_target_pairs={{0,4},{1,5},{2,6},{3,7},{4,0},{5,1},{6,2},{7,3},{8,12},{9,13},{10,... | collective-permute-start | bytes 589832 | tf_op jit(solution)/shard_map/ppermute | solution.py:257
  68.3 11.9 %collective-permute-start.4 = (bf16[48,2048]{1,0:T(8,128)(2,1)S(1)}, bf16[48,2048]{1,0:T(8,128)(2,1)S(1)}, u32[]{:S(2)}, u32[]{:S(2)}) collective-permute-start(bf16[48,2048]{1,0:T(8,128)(2,1)S(1)} %get-tuple-element.23), channel_id=1, source_target_pairs={{0,6},{1,7},{2,0},{3,1},{4,2},{5,3},{6,4},{7,5},{8,14},{9,15},{10,... | collective-permute-start | bytes 589832 | tf_op jit(solution)/shard_map/ppermute | solution.py:257
  74.8 12.0 %all-to-all-start.3 = ((f32[16,16,128]{2,1,0:T(8,128)}), f32[16,16,128]{2,1,0:T(8,128)S(1)}, u32[]{:S(2)}, u32[]{:S(2)}) async-start(f32[16,16,128]{2,1,0:T(8,128)} %shard_map.79.refs_6_), calls=%async_computation.3 | async-start | bytes 262144 | tf_op jit(solution)/shard_map/all_to_all | solution.py:287
  80.2 3.6 %copy-start.2 = (f32[16,128]{1,0:T(8,128)S(1)}, f32[16,128]{1,0:T(8,128)}, u32[]{:S(2)}) copy-start(f32[16,128]{1,0:T(8,128)} %get-tuple-element.17.bias) | copy-start | bytes 24580
  80.3 3.5 %collective-permute-start.5 = (bf16[10,8,2048]{2,1,0:T(8,128)(2,1)S(1)}, bf16[10,8,2048]{2,1,0:T(8,128)(2,1)S(1)}, u32[]{:S(2)}, u32[]{:S(2)}) collective-permute-start(bf16[10,8,2048]{2,1,0:T(8,128)(2,1)S(1)} %get-tuple-element.25.mine), channel_id=1, source_target_pairs={{0,1},{1,0},{2,3},{3,2},{4,5},{5,4},{6,7},{7,6},{8,9},{9,8},{10,11... | collective-permute-start | bytes 983048 | tf_op jit(solution)/shard_map/ppermute | solution.py:286

commit v8 on v7

--- a/solution.py
+++ b/solution.py
@@ -149,7 +149,7 @@
     bias_out[...] = flat[216:217, 0:16]
 
 
-def input_grad_body(kernel, after, here, before, own, first, second, third, blocks):
+def input_grad_body(kernel, after, here, before, kept, sent):
     left = jnp.concatenate([kernel[:, b].reshape(144, 64) for b in range(3)], axis=1)
     right = jnp.concatenate(
         [from_col(g[0:16], 1 - c) for g in (after, here, before) for c in range(3)], axis=0
@@ -158,14 +158,13 @@
     total = sums[64:128]
     total = total + from_row(sums[0:64], 1)
     total = total + from_row(sums[128:192], -1)
+    odd = lax.rem(lax.axis_index("chan"), 2) == 1
     for y in range(4):
-        blocks[y] = total[16 * y : 16 * y + 16]
-    y = lax.div(lax.axis_index("chan"), 2)
-    own[...] = blocks[y]
-    for k, out in enumerate((first, second, third)):
-        out[0:16], out[16:32] = halves(blocks[lax.rem(y + k + 1, 4)])
-        out[32:40] = before[16:24]
-        out[40:48] = after[16:24]
+        first, second = total[16 * y : 16 * y + 8], total[16 * y + 8 : 16 * y + 16]
+        kept[y] = jnp.where(odd, second, first)
+        sent[y], sent[4 + y] = halves(jnp.where(odd, first, second))
+    sent[8] = before[16:24]
+    sent[9] = after[16:24]
 
 
 def halves(value):
@@ -173,33 +172,37 @@
     return high, (value - high.astype(F32)).astype(BF16)
 
 
-def join_body(own, first, second, third, before, after, kept, sent):
+def join_body(kept, got, before, after, own, *sent):
     chan = lax.axis_index("chan")
     y, odd = lax.div(chan, 2), lax.rem(chan, 2) == 1
-    total = own[...]
+    for k, out in enumerate((own, *sent)):
+        block = lax.rem(y + k, 4)
+        total = kept[block] + got[block].astype(F32) + got[4 + block].astype(F32)
+        if k == 0:
+            out[...] = total
+        else:
+            out[0:8], out[8:16] = halves(total)
+    for row, mine, theirs in ((16, before, got[8]), (32, after, got[9])):
+        mine, theirs = mine[16:24].astype(F32), theirs.astype(F32)
+        first = jnp.where(odd, theirs, mine).astype(BF16)
+        second = jnp.where(odd, mine, theirs).astype(BF16)
+        for out in sent:
+            out[row : row + 8] = first
+            out[row + 8 : row + 16] = second
+
+
+def feature_body(
+    kernel, bias, here, share, own, first, second, third, out, grad_out, before, after, spare, spare_g
+):
+    total = share[...]
     for part in (first, second, third):
-        total = total + (part[0:16].astype(F32) + part[16:32].astype(F32))
-    kept[...] = jnp.where(odd, total[8:16], total[0:8])
-    sent[0], sent[1] = halves(jnp.where(odd, total[0:8], total[8:16]))
-    sent[2 + 2 * y] = before[16:24]
-    sent[3 + 2 * y] = after[16:24]
-    for k, part in enumerate((first, second, third)):
-        source = lax.rem(y + 3 - k, 4)
-        sent[2 + 2 * source] = part[32:40]
-        sent[3 + 2 * source] = part[40:48]
-
-
-def feature_body(
-    kernel, bias, here, kept, mine, theirs, out, grad_out, before, after, spare, spare_g
-):
-    total = kept[...] + (theirs[0].astype(F32) + theirs[1].astype(F32))
+        total = total + (part[0:8].astype(F32) + part[8:16].astype(F32))
     grad_out[...] = lanes_to_cells(total, spare_g)
-    odd = lax.rem(lax.axis_index("chan"), 2) == 1
-    for side, plane in enumerate((before, after)):
-        for y in range(4):
-            a, b = mine[2 + 2 * y + side].astype(F32), theirs[2 + 2 * y + side].astype(F32)
-            plane[16 * y : 16 * y + 8] = jnp.where(odd, b, a).astype(BF16)
-            plane[16 * y + 8 : 16 * y + 16] = jnp.where(odd, a, b).astype(BF16)
+    y = lax.div(lax.axis_index("chan"), 2)
+    for k, part in enumerate((own, first, second, third)):
+        place = pl.ds(pl.multiple_of(16 * lax.rem(y + 4 - k, 4), 16), 16)
+        before[place] = part[16:32]
+        after[place] = part[32:48]
     left = jnp.concatenate([kernel[a].reshape(144, 64) for a in range(3)], axis=1)
     right = jnp.concatenate([before[...], here[...], after[...]], axis=0)
     sums = jnp.dot(left, right, preferred_element_type=F32)
@@ -246,17 +249,6 @@
         [whole, after, here, before],
         flops=2 * 144 * 192 * CELLS,
     )
-    own, *shares = call(
-        input_grad_body,
-        [shape((16, CELLS), F32)] + [shape((48, CELLS), BF16)] * 3,
-        [weights, after, here, before],
-        [pltpu.VMEM((4, 16, CELLS), F32)],
-        flops=2 * 144 * 192 * CELLS,
-    )
-    others = [
-        lax.ppermute(part, "chan", [(i, (i + 2 * k + 2) % groups) for i in range(groups)])
-        for k, part in enumerate(shares)
-    ]
     near = X * ZL
     rows = 256 // near
     parts = lax.all_to_all(
@@ -268,22 +260,33 @@
         [parts],
     )
     parts = lax.all_to_all(spread, SLAB, 0, 0, axis_index_groups=FAR)
+
+    kept, sent = call(
+        input_grad_body,
+        [shape((4, 8, CELLS), F32), shape((10, 8, CELLS), BF16)],
+        [weights, after, here, before],
+        flops=2 * 144 * 192 * CELLS,
+        after=[spread],
+    )
+    got = lax.ppermute(sent, "chan", [(i, i ^ 1) for i in range(groups)])
+    share, *joined = call(
+        join_body,
+        [shape((8, CELLS), F32)] + [shape((48, CELLS), BF16)] * 3,
+        [kept, got, before, after],
+    )
+    others = [
+        lax.ppermute(part, "chan", [(i, (i + 2 * k + 2) % groups) for i in range(groups)])
+        for k, part in enumerate(joined)
+    ]
+
     factor = 1.0 / math.sqrt(slabs * CELLS)
     (spread,) = call(
         functools.partial(sum_body, factor),
         [shape((near, rows, 128), F32)],
         [parts],
         flops=FL,
-        after=[own],
-    )
-    kept, sent = call(
-        join_body,
-        [shape((8, CELLS), F32), shape((10, 8, CELLS), BF16)],
-        [own, *others, before, after],
-        after=[spread],
-        flops=FL,
-    )
-    got = lax.ppermute(sent, "chan", [(i, i ^ 1) for i in range(groups)])
+        after=[share],
+    )
     flat = lax.all_to_all(spread, SLAB, 0, 0, axis_index_groups=NEAR).reshape(256, 128)
     kernel_out, bias_out = call(
         unpack_body, [shape((3, 3, 3, 16, 64), F32), shape((1, 16), F32)], [flat]
@@ -292,14 +295,15 @@
     feature, input_grad = call(
         feature_body,
         [shape((16, 1, ROWS, COLS), BF16), shape((8, 1, ROWS, COLS), BF16)],
-        [weights, column, whole, kept, sent, got],
+        [weights, column, whole, share, joined[0], *others],
         [
             pltpu.VMEM((64, CELLS), BF16),
             pltpu.VMEM((64, CELLS), BF16),
             pltpu.VMEM((16 * ROWS, COLS), F32),
             pltpu.VMEM((8 * ROWS, COLS), F32),
         ],
-        flops=2 * 144 * 192 * CELLS,
+        flops=FL,
+        after=[spread],
     )
     return (
         feature,

time: 88.5 us -> 92 us (1.040)
  starting transfers between devices: 50.3 us -> 55.4 us
  blocking collectives: 20.9 us -> 16.5 us
  waiting for transfers between devices: 9.61 us -> 12.6 us
    all_to_all x1, starting transfers between devices: 12.1 us -> 19.3 us  [on_device(): parts = lax.all_to_all(spread, SLAB, 0, 0, axis_index_groups=FAR)]
    all_to_all x1, blocking collectives: 20.9 us -> 16.5 us  [on_device(): lax.all_to_all(partial.reshape(near, rows, 128), SLAB, 0, 0, axis_index_g...]
    all_to_all x1, waiting for transfers between devices: 3.91 us -> 0.01 us  [on_device(): parts = lax.all_to_all(spread, SLAB, 0, 0, axis_index_groups=FAR)]
    all_to_all x1, waiting for transfers between devices: 1.9 us -> 5.54 us  [on_device(): lax.all_to_all(spread, SLAB, 0, 0, axis_index_groups=NEAR).reshape(256, 128)]
    ppermute x1, starting transfers between devices: 4.55 us -> 1.28 us  [on_device(): before = lax.ppermute(here, SLAB, up)]
    ppermute x1, waiting for transfers between devices: 0.88 us -> 4.12 us  [on_device(): after = lax.ppermute(here, SLAB, down)]
    ppermute x3, starting transfers between devices: 8.67 us -> 10.4 us  [on_device(): lax.ppermute(part, 'chan', [(i, (i + 2 * k + 2) % groups) for i in range(...]
  transfers between devices with their start and end apart: 9 -> 9, of which waited for: 5 -> 4; matrix products, arithmetic and copies ran while one was open for 0% -> 0% of each run, Pallas kernels for 3% -> 3%
where the time goes in v8:
time: 92 us; the launch traced here: 91.3 us
  starting transfers between devices  55.4 us (60%)
  blocking collectives  16.5 us (18%)
  waiting for transfers between devices  12.6 us (14%)
  Pallas kernels  6.03 us (7%)
    all_to_all x1, starting transfers between devices, on_device(): parts = lax.all_to_all(spread, SLAB, 0, 0, axis_index_groups=FAR)  19.3 us
    all_to_all x1, blocking collectives, on_device(): lax.all_to_all(partial.reshape(near, rows, 128), SLAB, 0, 0, axis_index_g...  16.5 us
    all_to_all x1, starting transfers between devices, on_device(): whole = lax.all_to_all(sent, 'chan', 0, 0).reshape(64, CELLS)  16.4 us
    ppermute x3, starting transfers between devices, on_device(): lax.ppermute(part, 'chan', [(i, (i + 2 * k + 2) % groups) for i in range(...  10.4 us
    pallas_call x8, Pallas kernels, call(): pl.pallas_call(inner, out_shape=tuple(outs), in_specs=[pl.BlockSpec(memor...  6.03 us
    all_to_all x1, waiting for transfers between devices, on_device(): lax.all_to_all(spread, SLAB, 0, 0, axis_index_groups=NEAR).reshape(256, 128)  5.54 us
    all_to_all x1, starting transfers between devices, on_device(): lax.all_to_all(spread, SLAB, 0, 0, axis_index_groups=NEAR).reshape(256, 128)  4.86 us
    ppermute x1, waiting for transfers between devices, on_device(): after = lax.ppermute(here, SLAB, down)  4.12 us
  transfers between devices with their start and end apart: 9, of which 4 were waited for; matrix products, arithmetic and copies ran while one was open for 0% of the time, Pallas kernels for 3%

profile of v8, /device:TPU:24, one launch (start us, length us, event | category | flops | bytes accessed | tf_op | source)
XLA Modules:
  0.0 91.3 jit_solution(15436697990831518921)
XLA Ops:
  0.6 1.7 %shard_map.75 = (bf16[8,8,2048]{2,1,0:T(8,128)(2,1)}, bf16[24,2048]{1,0:T(8,128)(2,1)}, f32[16,128]{1,0:T(8,128)}) custom-call(bf16[8,1,16,128]{3,2,1,0:T(8,128)(2,1)} %volume.1, bf16[16,1,16,128]{3,2,1,0:T(8,128)(2,1)} %grad.1, f32[1,16]{1,0:T(1,128)} %bitcast.13), custom_call_target="tpu_custom_call" | custom-call | bytes 467008 | tf_op jit(solution)/shard_map/pallas_call | solution.py:34
  2.3 0.0 copy-start
  2.3 16.4 %all-to-all-start = ((bf16[8,8,2048]{2,1,0:T(8,128)(2,1)}), bf16[8,8,2048]{2,1,0:T(8,128)(2,1)S(1)}, u32[]{:S(2)}, u32[]{:S(2)}) async-start(bf16[8,8,2048]{2,1,0:T(8,128)(2,1)} %get-tuple-element.18), calls=%async_computation | async-start | bytes 524288 | tf_op jit(solution)/shard_map/all_to_all | solution.py:244
  18.7 0.0 copy-done
  18.7 1.3 %collective-permute-start.1 = (bf16[24,2048]{1,0:T(8,128)(2,1)S(1)}, bf16[24,2048]{1,0:T(8,128)(2,1)S(1)}, u32[]{:S(2)}, u32[]{:S(2)}) collective-permute-start(bf16[24,2048]{1,0:T(8,128)(2,1)S(1)} %copy-done), channel_id=1, source_target_pairs={{0,8},{8,16},{16,24},{24,32},{32,40},{40,48},{48,56},{56,64},{64,7... | collective-permute-start | bytes 294920 | tf_op jit(solution)/shard_map/ppermute | solution.py:242
  20.0 1.3 %collective-permute-start = (bf16[24,2048]{1,0:T(8,128)(2,1)S(1)}, bf16[24,2048]{1,0:T(8,128)(2,1)S(1)}, u32[]{:S(2)}, u32[]{:S(2)}) collective-permute-start(bf16[24,2048]{1,0:T(8,128)(2,1)S(1)} %copy-done), channel_id=1, source_target_pairs={{8,0},{16,8},{24,16},{32,24},{40,32},{48,40},{56,48},{64,56},{72,6... | collective-permute-start | bytes 294920 | tf_op jit(solution)/shard_map/ppermute | solution.py:243
  21.3 1.3 %collective-permute-done.1.before.refs_3_ = bf16[24,2048]{1,0:T(8,128)(2,1)S(1)} collective-permute-done((bf16[24,2048]{1,0:T(8,128)(2,1)S(1)}, bf16[24,2048]{1,0:T(8,128)(2,1)S(1)}, u32[]{:S(2)}, u32[]{:S(2)}) %collective-permute-start.1) | collective-permute-done | bytes 98336 | tf_op jit(solution)/shard_map/ppermute | solution.py:242
  22.6 4.1 %collective-permute-done.after.refs_1_ = bf16[24,2048]{1,0:T(8,128)(2,1)S(1)} collective-permute-done((bf16[24,2048]{1,0:T(8,128)(2,1)S(1)}, bf16[24,2048]{1,0:T(8,128)(2,1)S(1)}, u32[]{:S(2)}, u32[]{:S(2)}) %collective-permute-start) | collective-permute-done | bytes 98336 | tf_op jit(solution)/shard_map/ppermute | solution.py:243
  26.7 0.0 all-to-all-done
  26.7 0.6 shard_map.76
  27.3 16.5 %all_to_all.20.parts = f32[16,16,128]{2,1,0:T(8,128)S(1)} all-to-all(f32[16,16,128]{2,1,0:T(8,128)S(1)} %bitcast.10), channel_id=1, replica_groups={{16,272,528,784,24,280,536,792,0,256,512,768,8,264,520,776},{48,304,560..., dimensions={0} | all-to-all | bytes 262144 | tf_op jit(solution)/shard_map/all_to_all | solution.py:254
  43.8 0.6 shard_map.77.refs_4_
  44.4 0.0 copy-start.1
  44.4 19.3 %all-to-all-start.2 = ((f32[8,16,128]{2,1,0:T(8,128)}), f32[8,16,128]{2,1,0:T(8,128)S(1)}, u32[]{:S(2)}, u32[]{:S(2)}) async-start(f32[8,16,128]{2,1,0:T(8,128)} %shard_map.77.refs_4_), calls=%async_computation.2 | async-start | bytes 131072 | tf_op jit(solution)/shard_map/all_to_all | solution.py:262
  63.7 0.0 copy-done.1
  63.7 0.5 shard_map.78
  64.3 1.9 %collective-permute-start.2 = (bf16[10,8,2048]{2,1,0:T(8,128)(2,1)S(1)}, bf16[10,8,2048]{2,1,0:T(8,128)(2,1)S(1)}, u32[]{:S(2)}, u32[]{:S(2)}) collective-permute-start(bf16[10,8,2048]{2,1,0:T(8,128)(2,1)S(1)} %get-tuple-element.21), channel_id=1, source_target_pairs={{0,1},{1,0},{2,3},{3,2},{4,5},{5,4},{6,7},{7,6},{8,9},{9,8},{10,11... | collective-permute-start | bytes 983048 | tf_op jit(solution)/shard_map/ppermute | solution.py:271
  66.2 1.6 %collective-permute-done.2.got = bf16[10,8,2048]{2,1,0:T(8,128)(2,1)S(1)} collective-permute-done((bf16[10,8,2048]{2,1,0:T(8,128)(2,1)S(1)}, bf16[10,8,2048]{2,1,0:T(8,128)(2,1)S(1)}, u32[]{:S(2)}, u32[]{:S(2)}) %collective-permute-start.2) | collective-permute-done | bytes 327712 | tf_op jit(solution)/shard_map/ppermute | solution.py:271
  67.8 0.1 shard_map.79
  67.9 3.4 %collective-permute-start.4 = (bf16[48,2048]{1,0:T(8,128)(2,1)S(1)}, bf16[48,2048]{1,0:T(8,128)(2,1)S(1)}, u32[]{:S(2)}, u32[]{:S(2)}) collective-permute-start(bf16[48,2048]{1,0:T(8,128)(2,1)S(1)} %get-tuple-element.24), channel_id=1, source_target_pairs={{0,4},{1,5},{2,6},{3,7},{4,0},{5,1},{6,2},{7,3},{8,12},{9,13},{10,... | collective-permute-start | bytes 589832 | tf_op jit(solution)/shard_map/ppermute | solution.py:278
  71.3 1.9 %collective-permute-start.5 = (bf16[48,2048]{1,0:T(8,128)(2,1)S(1)}, bf16[48,2048]{1,0:T(8,128)(2,1)S(1)}, u32[]{:S(2)}, u32[]{:S(2)}) collective-permute-start(bf16[48,2048]{1,0:T(8,128)(2,1)S(1)} %get-tuple-element.25), channel_id=1, source_target_pairs={{0,6},{1,7},{2,0},{3,1},{4,2},{5,3},{6,4},{7,5},{8,14},{9,15},{10,... | collective-permute-start | bytes 589832 | tf_op jit(solution)/shard_map/ppermute | solution.py:278
  73.2 5.1 %collective-permute-start.3 = (bf16[48,2048]{1,0:T(8,128)(2,1)S(1)}, bf16[48,2048]{1,0:T(8,128)(2,1)S(1)}, u32[]{:S(2)}, u32[]{:S(2)}) collective-permute-start(bf16[48,2048]{1,0:T(8,128)(2,1)S(1)} %get-tuple-element.23.refs_4_), channel_id=1, source_target_pairs={{0,2},{1,3},{2,4},{3,5},{4,6},{5,7},{6,0},{7,1},{8,10},{9,11},{10,... | collective-permute-start | bytes 589832 | tf_op jit(solution)/shard_map/ppermute | solution.py:278
  78.3 0.0 all-to-all-done.2.refs_0_
  78.3 0.7 shard_map.80.refs_8_
  79.0 4.9 %all-to-all-start.3 = ((f32[16,16,128]{2,1,0:T(8,128)}), f32[16,16,128]{2,1,0:T(8,128)S(1)}, u32[]{:S(2)}, u32[]{:S(2)}) async-start(f32[16,16,128]{2,1,0:T(8,128)} %shard_map.80.refs_8_), calls=%async_computation.3 | async-start | bytes 262144 | tf_op jit(solution)/shard_map/all_to_all | solution.py:290
  83.9 0.0 collective-permute-done.4.refs_6_
  83.9 0.0 collective-permute-done.5.refs_7_
  83.9 0.0 collective-permute-done.3.refs_5_
  83.9 0.0 copy-done.2
  83.9 1.1 %shard_map.81 = (bf16[16,1,16,128]{3,2,1,0:T(8,128)(2,1)}, bf16[8,1,16,128]{3,2,1,0:T(8,128)(2,1)}) custom-call(bf16[3,3,3,16,64]{4,3,2,1,0:T(8,128)(2,1)S(1)} %bitcast.12, f32[16,128]{1,0:T(8,128)S(1)} %copy-done.2, bf16[64,2048]{1,0:T(8,128)(2,1)S(1)} %bitcast.8, f32[8,2048]{1,0:T(8,128)S(1)} %get-tuple-element.22.refs_1_.refs_3_, ...), custom_call_target="tpu_custom_call" | custom-call | flops 17179869184 | bytes 1406976 | tf_op jit(solution)/shard_map/pallas_call | solution.py:34
  85.0 5.5 %all-to-all-done.3 = f32[16,16,128]{2,1,0:T(8,128)S(1)} async-done(((f32[16,16,128]{2,1,0:T(8,128)}), f32[16,16,128]{2,1,0:T(8,128)S(1)}, u32[]{:S(2)}, u32[]{:S(2)}) %all-to-all-start.3) | async-done | bytes 131104 | tf_op jit(solution)/shard_map/all_to_all | solution.py:290
  90.5 0.8 shard_map.82
  (1 shorter events, 0.0 us)
Async XLA Ops:
  2.3 16.4 %copy-start = (bf16[24,2048]{1,0:T(8,128)(2,1)S(1)}, bf16[24,2048]{1,0:T(8,128)(2,1)}, u32[]{:S(2)}) copy-start(bf16[24,2048]{1,0:T(8,128)(2,1)} %get-tuple-element.19.here.refs_2_) | copy-start | bytes 294916
  2.3 24.4 %all-to-all-start = ((bf16[8,8,2048]{2,1,0:T(8,128)(2,1)}), bf16[8,8,2048]{2,1,0:T(8,128)(2,1)S(1)}, u32[]{:S(2)}, u32[]{:S(2)}) async-start(bf16[8,8,2048]{2,1,0:T(8,128)(2,1)} %get-tuple-element.18), calls=%async_computation | async-start | bytes 524288 | tf_op jit(solution)/shard_map/all_to_all | solution.py:244
  18.7 3.9 %collective-permute-start.1 = (bf16[24,2048]{1,0:T(8,128)(2,1)S(1)}, bf16[24,2048]{1,0:T(8,128)(2,1)S(1)}, u32[]{:S(2)}, u32[]{:S(2)}) collective-permute-start(bf16[24,2048]{1,0:T(8,128)(2,1)S(1)} %copy-done), channel_id=1, source_target_pairs={{0,8},{8,16},{16,24},{24,32},{32,40},{40,48},{48,56},{56,64},{64,7... | collective-permute-start | bytes 294920 | tf_op jit(solution)/shard_map/ppermute | solution.py:242
  20.0 6.7 %collective-permute-start = (bf16[24,2048]{1,0:T(8,128)(2,1)S(1)}, bf16[24,2048]{1,0:T(8,128)(2,1)S(1)}, u32[]{:S(2)}, u32[]{:S(2)}) collective-permute-start(bf16[24,2048]{1,0:T(8,128)(2,1)S(1)} %copy-done), channel_id=1, source_target_pairs={{8,0},{16,8},{24,16},{32,24},{40,32},{48,40},{56,48},{64,56},{72,6... | collective-permute-start | bytes 294920 | tf_op jit(solution)/shard_map/ppermute | solution.py:243
  44.4 19.3 %copy-start.1 = (bf16[3,3,3,64,16]{3,4,2,1,0:T(8,128)(2,1)S(1)}, bf16[3,3,3,64,16]{3,4,2,1,0:T(8,128)(2,1)}, u32[]{:S(2)}) copy-start(bf16[3,3,3,64,16]{3,4,2,1,0:T(8,128)(2,1)} %param.5) | copy-start | bytes 165892
  44.4 33.9 %all-to-all-start.2 = ((f32[8,16,128]{2,1,0:T(8,128)}), f32[8,16,128]{2,1,0:T(8,128)S(1)}, u32[]{:S(2)}, u32[]{:S(2)}) async-start(f32[8,16,128]{2,1,0:T(8,128)} %shard_map.77.refs_4_), calls=%async_computation.2 | async-start | bytes 131072 | tf_op jit(solution)/shard_map/all_to_all | solution.py:262
  64.3 3.5 %collective-permute-start.2 = (bf16[10,8,2048]{2,1,0:T(8,128)(2,1)S(1)}, bf16[10,8,2048]{2,1,0:T(8,128)(2,1)S(1)}, u32[]{:S(2)}, u32[]{:S(2)}) collective-permute-start(bf16[10,8,2048]{2,1,0:T(8,128)(2,1)S(1)} %get-tuple-element.21), channel_id=1, source_target_pairs={{0,1},{1,0},{2,3},{3,2},{4,5},{5,4},{6,7},{7,6},{8,9},{9,8},{10,11... | collective-permute-start | bytes 983048 | tf_op jit(solution)/shard_map/ppermute | solution.py:271
  67.9 16.0 %collective-permute-start.4 = (bf16[48,2048]{1,0:T(8,128)(2,1)S(1)}, bf16[48,2048]{1,0:T(8,128)(2,1)S(1)}, u32[]{:S(2)}, u32[]{:S(2)}) collective-permute-start(bf16[48,2048]{1,0:T(8,128)(2,1)S(1)} %get-tuple-element.24), channel_id=1, source_target_pairs={{0,4},{1,5},{2,6},{3,7},{4,0},{5,1},{6,2},{7,3},{8,12},{9,13},{10,... | collective-permute-start | bytes 589832 | tf_op jit(solution)/shard_map/ppermute | solution.py:278
  71.3 12.6 %collective-permute-start.5 = (bf16[48,2048]{1,0:T(8,128)(2,1)S(1)}, bf16[48,2048]{1,0:T(8,128)(2,1)S(1)}, u32[]{:S(2)}, u32[]{:S(2)}) collective-permute-start(bf16[48,2048]{1,0:T(8,128)(2,1)S(1)} %get-tuple-element.25), channel_id=1, source_target_pairs={{0,6},{1,7},{2,0},{3,1},{4,2},{5,3},{6,4},{7,5},{8,14},{9,15},{10,... | collective-permute-start | bytes 589832 | tf_op jit(solution)/shard_map/ppermute | solution.py:278
  73.2 10.7 %collective-permute-start.3 = (bf16[48,2048]{1,0:T(8,128)(2,1)S(1)}, bf16[48,2048]{1,0:T(8,128)(2,1)S(1)}, u32[]{:S(2)}, u32[]{:S(2)}) collective-permute-start(bf16[48,2048]{1,0:T(8,128)(2,1)S(1)} %get-tuple-element.23.refs_4_), channel_id=1, source_target_pairs={{0,2},{1,3},{2,4},{3,5},{4,6},{5,7},{6,0},{7,1},{8,10},{9,11},{10,... | collective-permute-start | bytes 589832 | tf_op jit(solution)/shard_map/ppermute | solution.py:278
  79.0 4.9 %copy-start.2 = (f32[16,128]{1,0:T(8,128)S(1)}, f32[16,128]{1,0:T(8,128)}, u32[]{:S(2)}) copy-start(f32[16,128]{1,0:T(8,128)} %get-tuple-element.17.refs_1_) | copy-start | bytes 24580
  79.0 11.5 %all-to-all-start.3 = ((f32[16,16,128]{2,1,0:T(8,128)}), f32[16,16,128]{2,1,0:T(8,128)S(1)}, u32[]{:S(2)}, u32[]{:S(2)}) async-start(f32[16,16,128]{2,1,0:T(8,128)} %shard_map.80.refs_8_), calls=%async_computation.3 | async-start | bytes 262144 | tf_op jit(solution)/shard_map/all_to_all | solution.py:290

commit v9 on v7

--- a/solution.py
+++ b/solution.py
@@ -12,7 +12,7 @@
 ZL = 4
 ZH = Z // ZL
 SLAB = "slab"
-FAR_ORDER = [(h + ZH * 3 // 4) % ZH for h in range(ZH)]
+FAR_ORDER = [(ZH * 3 // 4 - h) % ZH for h in range(ZH)]
 NEAR_ORDER = [(k + ZL // 2) % ZL for k in range(ZL)]
 FAR = [[x * Z + h * ZL + k for h in FAR_ORDER] for x in range(X) for k in range(ZL)]
 NEAR = [[x * Z + h * ZL + k for k in NEAR_ORDER for x in range(X)] for h in range(ZH)]
@@ -22,7 +22,7 @@
 F32, BF16 = jnp.float32, jnp.bfloat16
 
 
-def call(body, outs, args, scratch=(), flops=0, after=(), anywhere=False, limit=24):
+def call(body, outs, args, scratch=(), flops=0, after=(), anywhere=False, limit=24, loose=()):
     used, late = (len(args), len(after))
     inner = body
     if late:
@@ -36,7 +36,9 @@
         out_shape=tuple(outs),
         in_specs=[pl.BlockSpec(memory_space=space)] * used
         + [pl.BlockSpec(memory_space=pl.ANY)] * late,
-        out_specs=tuple(pl.BlockSpec(memory_space=pltpu.VMEM) for _ in outs),
+        out_specs=tuple(
+            pl.BlockSpec(memory_space=pl.ANY if k in loose else pltpu.VMEM) for k in range(len(outs))
+        ),
         scratch_shapes=list(scratch),
         compiler_params=pltpu.CompilerParams(vmem_limit_bytes=limit << 20),
         cost_estimate=pl.CostEstimate(flops=flops, bytes_accessed=moved, transcendentals=0),
@@ -84,7 +86,7 @@
 
 
 def pack_body(
-    volume, grad, bias, volume_out, plane_out, bias_out, here_v, here_g, here_b, spare_v, spare_g, sems
+    volume, grad, bias, volume_out, plane_out, bias_out, here_v, here_g, here_b, spare_v, spare_g, packed, sems
 ):
     copy_g = pltpu.make_async_copy(grad, here_g, sems.at[0])
     copy_v = pltpu.make_async_copy(volume, here_v, sems.at[1])
@@ -94,8 +96,13 @@
     copy_b.start()
     copy_v.wait()
     flat = cells_to_lanes(here_v, spare_v)
-    for k in range(volume_out.shape[0]):
-        volume_out[k] = flat
+    packed[...] = flat
+    copies = [
+        pltpu.make_async_copy(packed, volume_out.at[k], sems.at[3 + k])
+        for k in range(volume_out.shape[0])
+    ]
+    for copy in copies:
+        copy.start()
     plane_out[16:24] = flat
     copy_g.wait()
     plane_out[0:16] = cells_to_lanes(here_g, spare_g)
@@ -104,6 +111,8 @@
     lane = lax.broadcasted_iota(jnp.int32, (16, 16), 1)
     column = jnp.sum(jnp.where(row == lane, here_b[...], 0.0), axis=1, keepdims=True)
     bias_out[...] = jnp.broadcast_to(column, (16, COLS))
+    for copy in copies:
+        copy.wait()
 
 
 def kernel_grad_body(volume, after, here, before, out):
@@ -231,9 +240,11 @@
             pltpu.VMEM((1, 16), F32),
             pltpu.VMEM((8 * ROWS, COLS), F32),
             pltpu.VMEM((16 * ROWS, COLS), F32),
-            pltpu.SemaphoreType.DMA((3,)),
+            pltpu.VMEM((8, CELLS), BF16),
+            pltpu.SemaphoreType.DMA((3 + groups,)),
         ],
         anywhere=True,
+        loose=(0,),
         limit=60,
     )
     before = lax.ppermute(here, SLAB, up)

time: 88.5 us -> 88.6 us (level)
  no operation moved by 1% of the time
where the time goes in v9:
time: 88.6 us; the launch traced here: 87.7 us
  starting transfers between devices  49.8 us (56%)
  blocking collectives  20.9 us (24%)
  waiting for transfers between devices  9.69 us (11%)
  Pallas kernels  6.59 us (7%)
    all_to_all x1, blocking collectives, on_device(): lax.all_to_all(partial.reshape(near, rows, 128), SLAB, 0, 0, axis_index_g...  20.9 us
    all_to_all x1, starting transfers between devices, on_device(): whole = lax.all_to_all(sent, 'chan', 0, 0).reshape(64, CELLS)  16.4 us
    all_to_all x1, starting transfers between devices, on_device(): parts = lax.all_to_all(spread, SLAB, 0, 0, axis_index_groups=FAR)  12.1 us
    ppermute x3, starting transfers between devices, on_device(): lax.ppermute(part, 'chan', [(i, (i + 2 * k + 2) % groups) for i in range(...  8.66 us
    pallas_call x8, Pallas kernels, call(): pl.pallas_call(inner, out_shape=tuple(outs), in_specs=[pl.BlockSpec(memor...  6.59 us
    all_to_all x1, starting transfers between devices, on_device(): lax.all_to_all(spread, SLAB, 0, 0, axis_index_groups=NEAR).reshape(256, 128)  4.88 us
    ppermute x1, starting transfers between devices, on_device(): before = lax.ppermute(here, SLAB, up)  4.55 us
    all_to_all x1, waiting for transfers between devices, on_device(): parts = lax.all_to_all(spread, SLAB, 0, 0, axis_index_groups=FAR)  3.98 us
  transfers between devices with their start and end apart: 9, of which 5 were waited for; matrix products, arithmetic and copies ran while one was open for 0% of the time, Pallas kernels for 3%

profile of v9, /device:TPU:24, one launch (start us, length us, event | category | flops | bytes accessed | tf_op | source)
XLA Modules:
  0.0 87.7 jit_solution(3925938943806896463)
XLA Ops:
  0.6 2.2 %shard_map.75 = (bf16[8,8,2048]{2,1,0:T(8,128)(2,1)}, bf16[24,2048]{1,0:T(8,128)(2,1)}, f32[16,128]{1,0:T(8,128)}) custom-call(bf16[8,1,16,128]{3,2,1,0:T(8,128)(2,1)} %volume.1, bf16[16,1,16,128]{3,2,1,0:T(8,128)(2,1)} %grad.1, f32[1,16]{1,0:T(1,128)} %bitcast.13), custom_call_target="tpu_custom_call" | custom-call | bytes 467008 | tf_op jit(solution)/shard_map/pallas_call | solution.py:34
  2.9 0.0 copy-start.1
  2.9 16.4 %all-to-all-start = ((bf16[8,8,2048]{2,1,0:T(8,128)(2,1)}), bf16[8,8,2048]{2,1,0:T(8,128)(2,1)S(1)}, u32[]{:S(2)}, u32[]{:S(2)}) async-start(bf16[8,8,2048]{2,1,0:T(8,128)(2,1)} %get-tuple-element.18), calls=%async_computation | async-start | bytes 524288 | tf_op jit(solution)/shard_map/all_to_all | solution.py:252
  19.2 0.0 copy-done.1
  19.2 1.3 %collective-permute-start = (bf16[24,2048]{1,0:T(8,128)(2,1)S(1)}, bf16[24,2048]{1,0:T(8,128)(2,1)S(1)}, u32[]{:S(2)}, u32[]{:S(2)}) collective-permute-start(bf16[24,2048]{1,0:T(8,128)(2,1)S(1)} %copy-done.1), channel_id=1, source_target_pairs={{8,0},{16,8},{24,16},{32,24},{40,32},{48,40},{56,48},{64,56},{72,6... | collective-permute-start | bytes 294920 | tf_op jit(solution)/shard_map/ppermute | solution.py:251
  20.5 4.6 %collective-permute-start.1 = (bf16[24,2048]{1,0:T(8,128)(2,1)S(1)}, bf16[24,2048]{1,0:T(8,128)(2,1)S(1)}, u32[]{:S(2)}, u32[]{:S(2)}) collective-permute-start(bf16[24,2048]{1,0:T(8,128)(2,1)S(1)} %copy-done.1), channel_id=1, source_target_pairs={{0,8},{8,16},{16,24},{24,32},{32,40},{40,48},{48,56},{56,64},{64,7... | collective-permute-start | bytes 294920 | tf_op jit(solution)/shard_map/ppermute | solution.py:250
  25.1 0.9 %collective-permute-done.after.refs_5_ = bf16[24,2048]{1,0:T(8,128)(2,1)S(1)} collective-permute-done((bf16[24,2048]{1,0:T(8,128)(2,1)S(1)}, bf16[24,2048]{1,0:T(8,128)(2,1)S(1)}, u32[]{:S(2)}, u32[]{:S(2)}) %collective-permute-start) | collective-permute-done | bytes 98336 | tf_op jit(solution)/shard_map/ppermute | solution.py:251
  26.0 1.3 %collective-permute-done.1.before.refs_4_ = bf16[24,2048]{1,0:T(8,128)(2,1)S(1)} collective-permute-done((bf16[24,2048]{1,0:T(8,128)(2,1)S(1)}, bf16[24,2048]{1,0:T(8,128)(2,1)S(1)}, u32[]{:S(2)}, u32[]{:S(2)}) %collective-permute-start.1) | collective-permute-done | bytes 98336 | tf_op jit(solution)/shard_map/ppermute | solution.py:250
  27.3 0.0 all-to-all-done
  27.3 0.5 shard_map.77
  27.8 20.9 %all_to_all.20.parts = f32[16,16,128]{2,1,0:T(8,128)S(1)} all-to-all(f32[16,16,128]{2,1,0:T(8,128)S(1)} %bitcast.10), channel_id=1, replica_groups={{16,272,528,784,24,280,536,792,0,256,512,768,8,264,520,776},{48,304,560..., dimensions={0} | all-to-all | bytes 262144 | tf_op jit(solution)/shard_map/all_to_all | solution.py:273
  48.7 0.6 shard_map.78
  49.3 12.1 %all-to-all-start.2 = ((f32[8,16,128]{2,1,0:T(8,128)}), f32[8,16,128]{2,1,0:T(8,128)S(1)}, u32[]{:S(2)}, u32[]{:S(2)}) async-start(f32[8,16,128]{2,1,0:T(8,128)} %shard_map.78), calls=%async_computation.2 | async-start | bytes 131072 | tf_op jit(solution)/shard_map/all_to_all | solution.py:281
  61.5 0.0 copy-done
  61.5 0.6 shard_map.76
  62.1 2.2 %collective-permute-start.2 = (bf16[48,2048]{1,0:T(8,128)(2,1)S(1)}, bf16[48,2048]{1,0:T(8,128)(2,1)S(1)}, u32[]{:S(2)}, u32[]{:S(2)}) collective-permute-start(bf16[48,2048]{1,0:T(8,128)(2,1)S(1)} %get-tuple-element.21), channel_id=1, source_target_pairs={{0,2},{1,3},{2,4},{3,5},{4,6},{5,7},{6,0},{7,1},{8,10},{9,11},{10,... | collective-permute-start | bytes 589832 | tf_op jit(solution)/shard_map/ppermute | solution.py:268
  64.3 4.5 %collective-permute-start.3 = (bf16[48,2048]{1,0:T(8,128)(2,1)S(1)}, bf16[48,2048]{1,0:T(8,128)(2,1)S(1)}, u32[]{:S(2)}, u32[]{:S(2)}) collective-permute-start(bf16[48,2048]{1,0:T(8,128)(2,1)S(1)} %get-tuple-element.22), channel_id=1, source_target_pairs={{0,4},{1,5},{2,6},{3,7},{4,0},{5,1},{6,2},{7,3},{8,12},{9,13},{10,... | collective-permute-start | bytes 589832 | tf_op jit(solution)/shard_map/ppermute | solution.py:268
  68.8 1.9 %collective-permute-start.4 = (bf16[48,2048]{1,0:T(8,128)(2,1)S(1)}, bf16[48,2048]{1,0:T(8,128)(2,1)S(1)}, u32[]{:S(2)}, u32[]{:S(2)}) collective-permute-start(bf16[48,2048]{1,0:T(8,128)(2,1)S(1)} %get-tuple-element.23), channel_id=1, source_target_pairs={{0,6},{1,7},{2,0},{3,1},{4,2},{5,3},{6,4},{7,5},{8,14},{9,15},{10,... | collective-permute-start | bytes 589832 | tf_op jit(solution)/shard_map/ppermute | solution.py:268
  70.7 4.0 %all-to-all-done.2.refs_0_ = f32[8,16,128]{2,1,0:T(8,128)S(1)} async-done(((f32[8,16,128]{2,1,0:T(8,128)}), f32[8,16,128]{2,1,0:T(8,128)S(1)}, u32[]{:S(2)}, u32[]{:S(2)}) %all-to-all-start.2) | async-done | bytes 65568 | tf_op jit(solution)/shard_map/all_to_all | solution.py:281
  74.7 0.7 shard_map.79.refs_6_
  75.4 4.9 %all-to-all-start.3 = ((f32[16,16,128]{2,1,0:T(8,128)}), f32[16,16,128]{2,1,0:T(8,128)S(1)}, u32[]{:S(2)}, u32[]{:S(2)}) async-start(f32[16,16,128]{2,1,0:T(8,128)} %shard_map.79.refs_6_), calls=%async_computation.3 | async-start | bytes 262144 | tf_op jit(solution)/shard_map/all_to_all | solution.py:298
  80.3 0.0 collective-permute-done.2.refs_1_
  80.3 0.0 collective-permute-done.3.refs_2_
  80.3 0.0 collective-permute-done.4.refs_3_
  80.3 0.0 copy-start.2
  80.3 0.1 shard_map.80
  80.4 1.9 %collective-permute-start.5 = (bf16[10,8,2048]{2,1,0:T(8,128)(2,1)S(1)}, bf16[10,8,2048]{2,1,0:T(8,128)(2,1)S(1)}, u32[]{:S(2)}, u32[]{:S(2)}) collective-permute-start(bf16[10,8,2048]{2,1,0:T(8,128)(2,1)S(1)} %get-tuple-element.25.mine), channel_id=1, source_target_pairs={{0,1},{1,0},{2,3},{3,2},{4,5},{5,4},{6,7},{7,6},{8,9},{9,8},{10,11... | collective-permute-start | bytes 983048 | tf_op jit(solution)/shard_map/ppermute | solution.py:297
  82.3 1.6 %collective-permute-done.5.theirs = bf16[10,8,2048]{2,1,0:T(8,128)(2,1)S(1)} collective-permute-done((bf16[10,8,2048]{2,1,0:T(8,128)(2,1)S(1)}, bf16[10,8,2048]{2,1,0:T(8,128)(2,1)S(1)}, u32[]{:S(2)}, u32[]{:S(2)}) %collective-permute-start.5) | collective-permute-done | bytes 327712 | tf_op jit(solution)/shard_map/ppermute | solution.py:297
  83.9 0.0 copy-done.2
  83.9 1.1 %shard_map.81 = (bf16[16,1,16,128]{3,2,1,0:T(8,128)(2,1)}, bf16[8,1,16,128]{3,2,1,0:T(8,128)(2,1)}) custom-call(bf16[3,3,3,16,64]{4,3,2,1,0:T(8,128)(2,1)S(1)} %bitcast.12, f32[16,128]{1,0:T(8,128)S(1)} %copy-done.2, bf16[64,2048]{1,0:T(8,128)(2,1)S(1)} %bitcast.8, f32[8,2048]{1,0:T(8,128)S(1)} %get-tuple-element.24.kept, ...), custom_call_target="tpu_custom_call" | custom-call | flops 113246208 | bytes 1144832 | tf_op jit(solution)/shard_map/pallas_call | solution.py:34
  85.0 1.9 %all-to-all-done.3 = f32[16,16,128]{2,1,0:T(8,128)S(1)} async-done(((f32[16,16,128]{2,1,0:T(8,128)}), f32[16,16,128]{2,1,0:T(8,128)S(1)}, u32[]{:S(2)}, u32[]{:S(2)}) %all-to-all-start.3) | async-done | bytes 131104 | tf_op jit(solution)/shard_map/all_to_all | solution.py:298
  86.9 0.8 shard_map.82
  (1 shorter events, 0.0 us)
Async XLA Ops:
  2.9 16.4 %copy-start.1 = (bf16[24,2048]{1,0:T(8,128)(2,1)S(1)}, bf16[24,2048]{1,0:T(8,128)(2,1)}, u32[]{:S(2)}) copy-start(bf16[24,2048]{1,0:T(8,128)(2,1)} %get-tuple-element.19.here) | copy-start | bytes 294916
  2.9 24.4 %all-to-all-start = ((bf16[8,8,2048]{2,1,0:T(8,128)(2,1)}), bf16[8,8,2048]{2,1,0:T(8,128)(2,1)S(1)}, u32[]{:S(2)}, u32[]{:S(2)}) async-start(bf16[8,8,2048]{2,1,0:T(8,128)(2,1)} %get-tuple-element.18), calls=%async_computation | async-start | bytes 524288 | tf_op jit(solution)/shard_map/all_to_all | solution.py:252
  19.2 6.7 %collective-permute-start = (bf16[24,2048]{1,0:T(8,128)(2,1)S(1)}, bf16[24,2048]{1,0:T(8,128)(2,1)S(1)}, u32[]{:S(2)}, u32[]{:S(2)}) collective-permute-start(bf16[24,2048]{1,0:T(8,128)(2,1)S(1)} %copy-done.1), channel_id=1, source_target_pairs={{8,0},{16,8},{24,16},{32,24},{40,32},{48,40},{56,48},{64,56},{72,6... | collective-permute-start | bytes 294920 | tf_op jit(solution)/shard_map/ppermute | solution.py:251
  20.5 6.8 %collective-permute-start.1 = (bf16[24,2048]{1,0:T(8,128)(2,1)S(1)}, bf16[24,2048]{1,0:T(8,128)(2,1)S(1)}, u32[]{:S(2)}, u32[]{:S(2)}) collective-permute-start(bf16[24,2048]{1,0:T(8,128)(2,1)S(1)} %copy-done.1), channel_id=1, source_target_pairs={{0,8},{8,16},{16,24},{24,32},{32,40},{40,48},{48,56},{56,64},{64,7... | collective-permute-start | bytes 294920 | tf_op jit(solution)/shard_map/ppermute | solution.py:250
  49.3 12.2 %copy-start = (bf16[3,3,3,64,16]{3,4,2,1,0:T(8,128)(2,1)S(1)}, bf16[3,3,3,64,16]{3,4,2,1,0:T(8,128)(2,1)}, u32[]{:S(2)}) copy-start(bf16[3,3,3,64,16]{3,4,2,1,0:T(8,128)(2,1)} %param.5) | copy-start | bytes 165892
  49.3 25.4 %all-to-all-start.2 = ((f32[8,16,128]{2,1,0:T(8,128)}), f32[8,16,128]{2,1,0:T(8,128)S(1)}, u32[]{:S(2)}, u32[]{:S(2)}) async-start(f32[8,16,128]{2,1,0:T(8,128)} %shard_map.78), calls=%async_computation.2 | async-start | bytes 131072 | tf_op jit(solution)/shard_map/all_to_all | solution.py:281
  62.1 18.2 %collective-permute-start.2 = (bf16[48,2048]{1,0:T(8,128)(2,1)S(1)}, bf16[48,2048]{1,0:T(8,128)(2,1)S(1)}, u32[]{:S(2)}, u32[]{:S(2)}) collective-permute-start(bf16[48,2048]{1,0:T(8,128)(2,1)S(1)} %get-tuple-element.21), channel_id=1, source_target_pairs={{0,2},{1,3},{2,4},{3,5},{4,6},{5,7},{6,0},{7,1},{8,10},{9,11},{10,... | collective-permute-start | bytes 589832 | tf_op jit(solution)/shard_map/ppermute | solution.py:268
  64.3 16.0 %collective-permute-start.3 = (bf16[48,2048]{1,0:T(8,128)(2,1)S(1)}, bf16[48,2048]{1,0:T(8,128)(2,1)S(1)}, u32[]{:S(2)}, u32[]{:S(2)}) collective-permute-start(bf16[48,2048]{1,0:T(8,128)(2,1)S(1)} %get-tuple-element.22), channel_id=1, source_target_pairs={{0,4},{1,5},{2,6},{3,7},{4,0},{5,1},{6,2},{7,3},{8,12},{9,13},{10,... | collective-permute-start | bytes 589832 | tf_op jit(solution)/shard_map/ppermute | solution.py:268
  68.8 11.5 %collective-permute-start.4 = (bf16[48,2048]{1,0:T(8,128)(2,1)S(1)}, bf16[48,2048]{1,0:T(8,128)(2,1)S(1)}, u32[]{:S(2)}, u32[]{:S(2)}) collective-permute-start(bf16[48,2048]{1,0:T(8,128)(2,1)S(1)} %get-tuple-element.23), channel_id=1, source_target_pairs={{0,6},{1,7},{2,0},{3,1},{4,2},{5,3},{6,4},{7,5},{8,14},{9,15},{10,... | collective-permute-start | bytes 589832 | tf_op jit(solution)/shard_map/ppermute | solution.py:268
  75.4 11.5 %all-to-all-start.3 = ((f32[16,16,128]{2,1,0:T(8,128)}), f32[16,16,128]{2,1,0:T(8,128)S(1)}, u32[]{:S(2)}, u32[]{:S(2)}) async-start(f32[16,16,128]{2,1,0:T(8,128)} %shard_map.79.refs_6_), calls=%async_computation.3 | async-start | bytes 262144 | tf_op jit(solution)/shard_map/all_to_all | solution.py:298
  80.3 3.6 %copy-start.2 = (f32[16,128]{1,0:T(8,128)S(1)}, f32[16,128]{1,0:T(8,128)}, u32[]{:S(2)}) copy-start(f32[16,128]{1,0:T(8,128)} %get-tuple-element.17.bias) | copy-start | bytes 24580
  80.4 3.5 %collective-permute-start.5 = (bf16[10,8,2048]{2,1,0:T(8,128)(2,1)S(1)}, bf16[10,8,2048]{2,1,0:T(8,128)(2,1)S(1)}, u32[]{:S(2)}, u32[]{:S(2)}) collective-permute-start(bf16[10,8,2048]{2,1,0:T(8,128)(2,1)S(1)} %get-tuple-element.25.mine), channel_id=1, source_target_pairs={{0,1},{1,0},{2,3},{3,2},{4,5},{5,4},{6,7},{7,6},{8,9},{9,8},{10,11... | collective-permute-start | bytes 983048 | tf_op jit(solution)/shard_map/ppermute | solution.py:297

commit v10 on v7

--- a/solution.py
+++ b/solution.py
@@ -12,7 +12,7 @@
 ZL = 4
 ZH = Z // ZL
 SLAB = "slab"
-FAR_ORDER = [(h + ZH * 3 // 4) % ZH for h in range(ZH)]
+FAR_ORDER = [(ZH * 3 // 4 - h) % ZH for h in range(ZH)]
 NEAR_ORDER = [(k + ZL // 2) % ZL for k in range(ZL)]
 FAR = [[x * Z + h * ZL + k for h in FAR_ORDER] for x in range(X) for k in range(ZL)]
 NEAR = [[x * Z + h * ZL + k for k in NEAR_ORDER for x in range(X)] for h in range(ZH)]

time: 88.5 us -> 88 us (level)
  no operation moved by 1% of the time
where the time goes in v10:
time: 88 us; the launch traced here: 87.2 us
  starting transfers between devices  49.8 us (57%)
  blocking collectives  20.9 us (24%)
  waiting for transfers between devices  9.68 us (11%)
  Pallas kernels  6.05 us (7%)
    all_to_all x1, blocking collectives, on_device(): lax.all_to_all(partial.reshape(near, rows, 128), SLAB, 0, 0, axis_index_g...  20.9 us
    all_to_all x1, starting transfers between devices, on_device(): whole = lax.all_to_all(sent, 'chan', 0, 0).reshape(64, CELLS)  16.4 us
    all_to_all x1, starting transfers between devices, on_device(): parts = lax.all_to_all(spread, SLAB, 0, 0, axis_index_groups=FAR)  12.1 us
    ppermute x3, starting transfers between devices, on_device(): lax.ppermute(part, 'chan', [(i, (i + 2 * k + 2) % groups) for i in range(...  8.67 us
    pallas_call x8, Pallas kernels, call(): pl.pallas_call(inner, out_shape=tuple(outs), in_specs=[pl.BlockSpec(memor...  6.05 us
    all_to_all x1, starting transfers between devices, on_device(): lax.all_to_all(spread, SLAB, 0, 0, axis_index_groups=NEAR).reshape(256, 128)  4.88 us
    ppermute x1, starting transfers between devices, on_device(): before = lax.ppermute(here, SLAB, up)  4.55 us
    all_to_all x1, waiting for transfers between devices, on_device(): parts = lax.all_to_all(spread, SLAB, 0, 0, axis_index_groups=FAR)  3.97 us
  transfers between devices with their start and end apart: 9, of which 5 were waited for; matrix products, arithmetic and copies ran while one was open for 0% of the time, Pallas kernels for 3%

profile of v10, /device:TPU:24, one launch (start us, length us, event | category | flops | bytes accessed | tf_op | source)
XLA Modules:
  0.0 87.2 jit_solution(8301189027723155920)
XLA Ops:
  0.6 1.7 %shard_map.75 = (bf16[8,8,2048]{2,1,0:T(8,128)(2,1)}, bf16[24,2048]{1,0:T(8,128)(2,1)}, f32[16,128]{1,0:T(8,128)}) custom-call(bf16[8,1,16,128]{3,2,1,0:T(8,128)(2,1)} %volume.1, bf16[16,1,16,128]{3,2,1,0:T(8,128)(2,1)} %grad.1, f32[1,16]{1,0:T(1,128)} %bitcast.13), custom_call_target="tpu_custom_call" | custom-call | bytes 467008 | tf_op jit(solution)/shard_map/pallas_call | solution.py:34
  2.3 0.0 copy-start.1
  2.3 16.4 %all-to-all-start = ((bf16[8,8,2048]{2,1,0:T(8,128)(2,1)}), bf16[8,8,2048]{2,1,0:T(8,128)(2,1)S(1)}, u32[]{:S(2)}, u32[]{:S(2)}) async-start(bf16[8,8,2048]{2,1,0:T(8,128)(2,1)} %get-tuple-element.18), calls=%async_computation | async-start | bytes 524288 | tf_op jit(solution)/shard_map/all_to_all | solution.py:241
  18.7 0.0 copy-done.1
  18.7 1.3 %collective-permute-start = (bf16[24,2048]{1,0:T(8,128)(2,1)S(1)}, bf16[24,2048]{1,0:T(8,128)(2,1)S(1)}, u32[]{:S(2)}, u32[]{:S(2)}) collective-permute-start(bf16[24,2048]{1,0:T(8,128)(2,1)S(1)} %copy-done.1), channel_id=1, source_target_pairs={{8,0},{16,8},{24,16},{32,24},{40,32},{48,40},{56,48},{64,56},{72,6... | collective-permute-start | bytes 294920 | tf_op jit(solution)/shard_map/ppermute | solution.py:240
  20.0 4.6 %collective-permute-start.1 = (bf16[24,2048]{1,0:T(8,128)(2,1)S(1)}, bf16[24,2048]{1,0:T(8,128)(2,1)S(1)}, u32[]{:S(2)}, u32[]{:S(2)}) collective-permute-start(bf16[24,2048]{1,0:T(8,128)(2,1)S(1)} %copy-done.1), channel_id=1, source_target_pairs={{0,8},{8,16},{16,24},{24,32},{32,40},{40,48},{48,56},{56,64},{64,7... | collective-permute-start | bytes 294920 | tf_op jit(solution)/shard_map/ppermute | solution.py:239
  24.5 0.9 %collective-permute-done.after.refs_5_ = bf16[24,2048]{1,0:T(8,128)(2,1)S(1)} collective-permute-done((bf16[24,2048]{1,0:T(8,128)(2,1)S(1)}, bf16[24,2048]{1,0:T(8,128)(2,1)S(1)}, u32[]{:S(2)}, u32[]{:S(2)}) %collective-permute-start) | collective-permute-done | bytes 98336 | tf_op jit(solution)/shard_map/ppermute | solution.py:240
  25.4 1.3 %collective-permute-done.1.before.refs_4_ = bf16[24,2048]{1,0:T(8,128)(2,1)S(1)} collective-permute-done((bf16[24,2048]{1,0:T(8,128)(2,1)S(1)}, bf16[24,2048]{1,0:T(8,128)(2,1)S(1)}, u32[]{:S(2)}, u32[]{:S(2)}) %collective-permute-start.1) | collective-permute-done | bytes 98336 | tf_op jit(solution)/shard_map/ppermute | solution.py:239
  26.7 0.0 all-to-all-done
  26.7 0.6 shard_map.77
  27.3 20.9 %all_to_all.20.parts = f32[16,16,128]{2,1,0:T(8,128)S(1)} all-to-all(f32[16,16,128]{2,1,0:T(8,128)S(1)} %bitcast.10), channel_id=1, replica_groups={{16,272,528,784,24,280,536,792,0,256,512,768,8,264,520,776},{48,304,560..., dimensions={0} | all-to-all | bytes 262144 | tf_op jit(solution)/shard_map/all_to_all | solution.py:262
  48.1 0.6 shard_map.78
  48.8 12.1 %all-to-all-start.2 = ((f32[8,16,128]{2,1,0:T(8,128)}), f32[8,16,128]{2,1,0:T(8,128)S(1)}, u32[]{:S(2)}, u32[]{:S(2)}) async-start(f32[8,16,128]{2,1,0:T(8,128)} %shard_map.78), calls=%async_computation.2 | async-start | bytes 131072 | tf_op jit(solution)/shard_map/all_to_all | solution.py:270
  60.9 0.0 copy-done
  60.9 0.6 shard_map.76
  61.5 2.2 %collective-permute-start.2 = (bf16[48,2048]{1,0:T(8,128)(2,1)S(1)}, bf16[48,2048]{1,0:T(8,128)(2,1)S(1)}, u32[]{:S(2)}, u32[]{:S(2)}) collective-permute-start(bf16[48,2048]{1,0:T(8,128)(2,1)S(1)} %get-tuple-element.21), channel_id=1, source_target_pairs={{0,2},{1,3},{2,4},{3,5},{4,6},{5,7},{6,0},{7,1},{8,10},{9,11},{10,... | collective-permute-start | bytes 589832 | tf_op jit(solution)/shard_map/ppermute | solution.py:257
  63.7 4.5 %collective-permute-start.3 = (bf16[48,2048]{1,0:T(8,128)(2,1)S(1)}, bf16[48,2048]{1,0:T(8,128)(2,1)S(1)}, u32[]{:S(2)}, u32[]{:S(2)}) collective-permute-start(bf16[48,2048]{1,0:T(8,128)(2,1)S(1)} %get-tuple-element.22), channel_id=1, source_target_pairs={{0,4},{1,5},{2,6},{3,7},{4,0},{5,1},{6,2},{7,3},{8,12},{9,13},{10,... | collective-permute-start | bytes 589832 | tf_op jit(solution)/shard_map/ppermute | solution.py:257
  68.3 1.9 %collective-permute-start.4 = (bf16[48,2048]{1,0:T(8,128)(2,1)S(1)}, bf16[48,2048]{1,0:T(8,128)(2,1)S(1)}, u32[]{:S(2)}, u32[]{:S(2)}) collective-permute-start(bf16[48,2048]{1,0:T(8,128)(2,1)S(1)} %get-tuple-element.23), channel_id=1, source_target_pairs={{0,6},{1,7},{2,0},{3,1},{4,2},{5,3},{6,4},{7,5},{8,14},{9,15},{10,... | collective-permute-start | bytes 589832 | tf_op jit(solution)/shard_map/ppermute | solution.py:257
  70.2 4.0 %all-to-all-done.2.refs_0_ = f32[8,16,128]{2,1,0:T(8,128)S(1)} async-done(((f32[8,16,128]{2,1,0:T(8,128)}), f32[8,16,128]{2,1,0:T(8,128)S(1)}, u32[]{:S(2)}, u32[]{:S(2)}) %all-to-all-start.2) | async-done | bytes 65568 | tf_op jit(solution)/shard_map/all_to_all | solution.py:270
  74.2 0.7 shard_map.79.refs_6_
  74.8 4.9 %all-to-all-start.3 = ((f32[16,16,128]{2,1,0:T(8,128)}), f32[16,16,128]{2,1,0:T(8,128)S(1)}, u32[]{:S(2)}, u32[]{:S(2)}) async-start(f32[16,16,128]{2,1,0:T(8,128)} %shard_map.79.refs_6_), calls=%async_computation.3 | async-start | bytes 262144 | tf_op jit(solution)/shard_map/all_to_all | solution.py:287
  79.7 0.0 collective-permute-done.2.refs_1_
  79.7 0.0 collective-permute-done.3.refs_2_
  79.7 0.0 collective-permute-done.4.refs_3_
  79.7 0.0 copy-start.2
  79.7 0.1 shard_map.80
  79.8 1.9 %collective-permute-start.5 = (bf16[10,8,2048]{2,1,0:T(8,128)(2,1)S(1)}, bf16[10,8,2048]{2,1,0:T(8,128)(2,1)S(1)}, u32[]{:S(2)}, u32[]{:S(2)}) collective-permute-start(bf16[10,8,2048]{2,1,0:T(8,128)(2,1)S(1)} %get-tuple-element.25.mine), channel_id=1, source_target_pairs={{0,1},{1,0},{2,3},{3,2},{4,5},{5,4},{6,7},{7,6},{8,9},{9,8},{10,11... | collective-permute-start | bytes 983048 | tf_op jit(solution)/shard_map/ppermute | solution.py:286
  81.8 1.6 %collective-permute-done.5.theirs = bf16[10,8,2048]{2,1,0:T(8,128)(2,1)S(1)} collective-permute-done((bf16[10,8,2048]{2,1,0:T(8,128)(2,1)S(1)}, bf16[10,8,2048]{2,1,0:T(8,128)(2,1)S(1)}, u32[]{:S(2)}, u32[]{:S(2)}) %collective-permute-start.5) | collective-permute-done | bytes 327712 | tf_op jit(solution)/shard_map/ppermute | solution.py:286
  83.4 0.0 copy-done.2
  83.4 1.1 %shard_map.81 = (bf16[16,1,16,128]{3,2,1,0:T(8,128)(2,1)}, bf16[8,1,16,128]{3,2,1,0:T(8,128)(2,1)}) custom-call(bf16[3,3,3,16,64]{4,3,2,1,0:T(8,128)(2,1)S(1)} %bitcast.12, f32[16,128]{1,0:T(8,128)S(1)} %copy-done.2, bf16[64,2048]{1,0:T(8,128)(2,1)S(1)} %bitcast.8, f32[8,2048]{1,0:T(8,128)S(1)} %get-tuple-element.24.kept, ...), custom_call_target="tpu_custom_call" | custom-call | flops 113246208 | bytes 1144832 | tf_op jit(solution)/shard_map/pallas_call | solution.py:34
  84.5 1.9 %all-to-all-done.3 = f32[16,16,128]{2,1,0:T(8,128)S(1)} async-done(((f32[16,16,128]{2,1,0:T(8,128)}), f32[16,16,128]{2,1,0:T(8,128)S(1)}, u32[]{:S(2)}, u32[]{:S(2)}) %all-to-all-start.3) | async-done | bytes 131104 | tf_op jit(solution)/shard_map/all_to_all | solution.py:287
  86.4 0.8 shard_map.82
  (1 shorter events, 0.0 us)
Async XLA Ops:
  2.3 16.4 %copy-start.1 = (bf16[24,2048]{1,0:T(8,128)(2,1)S(1)}, bf16[24,2048]{1,0:T(8,128)(2,1)}, u32[]{:S(2)}) copy-start(bf16[24,2048]{1,0:T(8,128)(2,1)} %get-tuple-element.19.here) | copy-start | bytes 294916
  2.3 24.4 %all-to-all-start = ((bf16[8,8,2048]{2,1,0:T(8,128)(2,1)}), bf16[8,8,2048]{2,1,0:T(8,128)(2,1)S(1)}, u32[]{:S(2)}, u32[]{:S(2)}) async-start(bf16[8,8,2048]{2,1,0:T(8,128)(2,1)} %get-tuple-element.18), calls=%async_computation | async-start | bytes 524288 | tf_op jit(solution)/shard_map/all_to_all | solution.py:241
  18.7 6.7 %collective-permute-start = (bf16[24,2048]{1,0:T(8,128)(2,1)S(1)}, bf16[24,2048]{1,0:T(8,128)(2,1)S(1)}, u32[]{:S(2)}, u32[]{:S(2)}) collective-permute-start(bf16[24,2048]{1,0:T(8,128)(2,1)S(1)} %copy-done.1), channel_id=1, source_target_pairs={{8,0},{16,8},{24,16},{32,24},{40,32},{48,40},{56,48},{64,56},{72,6... | collective-permute-start | bytes 294920 | tf_op jit(solution)/shard_map/ppermute | solution.py:240
  20.0 6.8 %collective-permute-start.1 = (bf16[24,2048]{1,0:T(8,128)(2,1)S(1)}, bf16[24,2048]{1,0:T(8,128)(2,1)S(1)}, u32[]{:S(2)}, u32[]{:S(2)}) collective-permute-start(bf16[24,2048]{1,0:T(8,128)(2,1)S(1)} %copy-done.1), channel_id=1, source_target_pairs={{0,8},{8,16},{16,24},{24,32},{32,40},{40,48},{48,56},{56,64},{64,7... | collective-permute-start | bytes 294920 | tf_op jit(solution)/shard_map/ppermute | solution.py:239
  48.8 12.2 %copy-start = (bf16[3,3,3,64,16]{3,4,2,1,0:T(8,128)(2,1)S(1)}, bf16[3,3,3,64,16]{3,4,2,1,0:T(8,128)(2,1)}, u32[]{:S(2)}) copy-start(bf16[3,3,3,64,16]{3,4,2,1,0:T(8,128)(2,1)} %param.5) | copy-start | bytes 165892
  48.8 25.4 %all-to-all-start.2 = ((f32[8,16,128]{2,1,0:T(8,128)}), f32[8,16,128]{2,1,0:T(8,128)S(1)}, u32[]{:S(2)}, u32[]{:S(2)}) async-start(f32[8,16,128]{2,1,0:T(8,128)} %shard_map.78), calls=%async_computation.2 | async-start | bytes 131072 | tf_op jit(solution)/shard_map/all_to_all | solution.py:270
  61.5 18.2 %collective-permute-start.2 = (bf16[48,2048]{1,0:T(8,128)(2,1)S(1)}, bf16[48,2048]{1,0:T(8,128)(2,1)S(1)}, u32[]{:S(2)}, u32[]{:S(2)}) collective-permute-start(bf16[48,2048]{1,0:T(8,128)(2,1)S(1)} %get-tuple-element.21), channel_id=1, source_target_pairs={{0,2},{1,3},{2,4},{3,5},{4,6},{5,7},{6,0},{7,1},{8,10},{9,11},{10,... | collective-permute-start | bytes 589832 | tf_op jit(solution)/shard_map/ppermute | solution.py:257
  63.7 16.0 %collective-permute-start.3 = (bf16[48,2048]{1,0:T(8,128)(2,1)S(1)}, bf16[48,2048]{1,0:T(8,128)(2,1)S(1)}, u32[]{:S(2)}, u32[]{:S(2)}) collective-permute-start(bf16[48,2048]{1,0:T(8,128)(2,1)S(1)} %get-tuple-element.22), channel_id=1, source_target_pairs={{0,4},{1,5},{2,6},{3,7},{4,0},{5,1},{6,2},{7,3},{8,12},{9,13},{10,... | collective-permute-start | bytes 589832 | tf_op jit(solution)/shard_map/ppermute | solution.py:257
  68.3 11.5 %collective-permute-start.4 = (bf16[48,2048]{1,0:T(8,128)(2,1)S(1)}, bf16[48,2048]{1,0:T(8,128)(2,1)S(1)}, u32[]{:S(2)}, u32[]{:S(2)}) collective-permute-start(bf16[48,2048]{1,0:T(8,128)(2,1)S(1)} %get-tuple-element.23), channel_id=1, source_target_pairs={{0,6},{1,7},{2,0},{3,1},{4,2},{5,3},{6,4},{7,5},{8,14},{9,15},{10,... | collective-permute-start | bytes 589832 | tf_op jit(solution)/shard_map/ppermute | solution.py:257
  74.8 11.5 %all-to-all-start.3 = ((f32[16,16,128]{2,1,0:T(8,128)}), f32[16,16,128]{2,1,0:T(8,128)S(1)}, u32[]{:S(2)}, u32[]{:S(2)}) async-start(f32[16,16,128]{2,1,0:T(8,128)} %shard_map.79.refs_6_), calls=%async_computation.3 | async-start | bytes 262144 | tf_op jit(solution)/shard_map/all_to_all | solution.py:287
  79.7 3.6 %copy-start.2 = (f32[16,128]{1,0:T(8,128)S(1)}, f32[16,128]{1,0:T(8,128)}, u32[]{:S(2)}) copy-start(f32[16,128]{1,0:T(8,128)} %get-tuple-element.17.bias) | copy-start | bytes 24580
  79.8 3.5 %collective-permute-start.5 = (bf16[10,8,2048]{2,1,0:T(8,128)(2,1)S(1)}, bf16[10,8,2048]{2,1,0:T(8,128)(2,1)S(1)}, u32[]{:S(2)}, u32[]{:S(2)}) collective-permute-start(bf16[10,8,2048]{2,1,0:T(8,128)(2,1)S(1)} %get-tuple-element.25.mine), channel_id=1, source_target_pairs={{0,1},{1,0},{2,3},{3,2},{4,5},{5,4},{6,7},{7,6},{8,9},{9,8},{10,11... | collective-permute-start | bytes 983048 | tf_op jit(solution)/shard_map/ppermute | solution.py:286
